TPU v7x, 512 devices: a whole 4x8x8 slice. The times are simulated.
512 devices in a mesh: vrow: 2 (over y_lo), vcol: 8 (over z), pix: 32 (over x, y_hi, core).
Axes of the slice: x: 4, y: 8 (y_hi: 4, y_lo: 2; y = y_hi * 2 + y_lo), z: 8, core: 2. Of those that a mesh axis runs over, the one named last changes fastest.
Arguments:
- features: bfloat16 [16, 16, 64, 4096], P('vrow', 'vcol', None, 'pix'), may hold values from -400 to 400
- out_cotangent: bfloat16 [16, 16, 64, 4096], P('vrow', 'vcol', None, 'pix'), may hold values from -6 to 6
- norm_gain: float32 [64], replicated, may hold values from 0.25 to 1.75
- query_proj: bfloat16 [64, 64], replicated, may hold values from -0.75 to 0.75
- keyval_proj: bfloat16 [64, 128], replicated, may hold values from -0.75 to 0.75
- output_proj: bfloat16 [64, 64], replicated, may hold values from -0.75 to 0.75
Outputs:
- features_grad: bfloat16 [16, 16, 64, 4096], P('vrow', 'vcol', None, 'pix')
- query_proj_grad: float32 [64, 64], replicated
- keyval_proj_grad: float32 [64, 128], replicated
- output_proj_grad: float32 [64, 64], replicated
- norm_gain_grad: float32 [64], replicated
All inputs are finite; a program needn't handle non-finite values.
Results may differ from a plain program's by a relative error of at most 0.0085.
Values may be sent and summed in bfloat16 or wider, within the bound.
No kernel may reach another device: no remote copies, remote signals or barrier semaphores. Data moves between devices by JAX's collectives and lax.ppermute only.
A program may use at most 64 MiB of HBM per device.

v0:
```python
import math

import jax
import jax.numpy as jnp
from jax import lax
from jax.sharding import PartitionSpec as P

HEADS = 4


EPSILON = 1e-06
precise = lax.Precision.HIGHEST


def extended(shard, sides, width):
    for axis, dim in sides:
        count, length = (lax.axis_size(axis), shard.shape[dim])
        up = [(i, (i + 1) % count) for i in range(count - 1)]
        down = [(j, i) for i, j in up]
        last = lax.slice_in_dim(shard, length - width, length, axis=dim)
        leading = lax.slice_in_dim(shard, 0, width, axis=dim)
        before = lax.ppermute(last, axis, up)
        after = lax.ppermute(leading, axis, down)
        shard = jnp.concatenate([before, shard, after], axis=dim)
    return shard


def normalize(features, norm_gain):
    values = features.astype(jnp.float32)
    inv_norm = lax.rsqrt(jnp.mean(values * values, axis=2, keepdims=True) + EPSILON)
    scaled = values * inv_norm
    normed = (scaled * norm_gain[None, None, :, None]).astype(jnp.bfloat16)
    return (normed, scaled, inv_norm)


def unit_rows(raw_proj):
    inv_norm = lax.rsqrt(jnp.mean(raw_proj * raw_proj, axis=2, keepdims=True) + EPSILON)
    return (raw_proj * inv_norm, inv_norm)


def unit_back(unit_vals, inv_norm, upstream):
    return inv_norm * (upstream - unit_vals * jnp.mean(upstream * unit_vals, axis=2, keepdims=True))


def project(normed, weight):
    return jnp.einsum("uvdp,de->uvep", normed, weight, preferred_element_type=jnp.float32)


def split_heads(grid_data):
    view_rows, view_cols, channels, pixels = grid_data.shape
    return grid_data.astype(jnp.float32).reshape(
        view_rows, view_cols, HEADS, channels // HEADS, pixels
    )


def interior(grid_data):
    return grid_data[2:-2, 2:-2]


def window_at(grid_data, first_row, first_col, view_rows, view_cols):
    zero = jnp.zeros((), jnp.int32)
    starts = (first_row.astype(jnp.int32), first_col.astype(jnp.int32), zero, zero)
    sizes = (view_rows, view_cols, grid_data.shape[2], grid_data.shape[3])
    return lax.dynamic_slice(grid_data, starts, sizes)


def make_tokens(normed, query_proj, keyval_proj):
    channels = normed.shape[2]
    unit_query, query_inv = unit_rows(project(normed, query_proj))
    raw_keyval = project(normed, keyval_proj)
    unit_key, key_inv = unit_rows(raw_keyval[:, :, :channels])
    tokens = jnp.concatenate([unit_query, unit_key, raw_keyval[:, :, channels:]], axis=2).astype(
        jnp.bfloat16
    )
    return (tokens, (unit_query, query_inv, unit_key, key_inv))


def front_halo(normed, query_proj, keyval_proj):
    tokens, norm_stats = make_tokens(normed, query_proj, keyval_proj)
    tokens_pad = extended(tokens, (("vrow", 0), ("vcol", 1)), 2)
    return (tokens_pad, norm_stats)


def side_halo(side_data):
    return extended(side_data, (("vrow", 0), ("vcol", 1)), 2)


def attend(tokens_pad):
    channels = tokens_pad.shape[2] // 3
    own_tokens = interior(tokens_pad)
    view_rows, view_cols = (own_tokens.shape[0], own_tokens.shape[1])
    query_heads = split_heads(own_tokens[:, :, :channels])
    score_scale = (channels // HEADS) ** (-0.5)

    def attend_one_offset(offset, carry):
        exp_total, weighted = carry
        window = window_at(tokens_pad, offset // 5, offset % 5, view_rows, view_cols)
        key_heads = split_heads(window[:, :, channels : 2 * channels])
        values = split_heads(window[:, :, 2 * channels :])
        weight = jnp.exp(jnp.sum(query_heads * key_heads, axis=3) * score_scale)
        return (exp_total + weight, weighted + weight[:, :, :, None] * values)

    initial = (
        jnp.zeros(query_heads.shape[:3] + query_heads.shape[4:], jnp.float32),
        jnp.zeros(query_heads.shape, jnp.float32),
    )
    exp_total, weighted = lax.fori_loop(0, 25, attend_one_offset, initial)
    inv_total = 1.0 / exp_total
    return (query_heads, weighted * inv_total[:, :, :, None], inv_total)


def query_grads(tokens_pad, query_heads, out_heads, inv_total, spread):
    channels = tokens_pad.shape[2] // 3
    view_rows, view_cols, head_count, head_size, pixels = query_heads.shape
    score_scale = head_size ** (-0.5)

    def query_one_offset(offset, query_accum):
        window = window_at(tokens_pad, offset // 5, offset % 5, view_rows, view_cols)
        key_heads = split_heads(window[:, :, channels : 2 * channels])
        values = split_heads(window[:, :, 2 * channels :])
        attn_prob = jnp.exp(jnp.sum(query_heads * key_heads, axis=3) * score_scale) * inv_total
        prob_grad = jnp.sum(out_heads * values, axis=3)
        score_grad = attn_prob * (prob_grad - spread)
        return query_accum + score_grad[:, :, :, None] * key_heads

    query_accum = lax.fori_loop(0, 25, query_one_offset, jnp.zeros(query_heads.shape, jnp.float32))
    return (query_accum * score_scale).reshape(view_rows, view_cols, channels, pixels)


def key_grads(tokens_pad, side_pad):
    channels = tokens_pad.shape[2] // 3
    own_tokens = interior(tokens_pad)
    view_rows, view_cols, pixels = (own_tokens.shape[0], own_tokens.shape[1], own_tokens.shape[3])
    key_heads = split_heads(own_tokens[:, :, channels : 2 * channels])
    values = split_heads(own_tokens[:, :, 2 * channels :])
    score_scale = (channels // HEADS) ** (-0.5)

    def key_one_offset(offset, carry):
        key_accum, value_accum = carry
        first_row = 4 - offset // 5
        first_col = 4 - offset % 5
        queries = split_heads(
            window_at(tokens_pad, first_row, first_col, view_rows, view_cols)[:, :, :channels]
        )
        side_data = window_at(side_pad, first_row, first_col, view_rows, view_cols)
        out_heads = side_data[:, :, :channels].reshape(key_heads.shape)
        inv_total = side_data[:, :, channels : channels + HEADS]
        spread = side_data[:, :, channels + HEADS :]
        attn_prob = jnp.exp(jnp.sum(queries * key_heads, axis=3) * score_scale) * inv_total
        prob_grad = jnp.sum(out_heads * values, axis=3)
        score_grad = attn_prob * (prob_grad - spread)
        return (
            key_accum + score_grad[:, :, :, None] * queries,
            value_accum + attn_prob[:, :, :, None] * out_heads,
        )

    initial = (jnp.zeros(key_heads.shape, jnp.float32), jnp.zeros(key_heads.shape, jnp.float32))
    key_accum, value_accum = lax.fori_loop(0, 25, key_one_offset, initial)
    key_part = (key_accum * score_scale).reshape(view_rows, view_cols, channels, pixels)
    value_part = value_accum.reshape(view_rows, view_cols, channels, pixels)
    return jnp.concatenate([key_part, value_part], axis=2)


def middle(tokens_pad, cotangent, output_proj, surround):
    query_heads, attended, inv_total = attend(tokens_pad)
    view_rows, view_cols, head_count, head_size, pixels = attended.shape
    channels = head_count * head_size
    mixed_out = attended.reshape(view_rows, view_cols, channels, pixels).astype(jnp.bfloat16)
    out_grad = jnp.einsum(
        "uvep,de->uvdp", cotangent, output_proj, preferred_element_type=jnp.float32
    )
    out_heads = out_grad.reshape(attended.shape)
    spread = jnp.sum(out_heads * attended, axis=3)
    query_grad = query_grads(tokens_pad, query_heads, out_heads, inv_total, spread)
    side_pad = surround(jnp.concatenate([out_grad, inv_total, spread], axis=2))
    keyval_grad = key_grads(tokens_pad, side_pad)
    output_part = jnp.einsum(
        "uvdp,uvep->de", mixed_out, cotangent, preferred_element_type=jnp.float32
    )
    return (query_grad, keyval_grad, output_part)


def backward(normed, norm_stats, query_grad, keyval_grad, query_proj, keyval_proj):
    unit_query, query_inv, unit_key, key_inv = norm_stats
    channels = normed.shape[2]
    raw_query_grad = unit_back(unit_query, query_inv, query_grad)
    raw_keyval_grad = jnp.concatenate(
        [unit_back(unit_key, key_inv, keyval_grad[:, :, :channels]), keyval_grad[:, :, channels:]],
        axis=2,
    )
    normed_grad = jnp.einsum(
        "uvep,de->uvdp", raw_query_grad, query_proj.astype(jnp.float32), precision=precise
    )
    normed_grad = normed_grad + jnp.einsum(
        "uvep,de->uvdp", raw_keyval_grad, keyval_proj.astype(jnp.float32), precision=precise
    )
    normed_float = normed.astype(jnp.float32)
    query_part = jnp.einsum("uvdp,uvep->de", normed_float, raw_query_grad, precision=precise)
    keyval_part = jnp.einsum("uvdp,uvep->de", normed_float, raw_keyval_grad, precision=precise)
    return (normed_grad, query_part, keyval_part)


def norm_back(cotangent, scaled, inv_norm, norm_gain, normed_grad):
    scaled_grad = normed_grad * norm_gain[None, None, :, None]
    gain_part = jnp.sum(normed_grad * scaled, axis=(0, 1, 3))
    branch = inv_norm * (
        scaled_grad - scaled * jnp.mean(scaled_grad * scaled, axis=2, keepdims=True)
    )
    return ((cotangent.astype(jnp.float32) + branch).astype(jnp.bfloat16), gain_part)


def body(features, out_cotangent, norm_gain, query_proj, keyval_proj, output_proj):
    view_rows, view_cols, channels, pixels = features.shape
    block_size = min(pixels, 128)

    def one_block(block_index, loop_state):
        input_grads, weight_sums = loop_state
        normed, scaled, inv_norm = normalize(features, norm_gain)
        tokens_pad, norm_stats = front_halo(normed, query_proj, keyval_proj)
        query_grad, keyval_grad, output_part = middle(
            tokens_pad, out_cotangent, output_proj, side_halo
        )
        normed_grad, query_part, keyval_part = backward(
            normed, norm_stats, query_grad, keyval_grad, query_proj, keyval_proj
        )
        grad_block, gain_part = norm_back(out_cotangent, scaled, inv_norm, norm_gain, normed_grad)
        input_grads = grad_block
        parts = (query_part, keyval_part, output_part, gain_part)
        return (input_grads, tuple((summed + addend for summed, addend in zip(weight_sums, parts))))

    initial = (
        jnp.zeros(features.shape, jnp.bfloat16),
        (
            jnp.zeros((channels, channels), jnp.float32),
            jnp.zeros((channels, 2 * channels), jnp.float32),
            jnp.zeros((channels, channels), jnp.float32),
            jnp.zeros((channels,), jnp.float32),
        ),
    )
    features_grad, weight_sums = lax.fori_loop(0, pixels // block_size, one_block, initial)
    query_part, keyval_part, output_part, gain_part = weight_sums
    summed_grads = lax.psum(
        (query_part, keyval_part, output_part, gain_part), ("vrow", "vcol", "pix")
    )
    tokens_all = (
        view_rows
        * view_cols
        * pixels
        * lax.axis_size("vrow")
        * lax.axis_size("vcol")
        * lax.axis_size("pix")
    )
    factor = 1.0 / math.sqrt(tokens_all)
    return (
        features_grad,
        summed_grads[0] * factor,
        summed_grads[1] * factor,
        summed_grads[2] * factor,
        summed_grads[3] * factor,
    )


def solution(mesh):
    placed = (P("vrow", "vcol", None, "pix"), P("vrow", "vcol", None, "pix"), P(), P(), P(), P())
    return jax.shard_map(
        body,
        mesh=mesh,
        in_specs=placed,
        out_specs=(P("vrow", "vcol", None, "pix"), P(), P(), P(), P()),
        check_vma=False,
    )
```

profile of v0, /device:TPU:1, one launch (start us, length us, event | category | flops | bytes accessed | tf_op | source)
XLA Modules:
  0.0 634.9 jit_solution(4711121955925792370)
XLA Ops:
  11.2 4.2 collective-permute-start
  17.9 3.8 collective-permute-done.1
  22.9 6.0 collective-permute-start.2
  31.6 20.1 %collective-permute-done.2 = bf16[12,2,192,128]{3,2,1,0:T(8,128)(2,1)} collective-permute-done((bf16[12,2,192,128]{3,2,1,0:T(8,128)(2,1)}, bf16[12,2,192,128]{3,2,1,0:T(8,128)(2,1)}, u32[]{:S(2)}, u32[]{:S(2)}) %collective-permute-start.2) | collective-permute-done | bytes 1179680 | tf_op jit(solution)/shard_map/while/body/eval_jaxpr/ppermute | solution.py:22
  51.6 4.9 collective-permute-done.3
  56.5 4.1 pad_maximum_fusion
  60.7 39.3 %while.71 = (s32[]{:T(128)}, f32[8,2,4,128]{3,2,1,0:T(4,128)S(1)}, f32[8,2,4,16,128]{4,3,2,1,0:T(8,128)S(1)}, bf16[12,6,192,128]{3,2,1,0:T(8,128)(2,1)}, f32[8,2...) while((s32[]{:T(128)}, f32[8,2,4,128]{3,2,1,0:T(4,128)S(1)}, ...), condition=%wide.region_5.6_spmd.clone, body=%wide.region_3.5_spmd.clone.sunk | while | flops 933911 | bytes 3342695 | solution.py:107
  101.6 1.9 collective-permute-start.4
  104.9 86.6 %while.72 = (s32[]{:T(128)}, f32[8,2,4,16,128]{4,3,2,1,0:T(8,128)}, bf16[12,6,192,128]{3,2,1,0:T(8,128)(2,1)}, f32[8,2,4,16,128]{4,3,2,1,0:T(8,128)S(1)}, f32[8,...) while((s32[]{:T(128)}, f32[8,2,4,16,128]{4,3,2,1,0:T(8,128)}, ...), condition=%wide.region_10.11_spmd.clone, body=%wide.region_7.10_spmd.clone.sunk | while | flops 1327127 | bytes 3146114 | solution.py:126
  106.4 1.9 fusion.55
  109.7 2.1 fusion.55
  113.2 2.1 fusion.55
  116.6 2.1 fusion.55
  120.1 2.1 fusion.55
  123.6 2.1 fusion.55
  127.0 2.1 fusion.55
  130.5 2.1 fusion.55
  134.0 2.1 fusion.55
  137.4 2.1 fusion.55
  140.9 2.1 fusion.55
  144.4 2.1 fusion.55
  147.8 2.1 fusion.55
  151.3 2.1 fusion.55
  154.8 2.1 fusion.55
  158.2 2.1 fusion.55
  161.7 2.1 fusion.55
  165.2 2.1 fusion.55
  168.6 2.1 fusion.55
  172.1 2.1 fusion.55
  175.6 2.1 fusion.55
  179.0 2.1 fusion.55
  182.5 2.1 fusion.55
  186.0 2.1 fusion.55
  189.4 2.1 fusion.55
  192.6 1.8 convolution_bitcast_fusion.3
  195.6 3.9 collective-permute-start.6
  203.3 12.4 %collective-permute-done.6 = f32[12,2,72,128]{3,2,1,0:T(8,128)S(1)} collective-permute-done((f32[12,2,72,128]{3,2,1,0:T(8,128)S(1)}, f32[12,2,72,128]{3,2,1,0:T(8,128)S(1)}, u32[]{:S(2)}, u32[]{:S(2)}) %collective-permute-start.6) | collective-permute-done | bytes 884768 | tf_op jit(solution)/shard_map/while/body/eval_jaxpr/ppermute | solution.py:22
  215.7 6.0 collective-permute-done.7
  221.7 2.7 pad_maximum_fusion.1
  224.3 123.5 %while.73 = (s32[]{:T(128)}, f32[8,2,4,16,128]{4,3,2,1,0:T(8,128)S(1)}, f32[8,2,4,16,128]{4,3,2,1,0:T(8,128)S(1)}, bf16[12,6,192,128]{3,2,1,0:T(8,128)(2,1)}, f3...) while((s32[]{:T(128)}, ...), condition=%wide.region_15.16_spmd.clone, body=%wide.region_12.15_spmd.clone.sunk | while | flops 1589273 | bytes 5046703 | solution.py:158
  229.3 1.5 fusion.56
  234.2 1.5 fusion.56
  239.2 1.5 fusion.56
  244.1 1.5 fusion.56
  249.1 1.5 fusion.56
  254.0 1.5 fusion.56
  258.9 1.5 fusion.56
  353.8 270.3 %all-reduce.3.cloned.1.call-done = (f32[64,64]{1,0:T(8,128)}, f32[64,128]{1,0:T(8,128)}, f32[64,64]{1,0:T(8,128)}, f32[64]{0:T(128)}) async-done(((f32[64,64]{1,0:T(8,128)}, f32[64,128]{1,0:T(8,128)}, f32[64,64]{1,0:T(8,128)}, f32[64]{0:T(128)}), (f32[64,64]{1,0:T(8,128)}, f32[64,128]{1,0:T(8,128)}, f32[64,64]{1,0:T(8,128)}, f32[64]{0:T(128)})) %all-reduce.3.cloned.1.call-update) | async-done | bytes 65808 | tf_op jit(solution)/shard_map/psum | solution.py:242
  (330 shorter events, 212.3 us)
Async XLA Ops:
  7.2 1.2 copy-start
  7.2 2.7 copy-start.2
  7.2 2.7 copy-start.16
  7.2 2.7 copy-start.14
  7.2 616.9 %all-reduce.3.cloned.1.call-start = ((), (), s32[]{:S(2)}) async-start(), calls=%async_computation | async-start | bytes 197632 | tf_op jit(solution)/shard_map/psum | solution.py:242
  9.7 13.2 %copy-start.4 = (f32[8,2,128,128]{3,2,1,0:T(8,128)}, f32[8,2,128,128]{3,2,1,0:T(8,128)S(1)}, u32[]{:S(2)}) copy-start(f32[8,2,128,128]{3,2,1,0:T(8,128)S(1)} %convolution_bitcast_fusion) | copy-start | bytes 3145732
  9.8 20.6 %copy-start.8 = (bf16[8,2,64,128]{3,2,1,0:T(8,128)(2,1)}, bf16[8,2,64,128]{3,2,1,0:T(8,128)(2,1)S(1)}, u32[]{:S(2)}) copy-start(bf16[8,2,64,128]{3,2,1,0:T(8,128)(2,1)S(1)} %slice.144) | copy-start | bytes 786436
  10.2 0.8 copy-start.5
  11.1 19.2 %copy-start.7 = (bf16[8,2,64,128]{3,2,1,0:T(8,128)(2,1)}, bf16[8,2,64,128]{3,2,1,0:T(8,128)(2,1)S(1)}, u32[]{:S(2)}) copy-start(bf16[8,2,64,128]{3,2,1,0:T(8,128)(2,1)S(1)} %bitcast_convert_fusion) | copy-start | bytes 786436
  11.2 19.3 %copy-start.17 = (bf16[64,64]{1,0:T(8,128)(2,1)S(1)}, bf16[64,64]{1,0:T(8,128)(2,1)}, u32[]{:S(2)}) copy-start(bf16[64,64]{1,0:T(8,128)(2,1)} %param.17) | copy-start | bytes 24580
  11.2 6.8 %collective-permute-start = (bf16[2,2,192,128]{3,2,1,0:T(8,128)(2,1)S(1)}, bf16[2,2,192,128]{3,2,1,0:T(8,128)(2,1)S(1)}, u32[]{:S(2)}, u32[]{:S(2)}) collective-permute-start(bf16[2,2,192,128]{3,2,1,0:T(8,128)(2,1)S(1)} %get-tuple-element.687), channel_id=1, source_target_pairs={{0,256},{1,257},{2,258},{3,259},{4,260},{5,261},{6,262},{7,263},{8... | collective-permute-start | bytes 589832 | tf_op jit(solution)/shard_map/while/body/eval_jaxpr/ppermute | solution.py:22
  15.3 6.4 %collective-permute-start.1 = (bf16[2,2,192,128]{3,2,1,0:T(8,128)(2,1)S(1)}, bf16[2,2,192,128]{3,2,1,0:T(8,128)(2,1)S(1)}, u32[]{:S(2)}, u32[]{:S(2)}) collective-permute-start(bf16[2,2,192,128]{3,2,1,0:T(8,128)(2,1)S(1)} %get-tuple-element.688), channel_id=1, source_target_pairs={{256,0},{257,1},{258,2},{259,3},{260,4},{261,5},{262,6},{263,7},{2... | collective-permute-start | bytes 589832 | tf_op jit(solution)/shard_map/while/body/eval_jaxpr/ppermute | solution.py:23
  17.9 12.3 %copy-start.11 = (bf16[2,2,192,128]{3,2,1,0:T(8,128)(2,1)}, bf16[2,2,192,128]{3,2,1,0:T(8,128)(2,1)S(1)}, u32[]{:S(2)}) copy-start(bf16[2,2,192,128]{3,2,1,0:T(8,128)(2,1)S(1)} %collective-permute-done) | copy-start | bytes 589828
  21.7 8.6 %copy-start.13 = (bf16[2,2,192,128]{3,2,1,0:T(8,128)(2,1)}, bf16[2,2,192,128]{3,2,1,0:T(8,128)(2,1)S(1)}, u32[]{:S(2)}) copy-start(bf16[2,2,192,128]{3,2,1,0:T(8,128)(2,1)S(1)} %collective-permute-done.1) | copy-start | bytes 589828
  22.9 28.8 %collective-permute-start.2 = (bf16[12,2,192,128]{3,2,1,0:T(8,128)(2,1)}, bf16[12,2,192,128]{3,2,1,0:T(8,128)(2,1)}, u32[]{:S(2)}, u32[]{:S(2)}) collective-permute-start(bf16[12,2,192,128]{3,2,1,0:T(8,128)(2,1)} %pad_maximum_fusion.2), channel_id=1, source_target_pairs={{0,32},{32,64},{64,96},{96,128},{128,160},{160,192},{192,224},{1,3... | collective-permute-start | bytes 3538952 | tf_op jit(solution)/shard_map/while/body/eval_jaxpr/ppermute | solution.py:22
  28.9 27.6 %collective-permute-start.3 = (bf16[12,2,192,128]{3,2,1,0:T(8,128)(2,1)}, bf16[12,2,192,128]{3,2,1,0:T(8,128)(2,1)}, u32[]{:S(2)}, u32[]{:S(2)}) collective-permute-start(bf16[12,2,192,128]{3,2,1,0:T(8,128)(2,1)} %pad_maximum_fusion.2), channel_id=1, source_target_pairs={{32,0},{64,32},{96,64},{128,96},{160,128},{192,160},{224,192},{33,... | collective-permute-start | bytes 3538952 | tf_op jit(solution)/shard_map/while/body/eval_jaxpr/ppermute | solution.py:23
  30.2 26.3 %copy-start.12 = (bf16[2,2,192,128]{3,2,1,0:T(8,128)(2,1)S(1)}, bf16[2,2,192,128]{3,2,1,0:T(8,128)(2,1)}, u32[]{:S(2)}) copy-start(bf16[2,2,192,128]{3,2,1,0:T(8,128)(2,1)} %copy-done.11) | copy-start | bytes 589828
  101.6 93.0 %collective-permute-start.4 = (f32[2,2,72,128]{3,2,1,0:T(8,128)}, f32[2,2,72,128]{3,2,1,0:T(8,128)}, u32[]{:S(2)}, u32[]{:S(2)}) collective-permute-start(f32[2,2,72,128]{3,2,1,0:T(8,128)} %get-tuple-element.689), channel_id=1, source_target_pairs={{0,256},{1,257},{2,258},{3,259},{4,260},{5,261},{6,262},{7,263},{8... | collective-permute-start | bytes 442376 | tf_op jit(solution)/shard_map/while/body/eval_jaxpr/ppermute | solution.py:22
  103.6 91.0 %collective-permute-start.5 = (f32[2,2,72,128]{3,2,1,0:T(8,128)}, f32[2,2,72,128]{3,2,1,0:T(8,128)}, u32[]{:S(2)}, u32[]{:S(2)}) collective-permute-start(f32[2,2,72,128]{3,2,1,0:T(8,128)} %get-tuple-element.690), channel_id=1, source_target_pairs={{256,0},{257,1},{258,2},{259,3},{260,4},{261,5},{262,6},{263,7},{2... | collective-permute-start | bytes 442376 | tf_op jit(solution)/shard_map/while/body/eval_jaxpr/ppermute | solution.py:23
  104.9 87.8 %copy-start.9 = (bf16[8,2,64,128]{3,2,1,0:T(8,128)(2,1)S(1)}, bf16[8,2,64,128]{3,2,1,0:T(8,128)(2,1)}, u32[]{:S(2)}) copy-start(bf16[8,2,64,128]{3,2,1,0:T(8,128)(2,1)} %param.13) | copy-start | bytes 786436
  104.9 89.6 %copy-start.6 = (f32[8,2,128,64]{2,3,1,0:T(8,128)S(1)}, f32[8,2,128,64]{2,3,1,0:T(8,128)}, u32[]{:S(2)}) copy-start(f32[8,2,128,64]{2,3,1,0:T(8,128)} %copy-done.5) | copy-start | bytes 1572868
  192.6 8.4 %copy-start.3 = (bf16[8,2,64,128]{3,2,1,0:T(8,128)(2,1)S(1)}, bf16[8,2,64,128]{3,2,1,0:T(8,128)(2,1)}, u32[]{:S(2)}) copy-start(bf16[8,2,64,128]{3,2,1,0:T(8,128)(2,1)} %param.12) | copy-start | bytes 786436
  194.5 7.6 %copy-start.15 = (bf16[64,64]{1,0:T(8,128)(2,1)S(1)}, bf16[64,64]{1,0:T(8,128)(2,1)}, u32[]{:S(2)}) copy-start(bf16[64,64]{1,0:T(8,128)(2,1)} %param.15) | copy-start | bytes 24580
  195.6 20.0 %collective-permute-start.6 = (f32[12,2,72,128]{3,2,1,0:T(8,128)S(1)}, f32[12,2,72,128]{3,2,1,0:T(8,128)S(1)}, u32[]{:S(2)}, u32[]{:S(2)}) collective-permute-start(f32[12,2,72,128]{3,2,1,0:T(8,128)S(1)} %pad_maximum_fusion.4), channel_id=1, source_target_pairs={{0,32},{32,64},{64,96},{96,128},{128,160},{160,192},{192,224},{1,3... | collective-permute-start | bytes 2654216 | tf_op jit(solution)/shard_map/while/body/eval_jaxpr/ppermute | solution.py:22
  199.6 22.1 %collective-permute-start.7 = (f32[12,2,72,128]{3,2,1,0:T(8,128)S(1)}, f32[12,2,72,128]{3,2,1,0:T(8,128)S(1)}, u32[]{:S(2)}, u32[]{:S(2)}) collective-permute-start(f32[12,2,72,128]{3,2,1,0:T(8,128)S(1)} %pad_maximum_fusion.4), channel_id=1, source_target_pairs={{32,0},{64,32},{96,64},{128,96},{160,128},{192,160},{224,192},{33,... | collective-permute-start | bytes 2654216 | tf_op jit(solution)/shard_map/while/body/eval_jaxpr/ppermute | solution.py:23
  203.3 21.1 %copy-start.1 = (f32[8,2,4,16,128]{4,3,2,1,0:T(8,128)S(1)}, f32[8,2,4,16,128]{4,3,2,1,0:T(8,128)}, u32[]{:S(2)}) copy-start(f32[8,2,4,16,128]{4,3,2,1,0:T(8,128)} %custom-call.3) | copy-start | bytes 1572868
  347.9 3.8 copy-start.10
Sparse Core Ops, SparseCore 0:
  353.1 271.0 all-reduce.2
where the time goes:
time: 641 us; the launch traced here: 635 us
  waiting for transfers between devices  319 us (50%)
  other arithmetic  239 us (37%)
  local copies, waits for them, and re-layouts  28 us (4%)
  starting transfers between devices  21.2 us (3%)
  between operations  14.5 us (2%)
  matrix products  9.47 us (1%)
    psum x1, waiting for transfers between devices, body(): lax.psum((query_part, keyval_part, output_part, gain_part), ('vrow', 'vco...  270 us
    add x25, other arithmetic, query_one_offset(): return query_accum + score_grad[:, :, :, None] * key_heads  51.8 us
    reduce_sum x25, other arithmetic, key_one_offset(): jnp.sum(queries * key_heads, axis=3) * score_scale  36.5 us
    ppermute x4, waiting for transfers between devices, extended(): before = lax.ppermute(last, axis, up)  33.8 us
    reduce_sum x25, other arithmetic, query_one_offset(): jnp.sum(query_heads * key_heads, axis=3) * score_scale  33.7 us
    add x25, other arithmetic, key_one_offset(): value_accum + attn_prob[:, :, :, None] * out_heads  31.5 us
    add x25, other arithmetic, key_one_offset(): key_accum + score_grad[:, :, :, None] * queries  29.8 us
    slice x25, local copies, waits for them, and re-layouts, attend_one_offset(): values = split_heads(window[:, :, 2 * channels:])  27.1 us
  transfers between devices with their start and end apart: 9, of which 7 were waited for; matrix products, arithmetic and copies ran while one was open for 15% of the time, Pallas kernels for 0%

commit v1 on v0

v1 whole, which is shorter than its diff:
```python
import math

import jax
import jax.numpy as jnp
from jax import lax
from jax.experimental import pallas as pl
from jax.experimental.pallas import tpu as pltpu
from jax.sharding import PartitionSpec as P

HEADS = 4
SIZE = 16
CH = 64
ROWS = 8
COLS = 2
PIX = 128
S = 13
EPSILON = 1e-06
SCALE = SIZE ** (-0.5)
F32 = jnp.float32
BF16 = jnp.bfloat16

VM = pl.BlockSpec(memory_space=pltpu.VMEM)
SM = pl.BlockSpec(memory_space=pltpu.SMEM)


def inv_rms(values):
    return lax.rsqrt(jnp.mean(values * values, axis=0, keepdims=True) + EPSILON)


def total(terms):
    terms = list(terms)
    while len(terms) > 1:
        terms = [a + b for a, b in zip(terms[::2], terms[1::2])] + (
            [terms[-1]] if len(terms) % 2 else []
        )
    return terms[0]


def normed_pair(ref, row, gain):
    out = []
    for j in range(2):
        values = ref[row, j].astype(F32)
        out.append((values * inv_rms(values) * gain).astype(BF16))
    return jnp.concatenate(out, axis=1)


def put(ref, col, row, values):
    ref[col, pl.ds(row, values.shape[0], stride=S), :] = values


def take(ref, col, start):
    return ref[col, pl.ds(start, ROWS), :]


def each_piece(own, left, right, row_halo, left_corner, right_corner, halo_row, visit):
    def big(row, carry):
        visit(own, row, row + 2, 2)
        visit(left, row, row + 2, 0)
        visit(right, row, row + 2, 4)
        return carry

    def small(row, carry):
        visit(row_halo, row, row + halo_row, 2)
        visit(left_corner, row, row + halo_row, 0)
        visit(right_corner, row, row + halo_row, 4)
        return carry

    lax.fori_loop(0, ROWS, big, 0)
    lax.fori_loop(0, 2, small, 0)


def halo_start(side_ref):
    side = side_ref[0]
    return 10 - 10 * side, 10 * side


def clear_rows(refs, row):
    for ref in refs:
        zeros = jnp.zeros((ref.shape[1] // S, PIX), F32)
        for col in range(6):
            put(ref, col, row, zeros)
            put(ref, col, row + 1, zeros)


def forward_kernel(
    side, own, left, right, row_halo, left_corner, right_corner, cot, gain, w_in, w_out,
    qs, ks, vs, q_inv, k_inv, weights, prob_grads, attended, stats, ogs,
):
    halo_row, clear_row = halo_start(side)
    clear_rows((qs, ks, vs), clear_row)
    gain_full = gain[...]
    w_full = w_in[...]

    def visit(ref, row, to_row, col):
        normed = normed_pair(ref, row, gain_full)
        raw = jnp.dot(w_full, normed, preferred_element_type=F32)
        for j in range(2):
            part = raw[:, j * PIX : (j + 1) * PIX]
            query, key, value = part[:CH], part[CH : 2 * CH], part[2 * CH :]
            query_scale, key_scale = inv_rms(query), inv_rms(key)
            put(qs, col + j, to_row, (query * query_scale).astype(BF16).astype(F32))
            put(ks, col + j, to_row, (key * key_scale).astype(BF16).astype(F32))
            put(vs, col + j, to_row, value.astype(BF16).astype(F32))
            if ref is own:
                q_inv[j, pl.ds(row, 1), :] = query_scale
                k_inv[j, pl.ds(row, 1), :] = key_scale

    each_piece(own, left, right, row_halo, left_corner, right_corner, halo_row, visit)

    w_o = w_out[...]

    def own_out(row, carry):
        both = jnp.concatenate([cot[row, 0], cot[row, 1]], axis=1)
        og = jnp.dot(w_o, both, preferred_element_type=F32)
        for j in range(2):
            put(ogs, j, row, og[:, j * PIX : (j + 1) * PIX])
        return carry

    lax.fori_loop(0, ROWS, own_out, 0)

    def attend(step, carry):
        col, head = step // HEADS, step % HEADS
        base = head * (SIZE * S)
        query = [take(qs, col + 2, base + d * S + 2) * SCALE for d in range(SIZE)]
        og = [take(ogs, col, base + d * S) for d in range(SIZE)]
        acc = [jnp.zeros((ROWS, PIX), F32)] * SIZE
        exp_total = jnp.zeros((ROWS, PIX), F32)
        spread = jnp.zeros((ROWS, PIX), F32)
        for j in range(5):
            for i in range(5):
                key = [take(ks, col + j, base + d * S + i) for d in range(SIZE)]
                weight = jnp.exp(total(a * b for a, b in zip(query, key)))
                value = [take(vs, col + j, base + d * S + i) for d in range(SIZE)]
                prob_grad = total(a * b for a, b in zip(og, value))
                acc = [a + weight * b for a, b in zip(acc, value)]
                exp_total = exp_total + weight
                spread = spread + weight * prob_grad
                weights[step, 5 * j + i] = weight
                prob_grads[step, 5 * j + i] = prob_grad
        inv_total = 1.0 / exp_total
        for d in range(SIZE):
            attended[col, pl.ds(pl.multiple_of((head * SIZE + d) * ROWS, ROWS), ROWS), :] = (
                acc[d] * inv_total
            )
        stats[pl.ds(col * 8 + head, ROWS, stride=16), :] = inv_total
        stats[pl.ds(col * 8 + 4 + head, ROWS, stride=16), :] = spread * inv_total
        return carry

    lax.fori_loop(0, COLS * HEADS, attend, 0)


def unit_back(unit, scale, upstream):
    mean = jnp.sum(upstream * unit, axis=0, keepdims=True) * (1.0 / CH)
    return scale[None] * (upstream - unit * mean)


def own_channels(ref, col):
    return jnp.stack([take(ref, col + 2, d * S + 2) for d in range(CH)], axis=0)


def query_kernel(qs, ks, weights, prob_grads, stats, attended, cot, q_inv, raw_query, out_part, grads):
    def query_one(step, carry):
        col, head = step // HEADS, step % HEADS
        base = head * (SIZE * S)
        inv_total = stats[pl.ds(col * 8 + head, ROWS, stride=16), :]
        spread = stats[pl.ds(col * 8 + 4 + head, ROWS, stride=16), :]
        inv_total = inv_total * SCALE
        acc = [jnp.zeros((ROWS, PIX), F32)] * SIZE
        for j in range(5):
            for i in range(5):
                o = 5 * j + i
                score_grad = weights[step, o] * inv_total * (prob_grads[step, o] - spread)
                acc = [a + score_grad * take(ks, col + j, base + d * S + i) for d, a in enumerate(acc)]
        for d in range(SIZE):
            grads[col, head * SIZE + d] = acc[d]
        return carry

    lax.fori_loop(0, COLS * HEADS, query_one, 0)

    def finish(col, carry):
        raw = unit_back(own_channels(qs, col), q_inv[col], grads[col])
        raw_query[col] = raw.reshape(CH * ROWS, PIX)
        return carry

    lax.fori_loop(0, COLS, finish, 0)

    def out_grads(row, acc):
        mixed = [attended[j, pl.ds(row, CH, stride=ROWS), :].astype(BF16) for j in range(2)]
        return acc + lax.dot_general(
            jnp.concatenate(mixed, axis=1),
            jnp.concatenate([cot[row, 0], cot[row, 1]], axis=1),
            (((1,), (1,)), ((), ())),
            preferred_element_type=F32,
        )

    out_part[...] = lax.fori_loop(0, ROWS, out_grads, jnp.zeros((CH, CH), F32))


def key_kernel(
    side, qs, ks, vs, k_inv, raw_query, out_part,
    own, left, right, row_halo, left_corner, right_corner,
    own_st, left_st, right_st, row_st, left_corner_st, right_corner_st,
    feats, gain, w_back, w_out,
    feats_grad, weight_sums,
    ogs, sts, grads, raws,
):
    halo_row, clear_row = halo_start(side)
    clear_rows((ogs, sts), clear_row)
    w_o = w_out[...]

    def visit(ref, row, to_row, col):
        both = jnp.concatenate([ref[row, 0], ref[row, 1]], axis=1)
        og = jnp.dot(w_o, both, preferred_element_type=F32)
        for j in range(2):
            put(ogs, col + j, to_row, og[:, j * PIX : (j + 1) * PIX])

    each_piece(own, left, right, row_halo, left_corner, right_corner, halo_row, visit)

    def visit_stats(ref, row, to_row, col):
        for j in range(2):
            put(sts, col + j, to_row, ref[row, j])

    each_piece(
        own_st, left_st, right_st, row_st, left_corner_st, right_corner_st, halo_row, visit_stats
    )

    def key_one(step, carry):
        col, head = step // HEADS, step % HEADS
        base = head * (SIZE * S)
        key_acc = [jnp.zeros((ROWS, PIX), F32)] * SIZE
        value_acc = [jnp.zeros((ROWS, PIX), F32)] * SIZE
        for j in range(5):
            for i in range(5):
                query = [take(qs, col + j, base + d * S + i) for d in range(SIZE)]
                key = [take(ks, col + 2, base + d * S + 2) for d in range(SIZE)]
                inv_total = take(sts, col + j, head * S + i)
                spread = take(sts, col + j, (head + HEADS) * S + i)
                score = total(a * b for a, b in zip(query, key))
                prob = jnp.exp(score * SCALE) * inv_total
                og = [take(ogs, col + j, base + d * S + i) for d in range(SIZE)]
                value = [take(vs, col + 2, base + d * S + 2) for d in range(SIZE)]
                prob_grad = total(a * b for a, b in zip(og, value))
                score_grad = prob * (prob_grad - spread)
                key_acc = [a + score_grad * b for a, b in zip(key_acc, query)]
                value_acc = [a + prob * b for a, b in zip(value_acc, og)]
        for d in range(SIZE):
            grads[col, head * SIZE + d] = key_acc[d] * SCALE
            raws[col, pl.ds(pl.multiple_of((2 * CH + head * SIZE + d) * ROWS, ROWS), ROWS), :] = (
                value_acc[d]
            )
        return carry

    lax.fori_loop(0, COLS * HEADS, key_one, 0)

    def finish(col, carry):
        raw = unit_back(own_channels(ks, col), k_inv[col], grads[col])
        raws[col, CH * ROWS : 2 * CH * ROWS, :] = raw.reshape(CH * ROWS, PIX)
        raws[col, 0 : CH * ROWS, :] = raw_query[col]
        return carry

    lax.fori_loop(0, COLS, finish, 0)

    gain_full = gain[...]
    w_b = w_back[...]

    def view_row(row, acc):
        raw = jnp.concatenate(
            [raws[j, pl.ds(row, 3 * CH, stride=ROWS), :].astype(BF16) for j in range(2)], axis=1
        )
        normed_grad = jnp.dot(w_b, raw, preferred_element_type=F32)
        normed = []
        for j in range(2):
            values = feats[row, j].astype(F32)
            inv_norm = inv_rms(values)
            scaled = values * inv_norm
            normed.append((scaled * gain_full).astype(BF16))
            scaled_grad = normed_grad[:, j * PIX : (j + 1) * PIX] * gain_full
            mean = jnp.mean(scaled_grad * scaled, axis=0, keepdims=True)
            branch = inv_norm * (scaled_grad - scaled * mean)
            feats_grad[row, j] = (own[row, j].astype(F32) + branch).astype(BF16)
        return acc + lax.dot_general(
            jnp.concatenate(normed, axis=1),
            raw,
            (((1,), (1,)), ((), ())),
            preferred_element_type=F32,
        )

    sums = lax.fori_loop(0, ROWS, view_row, jnp.zeros((CH, 3 * CH), F32))
    weight_sums[0:CH, :] = sums[:, CH:]
    weight_sums[CH : 2 * CH, :] = jnp.concatenate([sums[:, :CH], out_part[...]], axis=1)


def call(kernel, outs, scratch, flops, *operands):
    return pl.pallas_call(
        kernel,
        out_shape=[jax.ShapeDtypeStruct(shape, dtype) for shape, dtype in outs],
        in_specs=[SM if x.dtype == jnp.int32 else VM for x in operands],
        out_specs=[VM] * len(outs),
        scratch_shapes=[pltpu.VMEM(shape, F32) for shape in scratch],
        compiler_params=pltpu.CompilerParams(vmem_limit_bytes=40 * 1024 * 1024),
        cost_estimate=pl.CostEstimate(flops=flops, bytes_accessed=1000000, transcendentals=0),
    )(*operands)


def neighbours(shard, row_edge):
    rows, cols = lax.axis_size("vrow"), lax.axis_size("vcol")
    up = [(i, i + 1) for i in range(cols - 1)]
    down = [(j, i) for i, j in up]
    cross = [(0, 1), (1, 0)]
    diag_up = [(a * cols + i, b * cols + j) for a, b in cross for i, j in up]
    diag_down = [(a * cols + i, b * cols + j) for a, b in cross for i, j in down]
    left = lax.ppermute(shard, "vcol", up)
    right = lax.ppermute(shard, "vcol", down)
    left_corner = lax.ppermute(row_edge, ("vrow", "vcol"), diag_up)
    right_corner = lax.ppermute(row_edge, ("vrow", "vcol"), diag_down)
    row_halo = lax.ppermute(row_edge, "vrow", cross)
    return left, right, row_halo, left_corner, right_corner


def sum_everywhere(values):
    group = ("vrow", "vcol")
    count, pix_count = lax.axis_size("vrow") * lax.axis_size("vcol"), lax.axis_size("pix")
    shares = lax.all_to_all(values.reshape(count, -1, PIX), group, 0, 0)
    share = jnp.sum(shares, axis=0)
    copies = jnp.broadcast_to(share[None], (pix_count,) + share.shape)
    share = jnp.sum(lax.all_to_all(copies, "pix", 0, 0), axis=0)
    copies = jnp.broadcast_to(share[None], (count,) + share.shape)
    return lax.all_to_all(copies, group, 0, 0).reshape(values.shape)


def body(features, out_cotangent, norm_gain, query_proj, keyval_proj, output_proj):
    vrow = lax.axis_index("vrow").astype(jnp.int32)
    side = vrow.reshape(1)
    edge_start = 6 - 6 * vrow

    def edge(values):
        return lax.dynamic_slice_in_dim(values, edge_start, 2, 0)

    feat_halo = neighbours(features, edge(features))
    cot_halo = neighbours(out_cotangent, edge(out_cotangent))

    gain = jnp.broadcast_to(norm_gain[:, None], (CH, PIX))
    w_back = jnp.concatenate([query_proj, keyval_proj], axis=1)
    w_in = w_back.T

    padded = ((6, CH * S, PIX), F32)
    lanes = ((COLS, ROWS, PIX), F32)
    offsets = ((COLS * HEADS, 25, ROWS, PIX), F32)
    channels = ((COLS, CH * ROWS, PIX), F32)
    qs, ks, vs, q_inv, k_inv, weights, prob_grads, attended, stats = call(
        forward_kernel,
        [padded, padded, padded, lanes, lanes, offsets, offsets, channels, ((ROWS * 16, PIX), F32)],
        [(COLS, CH * S, PIX)],
        4000000,
        side, features, *feat_halo, out_cotangent, gain, w_in, output_proj,
    )
    stats_view = stats.reshape(ROWS, COLS, 8, PIX)
    stats_halo = neighbours(stats_view, edge(stats_view))
    raw_query, out_part = call(
        query_kernel,
        [channels, ((CH, CH), F32)],
        [(COLS, CH, ROWS, PIX)],
        4000000,
        qs, ks, weights, prob_grads, stats, attended, out_cotangent, q_inv,
    )
    features_grad, weight_sums = call(
        key_kernel,
        [(features.shape, BF16), ((2 * CH, PIX), F32)],
        [(6, CH * S, PIX), (6, 8 * S, PIX), (COLS, CH, ROWS, PIX), (COLS, 3 * CH * ROWS, PIX)],
        4000000,
        side, qs, ks, vs, k_inv, raw_query, out_part,
        out_cotangent, *cot_halo, stats_view, *stats_halo,
        features, gain, w_back, output_proj,
    )
    tokens_all = (
        ROWS * COLS * PIX
        * lax.axis_size("vrow") * lax.axis_size("vcol") * lax.axis_size("pix")
    )
    sums = sum_everywhere(weight_sums) * (1.0 / math.sqrt(tokens_all))
    keyval_grad, query_grad, output_grad = sums[:CH], sums[CH:, :CH], sums[CH:, CH:]
    gain_grad = (
        jnp.sum(query_grad * query_proj.astype(F32), axis=1)
        + jnp.sum(keyval_grad * keyval_proj.astype(F32), axis=1)
    ) / norm_gain
    return features_grad, query_grad, keyval_grad, output_grad, gain_grad


def solution(mesh):
    placed = (P("vrow", "vcol", None, "pix"), P("vrow", "vcol", None, "pix"), P(), P(), P(), P())
    return jax.shard_map(
        body,
        mesh=mesh,
        in_specs=placed,
        out_specs=(P("vrow", "vcol", None, "pix"), P(), P(), P(), P()),
        check_vma=False,
    )
```

time: 641 us -> 133 us (0.21)
  waiting for transfers between devices: 319 us -> 1.85 us
  other arithmetic: 239 us -> 2.92 us
  blocking collectives: 0 us -> 54.5 us
  starting transfers between devices: 21.2 us -> 47.1 us
  local copies, waits for them, and re-layouts: 28 us -> 5.24 us
  Pallas kernels: 0 us -> 19.4 us
  between operations: 14.5 us -> 0.94 us
  matrix products: 9.47 us -> 0 us
    psum x1 -> x0, waiting for transfers between devices: 270 us -> none  [body(): lax.psum((query_part, keyval_part, output_part, gain_part), ('vrow', 'vco...]
    add x100 -> x0, other arithmetic: 119 us -> none  [the longest x25 51.8 us: query_one_offset(): return query_accum + score_grad[:, :, :, None] * key_heads]
    reduce_sum x79 -> x4, other arithmetic: 76.7 us -> 1.57 us  [the longest x1 0.79 us: body(): jnp.sum(query_grad * query_proj.astype(F32), axis=1)]
    all_to_all x0 -> x3, blocking collectives: none -> 54.5 us  [the longest x1 26.4 us: sum_everywhere(): share = jnp.sum(lax.all_to_all(copies, 'pix', 0, 0), axis=0)]
    ppermute x8 -> x15, waiting for transfers between devices: 48.4 us -> 1.85 us  [the longest x3 1.82 us: neighbours(): right_corner = lax.ppermute(row_edge, ('vrow', 'vcol'), diag_down)]
    mul x57 -> x1, other arithmetic: 31 us -> 0.01 us  [body(): sums = sum_everywhere(weight_sums) * (1.0 / math.sqrt(tokens_all))]
    slice x26 -> x0, local copies, waits for them, and re-layouts: 27.1 us -> none  [the longest x25 27.1 us: attend_one_offset(): values = split_heads(window[:, :, 2 * channels:])]
    ppermute x8 -> x15, starting transfers between devices: 21.2 us -> 47.1 us  [the longest x3 15.7 us: neighbours(): left_corner = lax.ppermute(row_edge, ('vrow', 'vcol'), diag_up)]
  transfers between devices with their start and end apart: 9 -> 15, of which waited for: 7 -> 1; matrix products, arithmetic and copies ran while one was open for 15% -> 3% of each run, Pallas kernels for 0% -> 7%
where the time goes in v1:
time: 133 us; the launch traced here: 132 us
  blocking collectives  54.5 us (41%)
  starting transfers between devices  47.1 us (35%)
  Pallas kernels  19.4 us (15%)
  local copies, waits for them, and re-layouts  5.24 us (4%)
  other arithmetic  2.92 us (2%)
  waiting for transfers between devices  1.85 us (1%)
    all_to_all x1, blocking collectives, sum_everywhere(): share = jnp.sum(lax.all_to_all(copies, 'pix', 0, 0), axis=0)  26.4 us
    pallas_call x3, Pallas kernels, call(): pl.pallas_call(kernel, out_shape=[jax.ShapeDtypeStruct(shape, dtype) for...  19.4 us
    all_to_all x1, blocking collectives, sum_everywhere(): shares = lax.all_to_all(values.reshape(count, -1, PIX), group, 0, 0)  18.1 us
    ppermute x3, starting transfers between devices, neighbours(): left_corner = lax.ppermute(row_edge, ('vrow', 'vcol'), diag_up)  15.7 us
    ppermute x3, starting transfers between devices, neighbours(): left = lax.ppermute(shard, 'vcol', up)  15.1 us
    all_to_all x1, blocking collectives, sum_everywhere(): return lax.all_to_all(copies, group, 0, 0).reshape(values.shape)  9.99 us
    ppermute x3, starting transfers between devices, neighbours(): row_halo = lax.ppermute(row_edge, 'vrow', cross)  8.58 us
    ppermute x3, starting transfers between devices, neighbours(): right = lax.ppermute(shard, 'vcol', down)  3.88 us
  transfers between devices with their start and end apart: 15, of which 1 were waited for; matrix products, arithmetic and copies ran while one was open for 3% of the time, Pallas kernels for 7%

profile of v1, /device:TPU:1, one launch (start us, length us, event | category | flops | bytes accessed | tf_op | source)
XLA Modules:
  0.0 131.9 jit_solution(12320674320246066540)
XLA Ops:
  0.6 4.8 %collective-permute-start = (bf16[8,2,64,128]{3,2,1,0:T(8,128)(2,1)}, bf16[8,2,64,128]{3,2,1,0:T(8,128)(2,1)S(1)}, u32[]{:S(2)}, u32[]{:S(2)}) collective-permute-start(bf16[8,2,64,128]{3,2,1,0:T(8,128)(2,1)} %feats.1), channel_id=1, source_target_pairs={{0,32},{32,64},{64,96},{96,128},{128,160},{160,192},{192,224},{1,3... | collective-permute-start | bytes 786440 | tf_op jit(solution)/shard_map/ppermute | solution.py:312
  5.5 0.9 constant_dynamic-slice_fusion.2
  6.4 3.2 %collective-permute-start.2 = (bf16[2,2,64,128]{3,2,1,0:T(8,128)(2,1)S(1)}, bf16[2,2,64,128]{3,2,1,0:T(8,128)(2,1)S(1)}, u32[]{:S(2)}, u32[]{:S(2)}) collective-permute-start(bf16[2,2,64,128]{3,2,1,0:T(8,128)(2,1)S(1)} %constant_dynamic-slice_fusion.2), channel_id=1, source_target_pairs={{0,256},{256,0},{1,257},{257,1},{2,258},{258,2},{3,259},{259,3},{4... | collective-permute-start | bytes 196616 | tf_op jit(solution)/shard_map/ppermute | solution.py:316
  9.6 3.8 %collective-permute-start.3 = (bf16[2,2,64,128]{3,2,1,0:T(8,128)(2,1)S(1)}, bf16[2,2,64,128]{3,2,1,0:T(8,128)(2,1)S(1)}, u32[]{:S(2)}, u32[]{:S(2)}) collective-permute-start(bf16[2,2,64,128]{3,2,1,0:T(8,128)(2,1)S(1)} %constant_dynamic-slice_fusion.2), channel_id=1, source_target_pairs={{0,288},{32,320},{64,352},{96,384},{128,416},{160,448},{192,480},{... | collective-permute-start | bytes 196616 | tf_op jit(solution)/shard_map/ppermute | solution.py:314
  13.4 1.3 collective-permute-start.1
  14.7 1.3 collective-permute-start.4
  16.0 0.0 collective-permute-done.2.row_halo
  16.0 5.3 %collective-permute-start.5 = (bf16[8,2,64,128]{3,2,1,0:T(8,128)(2,1)}, bf16[8,2,64,128]{3,2,1,0:T(8,128)(2,1)S(1)}, u32[]{:S(2)}, u32[]{:S(2)}) collective-permute-start(bf16[8,2,64,128]{3,2,1,0:T(8,128)(2,1)} %own.3), channel_id=1, source_target_pairs={{0,32},{32,64},{64,96},{96,128},{128,160},{160,192},{192,224},{1,3... | collective-permute-start | bytes 786440 | tf_op jit(solution)/shard_map/ppermute | solution.py:312
  21.3 0.0 collective-permute-done.3.left_corner
  21.3 1.3 collective-permute-start.6
  22.6 0.9 constant_dynamic-slice_fusion.1
  23.5 3.2 %collective-permute-start.7 = (bf16[2,2,64,128]{3,2,1,0:T(8,128)(2,1)S(1)}, bf16[2,2,64,128]{3,2,1,0:T(8,128)(2,1)S(1)}, u32[]{:S(2)}, u32[]{:S(2)}) collective-permute-start(bf16[2,2,64,128]{3,2,1,0:T(8,128)(2,1)S(1)} %constant_dynamic-slice_fusion.1), channel_id=1, source_target_pairs={{0,256},{256,0},{1,257},{257,1},{2,258},{258,2},{3,259},{259,3},{4... | collective-permute-start | bytes 196616 | tf_op jit(solution)/shard_map/ppermute | solution.py:316
  26.7 5.7 %collective-permute-start.8 = (bf16[2,2,64,128]{3,2,1,0:T(8,128)(2,1)S(1)}, bf16[2,2,64,128]{3,2,1,0:T(8,128)(2,1)S(1)}, u32[]{:S(2)}, u32[]{:S(2)}) collective-permute-start(bf16[2,2,64,128]{3,2,1,0:T(8,128)(2,1)S(1)} %constant_dynamic-slice_fusion.1), channel_id=1, source_target_pairs={{0,288},{32,320},{64,352},{96,384},{128,416},{160,448},{192,480},{... | collective-permute-start | bytes 196616 | tf_op jit(solution)/shard_map/ppermute | solution.py:314
  32.4 0.8 pad_maximum_fusion
  33.2 0.1 copy.12.w_in
  33.3 0.0 collective-permute-done.1.right
  33.4 1.3 collective-permute-start.9
  34.7 0.7 broadcast_in_dim.6.gain
  35.4 1.0 copy-done
  36.3 0.9 copy-done.1
  37.3 0.7 copy-done.2
  38.0 7.4 %shard_map.101 = (f32[6,832,128]{2,1,0:T(8,128)S(1)}, f32[6,832,128]{2,1,0:T(8,128)S(1)}, f32[6,832,128]{2,1,0:T(8,128)S(1)}, f32[2,8,128]{2,1,0:T(8,128)S(1)}, ...) custom-call(s32[1]{0:T(128)} %bitcast.side, ...), custom_call_target="tpu_custom_call" | custom-call | flops 4000000 | bytes 1000000 | tf_op jit(solution)/shard_map/pallas_call | solution.py:294
  45.4 0.0 collective-permute-done.7.row_halo
  45.4 5.0 %collective-permute-start.10 = (f32[8,2,8,128]{3,2,1,0:T(8,128)S(1)}, f32[8,2,8,128]{3,2,1,0:T(8,128)S(1)}, u32[]{:S(2)}, u32[]{:S(2)}) collective-permute-start(f32[8,2,8,128]{3,2,1,0:T(8,128)S(1)} %bitcast.10), channel_id=1, source_target_pairs={{0,32},{32,64},{64,96},{96,128},{128,160},{160,192},{192,224},{1,3... | collective-permute-start | bytes 196616 | tf_op jit(solution)/shard_map/ppermute | solution.py:312
  50.4 0.0 collective-permute-done.8.left_corner
  50.4 1.3 collective-permute-start.11
  51.7 0.0 collective-permute-done.9.right_corner
  51.7 2.2 %collective-permute-start.12 = (f32[2,2,8,128]{3,2,1,0:T(8,128)S(1)}, f32[2,2,8,128]{3,2,1,0:T(8,128)S(1)}, u32[]{:S(2)}, u32[]{:S(2)}) collective-permute-start(f32[2,2,8,128]{3,2,1,0:T(8,128)S(1)} %constant_dynamic-slice_fusion), channel_id=1, source_target_pairs={{0,256},{256,0},{1,257},{257,1},{2,258},{258,2},{3,259},{259,3},{4... | collective-permute-start | bytes 49160 | tf_op jit(solution)/shard_map/ppermute | solution.py:316
  53.9 0.0 collective-permute-done.5.left
  53.9 6.1 %collective-permute-start.13 = (f32[2,2,8,128]{3,2,1,0:T(8,128)S(1)}, f32[2,2,8,128]{3,2,1,0:T(8,128)S(1)}, u32[]{:S(2)}, u32[]{:S(2)}) collective-permute-start(f32[2,2,8,128]{3,2,1,0:T(8,128)S(1)} %constant_dynamic-slice_fusion), channel_id=1, source_target_pairs={{0,288},{32,320},{64,352},{96,384},{128,416},{160,448},{192,480},{... | collective-permute-start | bytes 49160 | tf_op jit(solution)/shard_map/ppermute | solution.py:314
  60.1 1.3 collective-permute-start.14
  61.4 0.0 copy-start.3
  61.4 2.4 %shard_map.102 = (f32[2,512,128]{2,1,0:T(8,128)S(1)}, f32[64,64]{1,0:T(8,128)S(1)}) custom-call(f32[6,832,128]{2,1,0:T(8,128)S(1)} %get-tuple-element.18.qs, f32[6,832,128]{2,1,0:T(8,128)S(1)} %get-tuple-element.19.ks, f32[8,25,8,128]{3,2,1,0:T(8,128)S(1)} %get-tuple-element.22.weights, f32[8,25,8,128]{3,2,1,0:T(8,128)S(1)} %get-tuple-element.23.prob_grads, ...), custom_call_target="tpu_custom_call" | custom-call | flops 4000000 | bytes 1000000 | tf_op jit(solution)/shard_map/pallas_call | solution.py:294
  63.8 0.0 collective-permute-done.12.row_st
  63.8 0.0 collective-permute-done.13.left_corner_st
  63.8 1.8 %collective-permute-done.14.right_corner_st = f32[2,2,8,128]{3,2,1,0:T(8,128)S(1)} collective-permute-done((f32[2,2,8,128]{3,2,1,0:T(8,128)S(1)}, f32[2,2,8,128]{3,2,1,0:T(8,128)S(1)}, u32[]{:S(2)}, u32[]{:S(2)}) %collective-permute-start.14) | collective-permute-done | bytes 16416 | tf_op jit(solution)/shard_map/ppermute | solution.py:315
  65.6 0.0 collective-permute-done.10.left_st
  65.6 0.0 collective-permute-done.11.right_st
  65.7 0.0 copy-start.4
  65.7 0.0 copy-start.5
  65.7 0.0 copy-start.6
  65.7 9.6 %shard_map.103 = (bf16[8,2,64,128]{3,2,1,0:T(8,128)(2,1)}, f32[128,128]{1,0:T(8,128)S(1)}) custom-call(s32[1]{0:T(128)} %bitcast.side, f32[6,832,128]{2,1,0:T(8,128)S(1)} %get-tuple-element.18.qs, f32[6,832,128]{2,1,0:T(8,128)S(1)} %get-tuple-element.19.ks, f32[6,832,128]{2,1,0:T(8,128)S(1)} %get-tuple-element.20.vs, ...), custom_call_target="tpu_custom_call" | custom-call | flops 4000000 | bytes 1000000 | tf_op jit(solution)/shard_map/pallas_call | solution.py:294
  75.3 18.1 %all_to_all.15 = f32[16,8,128]{2,1,0:T(8,128)S(1)} all-to-all(f32[16,8,128]{2,1,0:T(8,128)S(1)} %bitcast.14), channel_id=1, replica_groups=mesh['vrow'=2,'vcol'=8,'pix'=32] {'vrow','vcol'}, dimensions={0} | all-to-all | bytes 131072 | tf_op jit(solution)/shard_map/all_to_all | solution.py:323
  93.4 26.4 %all_to_all.16 = f32[32,8,128]{2,1,0:T(8,128)S(1)} all-to-all(f32[32,8,128]{2,1,0:T(8,128)S(1)} %broadcast_in_dim.7), channel_id=1, replica_groups=mesh['vrow'=2,'vcol'=8,'pix'=32] {'pix'}, dimensions={0} | all-to-all | bytes 262144 | tf_op jit(solution)/shard_map/all_to_all | solution.py:326
  119.9 10.0 %all_to_all.17 = f32[16,8,128]{2,1,0:T(8,128)S(1)} all-to-all(f32[16,8,128]{2,1,0:T(8,128)S(1)} %broadcast_in_dim.8), channel_id=1, replica_groups=mesh['vrow'=2,'vcol'=8,'pix'=32] {'vrow','vcol'}, dimensions={0} | all-to-all | bytes 131072 | tf_op jit(solution)/shard_map/all_to_all | solution.py:328
  129.9 0.8 multiply_reduce_fusion.1
  130.7 0.7 multiply_reduce_fusion
  131.4 0.5 add_divide_fusion
  (16 shorter events, 0.1 us)
Async XLA Ops:
  0.6 26.0 %collective-permute-start = (bf16[8,2,64,128]{3,2,1,0:T(8,128)(2,1)}, bf16[8,2,64,128]{3,2,1,0:T(8,128)(2,1)S(1)}, u32[]{:S(2)}, u32[]{:S(2)}) collective-permute-start(bf16[8,2,64,128]{3,2,1,0:T(8,128)(2,1)} %feats.1), channel_id=1, source_target_pairs={{0,32},{32,64},{64,96},{96,128},{128,160},{160,192},{192,224},{1,3... | collective-permute-start | bytes 786440 | tf_op jit(solution)/shard_map/ppermute | solution.py:312
  6.4 9.7 %collective-permute-start.2 = (bf16[2,2,64,128]{3,2,1,0:T(8,128)(2,1)S(1)}, bf16[2,2,64,128]{3,2,1,0:T(8,128)(2,1)S(1)}, u32[]{:S(2)}, u32[]{:S(2)}) collective-permute-start(bf16[2,2,64,128]{3,2,1,0:T(8,128)(2,1)S(1)} %constant_dynamic-slice_fusion.2), channel_id=1, source_target_pairs={{0,256},{256,0},{1,257},{257,1},{2,258},{258,2},{3,259},{259,3},{4... | collective-permute-start | bytes 196616 | tf_op jit(solution)/shard_map/ppermute | solution.py:316
  9.6 11.8 %collective-permute-start.3 = (bf16[2,2,64,128]{3,2,1,0:T(8,128)(2,1)S(1)}, bf16[2,2,64,128]{3,2,1,0:T(8,128)(2,1)S(1)}, u32[]{:S(2)}, u32[]{:S(2)}) collective-permute-start(bf16[2,2,64,128]{3,2,1,0:T(8,128)(2,1)S(1)} %constant_dynamic-slice_fusion.2), channel_id=1, source_target_pairs={{0,288},{32,320},{64,352},{96,384},{128,416},{160,448},{192,480},{... | collective-permute-start | bytes 196616 | tf_op jit(solution)/shard_map/ppermute | solution.py:314
  13.4 19.9 %collective-permute-start.1 = (bf16[8,2,64,128]{3,2,1,0:T(8,128)(2,1)}, bf16[8,2,64,128]{3,2,1,0:T(8,128)(2,1)S(1)}, u32[]{:S(2)}, u32[]{:S(2)}) collective-permute-start(bf16[8,2,64,128]{3,2,1,0:T(8,128)(2,1)} %feats.1), channel_id=1, source_target_pairs={{32,0},{64,32},{96,64},{128,96},{160,128},{192,160},{224,192},{33,... | collective-permute-start | bytes 786440 | tf_op jit(solution)/shard_map/ppermute | solution.py:313
  14.7 8.8 %collective-permute-start.4 = (bf16[2,2,64,128]{3,2,1,0:T(8,128)(2,1)S(1)}, bf16[2,2,64,128]{3,2,1,0:T(8,128)(2,1)S(1)}, u32[]{:S(2)}, u32[]{:S(2)}) collective-permute-start(bf16[2,2,64,128]{3,2,1,0:T(8,128)(2,1)S(1)} %constant_dynamic-slice_fusion.2), channel_id=1, source_target_pairs={{32,256},{64,288},{96,320},{128,352},{160,384},{192,416},{224,448}... | collective-permute-start | bytes 196616 | tf_op jit(solution)/shard_map/ppermute | solution.py:315
  16.0 37.9 %collective-permute-start.5 = (bf16[8,2,64,128]{3,2,1,0:T(8,128)(2,1)}, bf16[8,2,64,128]{3,2,1,0:T(8,128)(2,1)S(1)}, u32[]{:S(2)}, u32[]{:S(2)}) collective-permute-start(bf16[8,2,64,128]{3,2,1,0:T(8,128)(2,1)} %own.3), channel_id=1, source_target_pairs={{0,32},{32,64},{64,96},{96,128},{128,160},{160,192},{192,224},{1,3... | collective-permute-start | bytes 786440 | tf_op jit(solution)/shard_map/ppermute | solution.py:312
  21.3 38.7 %collective-permute-start.6 = (bf16[8,2,64,128]{3,2,1,0:T(8,128)(2,1)}, bf16[8,2,64,128]{3,2,1,0:T(8,128)(2,1)S(1)}, u32[]{:S(2)}, u32[]{:S(2)}) collective-permute-start(bf16[8,2,64,128]{3,2,1,0:T(8,128)(2,1)} %own.3), channel_id=1, source_target_pairs={{32,0},{64,32},{96,64},{128,96},{160,128},{192,160},{224,192},{33,... | collective-permute-start | bytes 786440 | tf_op jit(solution)/shard_map/ppermute | solution.py:313
  23.5 21.9 %collective-permute-start.7 = (bf16[2,2,64,128]{3,2,1,0:T(8,128)(2,1)S(1)}, bf16[2,2,64,128]{3,2,1,0:T(8,128)(2,1)S(1)}, u32[]{:S(2)}, u32[]{:S(2)}) collective-permute-start(bf16[2,2,64,128]{3,2,1,0:T(8,128)(2,1)S(1)} %constant_dynamic-slice_fusion.1), channel_id=1, source_target_pairs={{0,256},{256,0},{1,257},{257,1},{2,258},{258,2},{3,259},{259,3},{4... | collective-permute-start | bytes 196616 | tf_op jit(solution)/shard_map/ppermute | solution.py:316
  26.7 23.7 %collective-permute-start.8 = (bf16[2,2,64,128]{3,2,1,0:T(8,128)(2,1)S(1)}, bf16[2,2,64,128]{3,2,1,0:T(8,128)(2,1)S(1)}, u32[]{:S(2)}, u32[]{:S(2)}) collective-permute-start(bf16[2,2,64,128]{3,2,1,0:T(8,128)(2,1)S(1)} %constant_dynamic-slice_fusion.1), channel_id=1, source_target_pairs={{0,288},{32,320},{64,352},{96,384},{128,416},{160,448},{192,480},{... | collective-permute-start | bytes 196616 | tf_op jit(solution)/shard_map/ppermute | solution.py:314
  33.4 18.4 %collective-permute-start.9 = (bf16[2,2,64,128]{3,2,1,0:T(8,128)(2,1)S(1)}, bf16[2,2,64,128]{3,2,1,0:T(8,128)(2,1)S(1)}, u32[]{:S(2)}, u32[]{:S(2)}) collective-permute-start(bf16[2,2,64,128]{3,2,1,0:T(8,128)(2,1)S(1)} %constant_dynamic-slice_fusion.1), channel_id=1, source_target_pairs={{32,256},{64,288},{96,320},{128,352},{160,384},{192,416},{224,448}... | collective-permute-start | bytes 196616 | tf_op jit(solution)/shard_map/ppermute | solution.py:315
  35.4 1.0 copy-start
  36.3 0.9 copy-start.1
  37.3 0.7 copy-start.2
  45.4 20.3 %collective-permute-start.10 = (f32[8,2,8,128]{3,2,1,0:T(8,128)S(1)}, f32[8,2,8,128]{3,2,1,0:T(8,128)S(1)}, u32[]{:S(2)}, u32[]{:S(2)}) collective-permute-start(f32[8,2,8,128]{3,2,1,0:T(8,128)S(1)} %bitcast.10), channel_id=1, source_target_pairs={{0,32},{32,64},{64,96},{96,128},{128,160},{160,192},{192,224},{1,3... | collective-permute-start | bytes 196616 | tf_op jit(solution)/shard_map/ppermute | solution.py:312
  50.4 15.2 %collective-permute-start.11 = (f32[8,2,8,128]{3,2,1,0:T(8,128)S(1)}, f32[8,2,8,128]{3,2,1,0:T(8,128)S(1)}, u32[]{:S(2)}, u32[]{:S(2)}) collective-permute-start(f32[8,2,8,128]{3,2,1,0:T(8,128)S(1)} %bitcast.11), channel_id=1, source_target_pairs={{32,0},{64,32},{96,64},{128,96},{160,128},{192,160},{224,192},{33,... | collective-permute-start | bytes 196616 | tf_op jit(solution)/shard_map/ppermute | solution.py:313
  51.7 12.1 %collective-permute-start.12 = (f32[2,2,8,128]{3,2,1,0:T(8,128)S(1)}, f32[2,2,8,128]{3,2,1,0:T(8,128)S(1)}, u32[]{:S(2)}, u32[]{:S(2)}) collective-permute-start(f32[2,2,8,128]{3,2,1,0:T(8,128)S(1)} %constant_dynamic-slice_fusion), channel_id=1, source_target_pairs={{0,256},{256,0},{1,257},{257,1},{2,258},{258,2},{3,259},{259,3},{4... | collective-permute-start | bytes 49160 | tf_op jit(solution)/shard_map/ppermute | solution.py:316
  53.9 9.9 %collective-permute-start.13 = (f32[2,2,8,128]{3,2,1,0:T(8,128)S(1)}, f32[2,2,8,128]{3,2,1,0:T(8,128)S(1)}, u32[]{:S(2)}, u32[]{:S(2)}) collective-permute-start(f32[2,2,8,128]{3,2,1,0:T(8,128)S(1)} %constant_dynamic-slice_fusion), channel_id=1, source_target_pairs={{0,288},{32,320},{64,352},{96,384},{128,416},{160,448},{192,480},{... | collective-permute-start | bytes 49160 | tf_op jit(solution)/shard_map/ppermute | solution.py:314
  60.1 5.6 %collective-permute-start.14 = (f32[2,2,8,128]{3,2,1,0:T(8,128)S(1)}, f32[2,2,8,128]{3,2,1,0:T(8,128)S(1)}, u32[]{:S(2)}, u32[]{:S(2)}) collective-permute-start(f32[2,2,8,128]{3,2,1,0:T(8,128)S(1)} %constant_dynamic-slice_fusion), channel_id=1, source_target_pairs={{32,256},{64,288},{96,320},{128,352},{160,384},{192,416},{224,448}... | collective-permute-start | bytes 49160 | tf_op jit(solution)/shard_map/ppermute | solution.py:315
  61.4 4.3 %copy-start.3 = (bf16[64,64]{1,0:T(8,128)(2,1)S(1)}, bf16[64,64]{1,0:T(8,128)(2,1)}, u32[]{:S(2)}) copy-start(bf16[64,64]{1,0:T(8,128)(2,1)} %w_out.3) | copy-start | bytes 24580
  65.7 64.2 %copy-start.4 = (bf16[64,64]{1,0:T(8,128)(2,1)S(1)}, bf16[64,64]{1,0:T(8,128)(2,1)}, u32[]{:S(2)}) copy-start(bf16[64,64]{1,0:T(8,128)(2,1)} %param.9) | copy-start | bytes 24580
  65.7 65.0 %copy-start.5 = (bf16[64,128]{1,0:T(8,128)(2,1)S(1)}, bf16[64,128]{1,0:T(8,128)(2,1)}, u32[]{:S(2)}) copy-start(bf16[64,128]{1,0:T(8,128)(2,1)} %param.10) | copy-start | bytes 49156
  65.7 65.7 %copy-start.6 = (f32[64]{0:T(128)S(1)}, f32[64]{0:T(128)}, u32[]{:S(2)}) copy-start(f32[64]{0:T(128)} %param.8) | copy-start | bytes 772

commit v2 on v1

v2 whole, which is shorter than its diff:
```python
import functools
import math

import jax
import jax.numpy as jnp
from jax import lax
from jax.experimental import pallas as pl
from jax.experimental.pallas import tpu as pltpu
from jax.sharding import PartitionSpec as P


AXES = ("vrow", "vcol", "px", "py", "pc")
HEADS = 4
SIZE = 16
CH = 64
ROWS = 8
COLS = 2
PIX = 128
S = 13
EPSILON = 1e-06
SCALE = SIZE ** (-0.5)
F32 = jnp.float32
BF16 = jnp.bfloat16

VM = pl.BlockSpec(memory_space=pltpu.VMEM)
FAR = pl.BlockSpec(memory_space=pltpu.HBM)
SM = pl.BlockSpec(memory_space=pltpu.SMEM)


def inv_rms(values):
    return lax.rsqrt(jnp.mean(values * values, axis=0, keepdims=True) + EPSILON)


def total(terms):
    terms = list(terms)
    while len(terms) > 1:
        terms = [a + b for a, b in zip(terms[::2], terms[1::2])] + (
            [terms[-1]] if len(terms) % 2 else []
        )
    return terms[0]


def normed_pair(ref, row, gain):
    out = []
    for j in range(2):
        values = ref[row, j, 0:CH].astype(F32)
        out.append((values * inv_rms(values) * gain).astype(BF16))
    return jnp.concatenate(out, axis=1)


def put(ref, col, row, values):
    ref[col, pl.ds(row, values.shape[0], stride=S), :] = values


def take(ref, col, start):
    return ref[col, pl.ds(start, ROWS), :]


def row_pair(ref, row, first=0):
    return jnp.concatenate(
        [ref[row, 0, first : first + CH], ref[row, 1, first : first + CH]], axis=1
    )


def each_row(count, visits):
    def one(row, carry):
        for visit in visits:
            visit(row)
        return carry

    lax.fori_loop(0, count, one, 0)


def halo_start(side_ref):
    side = side_ref[0]
    return 10 - 10 * side, 10 * side, 6 - 6 * side


def clear_rows(refs, row):
    for ref in refs:
        zeros = jnp.zeros((ref.shape[1] // S, PIX), F32)
        for col in range(6):
            put(ref, col, row, zeros)
            put(ref, col, row + 1, zeros)


def project_views(ref, row, to_row, col, gain_full, w_full, qs, ks, vs, scales=None):
    raw = jnp.dot(w_full, normed_pair(ref, row, gain_full), preferred_element_type=F32)
    for j in range(2):
        part = raw[:, j * PIX : (j + 1) * PIX]
        query, key, value = part[:CH], part[CH : 2 * CH], part[2 * CH :]
        query_scale, key_scale = inv_rms(query), inv_rms(key)
        put(qs, col + j, to_row, (query * query_scale).astype(BF16).astype(F32))
        put(ks, col + j, to_row, (key * key_scale).astype(BF16).astype(F32))
        put(vs, col + j, to_row, value.astype(BF16).astype(F32))
        if scales is not None:
            scales[0][j, pl.ds(row, 1), :] = query_scale
            scales[1][j, pl.ds(row, 1), :] = key_scale


def project_out(both, to_row, col, w_o, ogs):
    og = jnp.dot(w_o, both, preferred_element_type=F32)
    for j in range(2):
        put(ogs, col + j, to_row, og[:, j * PIX : (j + 1) * PIX])


def eye():
    shape = (CH, CH)
    return lax.broadcasted_iota(jnp.int32, shape, 0) == lax.broadcasted_iota(jnp.int32, shape, 1)


def edge_kernel(side, feats, cot, edge, sems):
    _, _, edge_row = halo_start(side)
    copies = [
        pltpu.make_async_copy(
            source.at[pl.ds(edge_row, 2)], edge.at[:, :, k * CH : (k + 1) * CH], sems.at[k]
        )
        for k, source in enumerate((feats, cot))
    ]
    for copy in copies:
        copy.start()
    for copy in copies:
        copy.wait()


def own_kernel(
    side, feats_hbm, cot_hbm, gain, w_q_hbm, w_kv_hbm, w_out_hbm,
    qs, ks, vs, ogs, q_inv, k_inv, gain_out, w_in, w_back, feats, cot, w_q, w_kv, w_out, gain_row, sems,
):
    moves = (
        (gain, gain_row), (w_q_hbm, w_q), (w_kv_hbm, w_kv), (w_out_hbm, w_out),
        (feats_hbm, feats), (cot_hbm, cot),
    )
    copies = [pltpu.make_async_copy(a, b, sems.at[k]) for k, (a, b) in enumerate(moves)]
    for copy in copies:
        copy.start()
    _, clear_row, _ = halo_start(side)
    clear_rows((qs, ks, vs, ogs), clear_row)
    for copy in copies[:4]:
        copy.wait()
    gain_col = jnp.sum(
        jnp.where(eye(), jnp.broadcast_to(gain_row[...], (CH, CH)), 0.0), axis=1, keepdims=True
    )
    gain_full = jnp.broadcast_to(gain_col, (CH, PIX))
    gain_out[...] = gain_full
    w_in[0:CH, :] = w_q[...].astype(F32).T.astype(BF16)
    w_in[CH:, :] = w_kv[...].astype(F32).T.astype(BF16)
    w_back[...] = jnp.concatenate([w_q[...].astype(F32), w_kv[...].astype(F32)], axis=1).astype(BF16)
    w_full = w_in[...]
    w_o = w_out[...]
    for copy in copies[4:]:
        copy.wait()

    def visit(row):
        project_views(feats, row, row + 2, 2, gain_full, w_full, qs, ks, vs, (q_inv, k_inv))
        project_out(row_pair(cot, row), row + 2, 2, w_o, ogs)

    each_row(ROWS, (visit,))


def forward_kernel(
    side, left, right, row_halo, left_corner, right_corner, gain, w_in, ogs, qs_in, ks_in, vs_in,
    qs, ks, vs, weights, prob_grads, attended, stats, stats_edge,
):
    halo_row, _, edge_row = halo_start(side)
    gain_full = gain[...]
    w_full = w_in[...]

    def piece(ref, offset, col):
        return lambda row: project_views(ref, row, row + offset, col, gain_full, w_full, qs, ks, vs)

    each_row(ROWS, (piece(left, 2, 0), piece(right, 2, 4)))
    each_row(
        2, (piece(row_halo, halo_row, 2), piece(left_corner, halo_row, 0), piece(right_corner, halo_row, 4))
    )

    def attend(step, carry):
        col, head = step // HEADS, step % HEADS
        base = head * (SIZE * S)
        query = [take(qs, col + 2, base + d * S + 2) * SCALE for d in range(SIZE)]
        og = [take(ogs, col + 2, base + d * S + 2) for d in range(SIZE)]
        acc = [jnp.zeros((ROWS, PIX), F32)] * SIZE
        exp_total = jnp.zeros((ROWS, PIX), F32)
        spread = jnp.zeros((ROWS, PIX), F32)
        for j in range(5):
            for i in range(5):
                key = [take(ks, col + j, base + d * S + i) for d in range(SIZE)]
                weight = jnp.exp(total(a * b for a, b in zip(query, key)))
                value = [take(vs, col + j, base + d * S + i) for d in range(SIZE)]
                prob_grad = total(a * b for a, b in zip(og, value))
                acc = [a + weight * b for a, b in zip(acc, value)]
                exp_total = exp_total + weight
                spread = spread + weight * prob_grad
                weights[step, 5 * j + i] = weight
                prob_grads[step, 5 * j + i] = prob_grad
        inv_total = 1.0 / exp_total
        for d in range(SIZE):
            attended[col, pl.ds(pl.multiple_of((head * SIZE + d) * ROWS, ROWS), ROWS), :] = (
                acc[d] * inv_total
            )
        stats[pl.ds(col * 8 + head, ROWS, stride=16), :] = inv_total
        stats[pl.ds(col * 8 + 4 + head, ROWS, stride=16), :] = spread * inv_total
        return carry

    lax.fori_loop(0, COLS * HEADS, attend, 0)
    stats_edge[...] = stats[pl.ds(pl.multiple_of(edge_row * 16, 16), 32), :]


def unit_back(unit, scale, upstream):
    mean = jnp.sum(upstream * unit, axis=0, keepdims=True) * (1.0 / CH)
    return scale[None] * (upstream - unit * mean)


def own_channels(ref, col):
    return jnp.stack([take(ref, col + 2, d * S + 2) for d in range(CH)], axis=0)


def query_kernel(qs, ks, weights, prob_grads, stats, attended, cot, q_inv, raw_query, out_part, grads):
    def query_one(step, carry):
        col, head = step // HEADS, step % HEADS
        base = head * (SIZE * S)
        inv_total = stats[pl.ds(col * 8 + head, ROWS, stride=16), :]
        spread = stats[pl.ds(col * 8 + 4 + head, ROWS, stride=16), :]
        inv_total = inv_total * SCALE
        acc = [jnp.zeros((ROWS, PIX), F32)] * SIZE
        for j in range(5):
            for i in range(5):
                o = 5 * j + i
                score_grad = weights[step, o] * inv_total * (prob_grads[step, o] - spread)
                acc = [a + score_grad * take(ks, col + j, base + d * S + i) for d, a in enumerate(acc)]
        for d in range(SIZE):
            grads[col, head * SIZE + d] = acc[d]
        return carry

    lax.fori_loop(0, COLS * HEADS, query_one, 0)

    def finish(col, carry):
        raw = unit_back(own_channels(qs, col), q_inv[col], grads[col])
        raw_query[col] = raw.reshape(CH * ROWS, PIX)
        return carry

    lax.fori_loop(0, COLS, finish, 0)

    def out_grads(row, acc):
        mixed = [attended[j, pl.ds(row, CH, stride=ROWS), :].astype(BF16) for j in range(2)]
        return acc + lax.dot_general(
            jnp.concatenate(mixed, axis=1),
            row_pair(cot, row),
            (((1,), (1,)), ((), ())),
            preferred_element_type=F32,
        )

    out_part[...] = lax.fori_loop(0, ROWS, out_grads, jnp.zeros((CH, CH), F32))


def key_loop(view_cols, qs, ks, vs, ogs, sts, first, store):
    def key_one(step, carry):
        col, head = step // HEADS, step % HEADS
        base = head * (SIZE * S)
        key_acc, value_acc = first(col, head)
        for view_col in view_cols(col):
            for i in range(5):
                query = [take(qs, view_col, base + d * S + i) for d in range(SIZE)]
                key = [take(ks, col + 2, base + d * S + 2) for d in range(SIZE)]
                inv_total = take(sts, view_col, head * S + i)
                spread = take(sts, view_col, (head + HEADS) * S + i)
                score = total(a * b for a, b in zip(query, key))
                prob = jnp.exp(score * SCALE) * inv_total
                og = [take(ogs, view_col, base + d * S + i) for d in range(SIZE)]
                value = [take(vs, col + 2, base + d * S + 2) for d in range(SIZE)]
                prob_grad = total(a * b for a, b in zip(og, value))
                score_grad = prob * (prob_grad - spread)
                key_acc = [a + score_grad * b for a, b in zip(key_acc, query)]
                value_acc = [a + prob * b for a, b in zip(value_acc, og)]
        store(col, head, key_acc, value_acc)
        return carry

    lax.fori_loop(0, COLS * HEADS, key_one, 0)


def own_key_kernel(
    side, qs, ks, vs, stats, row_st, left, right, row_halo, left_corner, right_corner, w_out, ogs_in,
    ogs, key_grads, value_grads, sts,
):
    halo_row, clear_row, _ = halo_start(side)
    clear_rows((sts,), clear_row)
    w_o = w_out[...]

    def piece(ref, offset, col, first):
        return lambda row: project_out(row_pair(ref, row, first), row + offset, col, w_o, ogs)

    each_row(ROWS, (piece(left, 2, 0, 0), piece(right, 2, 4, 0)))
    each_row(
        2,
        (
            piece(row_halo, halo_row, 2, CH),
            piece(left_corner, halo_row, 0, CH),
            piece(right_corner, halo_row, 4, CH),
        ),
    )

    def own_stats(row):
        for j in range(2):
            put(sts, 2 + j, row + 2, stats[row, j])

    def halo_stats(row):
        for j in range(2):
            put(sts, 2 + j, row + halo_row, row_st[row, j])

    each_row(ROWS, (own_stats,))
    each_row(2, (halo_stats,))

    def first(col, head):
        zeros = [jnp.zeros((ROWS, PIX), F32)] * SIZE
        return zeros, zeros

    def store(col, head, key_acc, value_acc):
        for d in range(SIZE):
            key_grads[col, head * SIZE + d] = key_acc[d]
            value_grads[col, head * SIZE + d] = value_acc[d]

    key_loop(lambda col: (2, 3), qs, ks, vs, ogs, sts, first, store)


def key_kernel(
    side, qs, ks, vs, ogs, k_inv, raw_query, out_part, key_grads, value_grads,
    left_st, right_st, feats, cot, gain, w_back,
    feats_grad, weight_sums,
    sts, grads, raws,
):
    halo_row, clear_row, _ = halo_start(side)
    clear_rows((sts,), clear_row)

    def halo_stats(ref, offset, first, col):
        def one(row):
            for j in range(2):
                put(sts, col + j, row + offset, ref[row + first, j])

        return one

    each_row(ROWS, (halo_stats(left_st, 2, 0, 0), halo_stats(right_st, 2, 0, 4)))
    each_row(2, (halo_stats(left_st, halo_row, ROWS, 0), halo_stats(right_st, halo_row, ROWS, 4)))

    def first(col, head):
        return (
            [key_grads[col, head * SIZE + d] for d in range(SIZE)],
            [value_grads[col, head * SIZE + d] for d in range(SIZE)],
        )

    def store(col, head, key_acc, value_acc):
        for d in range(SIZE):
            grads[col, head * SIZE + d] = key_acc[d] * SCALE
            raws[col, pl.ds(pl.multiple_of((2 * CH + head * SIZE + d) * ROWS, ROWS), ROWS), :] = (
                value_acc[d]
            )

    key_loop(lambda col: (5 * col, 1, 4), qs, ks, vs, ogs, sts, first, store)

    def finish(col, carry):
        raw = unit_back(own_channels(ks, col), k_inv[col], grads[col])
        raws[col, CH * ROWS : 2 * CH * ROWS, :] = raw.reshape(CH * ROWS, PIX)
        raws[col, 0 : CH * ROWS, :] = raw_query[col]
        return carry

    lax.fori_loop(0, COLS, finish, 0)

    gain_full = gain[...]
    w_b = w_back[...]

    def view_row(row, acc):
        raw = jnp.concatenate(
            [raws[j, pl.ds(row, 3 * CH, stride=ROWS), :].astype(BF16) for j in range(2)], axis=1
        )
        normed_grad = jnp.dot(w_b, raw, preferred_element_type=F32)
        normed = []
        for j in range(2):
            values = feats[row, j].astype(F32)
            inv_norm = inv_rms(values)
            scaled = values * inv_norm
            normed.append((scaled * gain_full).astype(BF16))
            scaled_grad = normed_grad[:, j * PIX : (j + 1) * PIX] * gain_full
            mean = jnp.mean(scaled_grad * scaled, axis=0, keepdims=True)
            branch = inv_norm * (scaled_grad - scaled * mean)
            feats_grad[row, j] = (cot[row, j].astype(F32) + branch).astype(BF16)
        return acc + lax.dot_general(
            jnp.concatenate(normed, axis=1),
            raw,
            (((1,), (1,)), ((), ())),
            preferred_element_type=F32,
        )

    sums = lax.fori_loop(0, ROWS, view_row, jnp.zeros((CH, 3 * CH), F32))
    weight_sums[0:CH, :] = sums[:, CH:]
    weight_sums[CH : 2 * CH, :] = jnp.concatenate([sums[:, :CH], out_part[...]], axis=1)


def last_kernel(factor, sums, w_q, w_kv, gain, query_grad, keyval_grad, output_grad, gain_grad):
    keyval = sums[0:CH, :] * factor
    rest = sums[CH : 2 * CH, :] * factor
    query = rest[:, :CH]
    keyval_grad[...] = keyval
    query_grad[...] = query
    output_grad[...] = rest[:, CH:]
    col = jnp.sum(query * w_q[...].astype(F32), axis=1, keepdims=True) + jnp.sum(
        keyval * w_kv[...].astype(F32), axis=1, keepdims=True
    )
    line = jnp.sum(jnp.where(eye(), jnp.broadcast_to(col, (CH, CH)), 0.0), axis=0, keepdims=True)
    gain_grad[...] = line / gain[...]


def call(kernel, outs, scratch, flops, *operands, aliases=(), far=()):
    return pl.pallas_call(
        kernel,
        out_shape=[jax.ShapeDtypeStruct(shape, dtype) for shape, dtype in outs],
        in_specs=[
            SM if x.dtype == jnp.int32 else FAR if k in far else VM for k, x in enumerate(operands)
        ],
        out_specs=[VM] * len(outs),
        scratch_shapes=[pltpu.VMEM(x, F32) if isinstance(x, tuple) else x for x in scratch],
        input_output_aliases=dict(aliases),
        compiler_params=pltpu.CompilerParams(vmem_limit_bytes=32 * 1024 * 1024),
        cost_estimate=pl.CostEstimate(flops=flops, bytes_accessed=1000000, transcendentals=0),
    )(*operands)


def sum_everywhere(values):
    near, far = ("px", "pc", "vrow"), ("py", "vcol")
    near_count, far_count = (math.prod(lax.axis_size(a) for a in axes) for axes in (near, far))
    shares = lax.all_to_all(values.reshape(near_count, -1, PIX), near, 0, 0)
    share = jnp.sum(shares, axis=0).astype(BF16)
    copies = jnp.broadcast_to(share[None], (far_count,) + share.shape)
    share = jnp.sum(lax.all_to_all(copies, far, 0, 0).astype(F32), axis=0)
    copies = jnp.broadcast_to(share[None], (near_count,) + share.shape)
    return lax.all_to_all(copies, near, 0, 0).reshape(values.shape)


def layer(features, out_cotangent, norm_gain, query_proj, keyval_proj, output_proj):
    vrow = lax.axis_index("vrow").astype(jnp.int32)
    side = vrow.reshape(1)
    cols = lax.axis_size("vcol")
    up = [(i, i + 1) for i in range(cols - 1)]
    down = [(j, i) for i, j in up]
    cross = [(0, 1), (1, 0)]
    diag_up = [(a * cols + i, b * cols + j) for a, b in cross for i, j in up]
    diag_down = [(a * cols + i, b * cols + j) for a, b in cross for i, j in down]
    grid = ("vrow", "vcol")

    held = [pltpu.with_memory_space_constraint(x, pltpu.HBM) for x in (features, out_cotangent)]
    left = lax.ppermute(features, "vcol", up)
    right = lax.ppermute(features, "vcol", down)
    (edge,) = call(
        edge_kernel,
        [((2, COLS, 2 * CH, PIX), BF16)],
        [pltpu.SemaphoreType.DMA((2,))], 1000,
        side, *held, far=(1, 2),
    )
    row_halo = lax.ppermute(edge, "vrow", cross)
    left_corner = lax.ppermute(edge, grid, diag_up)
    right_corner = lax.ppermute(edge, grid, diag_down)

    padded = ((6, CH * S, PIX), F32)
    lanes = ((COLS, ROWS, PIX), F32)
    offsets = ((COLS * HEADS, 25, ROWS, PIX), F32)
    channels = ((COLS, CH * ROWS, PIX), F32)
    tiles = ((COLS, CH, ROWS, PIX), F32)
    gain = norm_gain.reshape(1, CH)
    views = (features.shape, BF16)
    (
        qs, ks, vs, ogs, q_inv, k_inv, gain_full, w_in, w_back, feats, cot, w_q, w_kv, w_out, gain_row,
    ) = call(
        own_kernel,
        [
            padded, padded, padded, padded, lanes, lanes, ((CH, PIX), F32), ((3 * CH, CH), BF16),
            ((CH, 3 * CH), BF16), views, views, ((CH, CH), BF16), ((CH, 2 * CH), BF16),
            ((CH, CH), BF16), ((1, CH), F32),
        ],
        [pltpu.SemaphoreType.DMA((6,))], 2000000,
        side, *held, *(pltpu.with_memory_space_constraint(x, pltpu.HBM) for x in (gain, query_proj, keyval_proj, output_proj)),
        far=(1, 2, 3, 4, 5, 6),
    )
    left_cot = lax.ppermute(out_cotangent, "vcol", up)
    right_cot = lax.ppermute(out_cotangent, "vcol", down)
    qs, ks, vs, weights, prob_grads, attended, stats, stats_edge = call(
        forward_kernel,
        [padded, padded, padded, offsets, offsets, channels, ((ROWS * 16, PIX), F32), ((32, PIX), F32)],
        [], 4000000,
        side, left, right, row_halo, left_corner, right_corner, gain_full, w_in, ogs, qs, ks, vs,
        aliases=((9, 0), (10, 1), (11, 2)),
    )
    stats_view = stats.reshape(ROWS, COLS, 8, PIX)
    row_st = lax.ppermute(stats_edge.reshape(2, COLS, 8, PIX), "vrow", cross)
    raw_query, out_part = call(
        query_kernel,
        [channels, ((CH, CH), F32)],
        [(COLS, CH, ROWS, PIX)], 2000000,
        qs, ks, weights, prob_grads, stats, attended, cot, q_inv,
    )
    all_st = jnp.concatenate([stats_view, row_st], axis=0)
    left_st = lax.ppermute(all_st, "vcol", up)
    right_st = lax.ppermute(all_st, "vcol", down)
    ogs, key_grads, value_grads = call(
        own_key_kernel,
        [padded, tiles, tiles],
        [(6, 8 * S, PIX)], 3000000,
        side, qs, ks, vs, stats_view, row_st,
        left_cot, right_cot, row_halo, left_corner, right_corner, w_out, ogs,
        aliases=((12, 0),),
    )
    features_grad, weight_sums = call(
        key_kernel,
        [(features.shape, BF16), ((2 * CH, PIX), F32)],
        [(6, 8 * S, PIX), (COLS, CH, ROWS, PIX), (COLS, 3 * CH * ROWS, PIX)], 4000000,
        side, qs, ks, vs, ogs, k_inv, raw_query, out_part, key_grads, value_grads,
        left_st, right_st, feats, cot, gain_full, w_back,
    )
    tokens_all = ROWS * COLS * PIX * math.prod(lax.axis_size(a) for a in AXES)
    query_grad, keyval_grad, output_grad, gain_grad = call(
        functools.partial(last_kernel, 1.0 / math.sqrt(tokens_all)),
        [((CH, CH), F32), ((CH, 2 * CH), F32), ((CH, CH), F32), ((1, CH), F32)],
        [], 100000,
        sum_everywhere(weight_sums), w_q, w_kv, gain_row,
    )
    return features_grad, query_grad, keyval_grad, output_grad, gain_grad.reshape(CH)


def solution(mesh):
    rows, cols, _ = mesh.devices.shape
    parts = jax.sharding.Mesh(mesh.devices.reshape(rows, cols, 4, 4, 2), AXES)
    placed = P("vrow", "vcol", None, AXES[2:])
    return jax.shard_map(
        layer,
        mesh=parts,
        in_specs=(placed, placed, P(), P(), P(), P()),
        out_specs=(placed, P(), P(), P(), P()),
        check_vma=False,
    )
```

time: 133 us -> 110 us (0.83)
  starting transfers between devices: 47.1 us -> 31 us
  local copies, waits for them, and re-layouts: 5.24 us -> 0.02 us
  other arithmetic: 2.92 us -> 0.06 us
  Pallas kernels: 19.4 us -> 21.6 us
    ppermute x15 -> x10, starting transfers between devices: 47.1 us -> 31 us  [the longest x1 5.44 us: layer(): left_st = lax.ppermute(all_st, 'vcol', up)]
    unnamed x14 -> x0, local copies, waits for them, and re-layouts: 2.65 us -> none
    pallas_call x3 -> x7, Pallas kernels: 19.4 us -> 21.6 us  [call(): pl.pallas_call(kernel, out_shape=[jax.ShapeDtypeStruct(shape, dtype) for...]
    dynamic_slice x3 -> x0, local copies, waits for them, and re-layouts: 1.74 us -> none  [edge(): return lax.dynamic_slice_in_dim(values, edge_start, 2, 0)]
    reduce_sum x4 -> x2, other arithmetic: 1.57 us -> 0.06 us  [the longest x1 0.04 us: sum_everywhere(): share = jnp.sum(lax.all_to_all(copies, far, 0, 0).astype(F32), axis=0)]
  transfers between devices with their start and end apart: 15 -> 10, of which waited for: 1 -> 1; matrix products, arithmetic and copies ran while one was open for 3% -> 0% of each run, Pallas kernels for 7% -> 14%
where the time goes in v2:
time: 110 us; the launch traced here: 109 us
  blocking collectives  53.9 us (49%)
  starting transfers between devices  31 us (28%)
  Pallas kernels  21.6 us (20%)
  waiting for transfers between devices  1.67 us (2%)
    all_to_all x1, blocking collectives, sum_everywhere(): share = jnp.sum(lax.all_to_all(copies, far, 0, 0).astype(F32), axis=0)  28.9 us
    pallas_call x7, Pallas kernels, call(): pl.pallas_call(kernel, out_shape=[jax.ShapeDtypeStruct(shape, dtype) for...  21.6 us
    all_to_all x1, blocking collectives, sum_everywhere(): shares = lax.all_to_all(values.reshape(near_count, -1, PIX), near, 0, 0)  14.8 us
    all_to_all x1, blocking collectives, sum_everywhere(): return lax.all_to_all(copies, near, 0, 0).reshape(values.shape)  10.2 us
    ppermute x1, starting transfers between devices, layer(): left_st = lax.ppermute(all_st, 'vcol', up)  5.44 us
    ppermute x1, starting transfers between devices, layer(): left_cot = lax.ppermute(out_cotangent, 'vcol', up)  5.02 us
    ppermute x1, starting transfers between devices, layer(): left = lax.ppermute(features, 'vcol', up)  4.83 us
    ppermute x1, starting transfers between devices, layer(): left_corner = lax.ppermute(edge, grid, diag_up)  4.51 us
  transfers between devices with their start and end apart: 10, of which 1 were waited for; matrix products, arithmetic and copies ran while one was open for 0% of the time, Pallas kernels for 14%

profile of v2, /device:TPU:1, one launch (start us, length us, event | category | flops | bytes accessed | tf_op | source)
XLA Modules:
  0.0 109.1 jit_solution(9287936946464786509)
XLA Ops:
  0.6 4.8 %collective-permute-start = (bf16[8,2,64,128]{3,2,1,0:T(8,128)(2,1)}, bf16[8,2,64,128]{3,2,1,0:T(8,128)(2,1)S(1)}, u32[]{:S(2)}, u32[]{:S(2)}) collective-permute-start(bf16[8,2,64,128]{3,2,1,0:T(8,128)(2,1)} %feats_hbm.1), channel_id=1, source_target_pairs={{0,32},{32,64},{64,96},{96,128},{128,160},{160,192},{192,224},{1,3... | collective-permute-start | bytes 786440 | tf_op jit(solution)/shard_map/ppermute | solution.py:449
  5.5 1.3 %collective-permute-start.1 = (bf16[8,2,64,128]{3,2,1,0:T(8,128)(2,1)}, bf16[8,2,64,128]{3,2,1,0:T(8,128)(2,1)S(1)}, u32[]{:S(2)}, u32[]{:S(2)}) collective-permute-start(bf16[8,2,64,128]{3,2,1,0:T(8,128)(2,1)} %feats_hbm.1), channel_id=1, source_target_pairs={{32,0},{64,32},{96,64},{128,96},{160,128},{192,160},{224,192},{33,... | collective-permute-start | bytes 786440 | tf_op jit(solution)/shard_map/ppermute | solution.py:450
  6.8 0.9 shard_map.101
  7.7 3.2 %collective-permute-start.2 = (bf16[2,2,128,128]{3,2,1,0:T(8,128)(2,1)S(1)}, bf16[2,2,128,128]{3,2,1,0:T(8,128)(2,1)S(1)}, u32[]{:S(2)}, u32[]{:S(2)}) collective-permute-start(bf16[2,2,128,128]{3,2,1,0:T(8,128)(2,1)S(1)} %shard_map.101), channel_id=1, source_target_pairs={{0,256},{256,0},{1,257},{257,1},{2,258},{258,2},{3,259},{259,3},{4... | collective-permute-start | bytes 393224 | tf_op jit(solution)/shard_map/ppermute | solution.py:457
  10.9 4.5 %collective-permute-start.3 = (bf16[2,2,128,128]{3,2,1,0:T(8,128)(2,1)S(1)}, bf16[2,2,128,128]{3,2,1,0:T(8,128)(2,1)S(1)}, u32[]{:S(2)}, u32[]{:S(2)}) collective-permute-start(bf16[2,2,128,128]{3,2,1,0:T(8,128)(2,1)S(1)} %shard_map.101), channel_id=1, source_target_pairs={{0,288},{32,320},{64,352},{96,384},{128,416},{160,448},{192,480},{... | collective-permute-start | bytes 393224 | tf_op jit(solution)/shard_map/ppermute | solution.py:458
  15.4 1.3 %collective-permute-start.4 = (bf16[2,2,128,128]{3,2,1,0:T(8,128)(2,1)S(1)}, bf16[2,2,128,128]{3,2,1,0:T(8,128)(2,1)S(1)}, u32[]{:S(2)}, u32[]{:S(2)}) collective-permute-start(bf16[2,2,128,128]{3,2,1,0:T(8,128)(2,1)S(1)} %shard_map.101), channel_id=1, source_target_pairs={{32,256},{64,288},{96,320},{128,352},{160,384},{192,416},{224,448}... | collective-permute-start | bytes 393224 | tf_op jit(solution)/shard_map/ppermute | solution.py:459
  16.7 0.0 collective-permute-done.2.row_halo
  16.7 5.0 %collective-permute-start.6 = (bf16[8,2,64,128]{3,2,1,0:T(8,128)(2,1)}, bf16[8,2,64,128]{3,2,1,0:T(8,128)(2,1)S(1)}, u32[]{:S(2)}, u32[]{:S(2)}) collective-permute-start(bf16[8,2,64,128]{3,2,1,0:T(8,128)(2,1)} %cot_hbm.1), channel_id=1, source_target_pairs={{0,32},{32,64},{64,96},{96,128},{128,160},{160,192},{192,224},{1,3... | collective-permute-start | bytes 786440 | tf_op jit(solution)/shard_map/ppermute | solution.py:481
  21.7 0.0 collective-permute-done.3.left_corner
  21.7 1.3 %collective-permute-start.7 = (bf16[8,2,64,128]{3,2,1,0:T(8,128)(2,1)}, bf16[8,2,64,128]{3,2,1,0:T(8,128)(2,1)S(1)}, u32[]{:S(2)}, u32[]{:S(2)}) collective-permute-start(bf16[8,2,64,128]{3,2,1,0:T(8,128)(2,1)} %cot_hbm.1), channel_id=1, source_target_pairs={{32,0},{64,32},{96,64},{128,96},{160,128},{192,160},{224,192},{33,... | collective-permute-start | bytes 786440 | tf_op jit(solution)/shard_map/ppermute | solution.py:482
  23.0 2.9 %shard_map.102 = (f32[6,832,128]{2,1,0:T(8,128)S(1)}, f32[6,832,128]{2,1,0:T(8,128)S(1)}, f32[6,832,128]{2,1,0:T(8,128)S(1)}, f32[6,832,128]{2,1,0:T(8,128)S(1)}...) custom-call(s32[1]{0:T(128)} %bitcast.side, ...), custom_call_target="tpu_custom_call" | custom-call | flops 2000000 | bytes 1000000 | tf_op jit(solution)/shard_map/pallas_call | solution.py:412
  26.0 0.0 collective-permute-done.4.right_corner
  26.0 0.0 collective-permute-done.left
  26.0 0.0 collective-permute-done.1.right
  26.0 6.0 %shard_map.103 = (f32[6,832,128]{2,1,0:T(8,128)S(1)}, f32[6,832,128]{2,1,0:T(8,128)S(1)}, f32[6,832,128]{2,1,0:T(8,128)S(1)}, f32[8,25,8,128]{3,2,1,0:T(8,128)S(...) custom-call(s32[1]{0:T(128)} %bitcast.side, ...), custom_call_target="tpu_custom_call", output_to_operand_aliasing={{0}: (9, {}), {1}: (10, {}), {2}: (11, {})} | custom-call | flops 4000000 | bytes 1000000 | tf_op jit(solution)/shard_map/pallas_call | solution.py:412
  32.0 2.8 %collective-permute-start.5 = (f32[2,2,8,128]{3,2,1,0:T(8,128)S(1)}, f32[2,2,8,128]{3,2,1,0:T(8,128)S(1)}, u32[]{:S(2)}, u32[]{:S(2)}) collective-permute-start(f32[2,2,8,128]{3,2,1,0:T(8,128)S(1)} %bitcast.11), channel_id=1, source_target_pairs={{0,256},{256,0},{1,257},{257,1},{2,258},{258,2},{3,259},{259,3},{4... | collective-permute-start | bytes 49160 | tf_op jit(solution)/shard_map/ppermute | solution.py:491
  34.8 1.6 %collective-permute-done.5.row_st = f32[2,2,8,128]{3,2,1,0:T(8,128)S(1)} collective-permute-done((f32[2,2,8,128]{3,2,1,0:T(8,128)S(1)}, f32[2,2,8,128]{3,2,1,0:T(8,128)S(1)}, u32[]{:S(2)}, u32[]{:S(2)}) %collective-permute-start.5) | collective-permute-done | bytes 16416 | tf_op jit(solution)/shard_map/ppermute | solution.py:491
  36.4 5.4 %collective-permute-start.8 = (f32[10,2,8,128]{3,2,1,0:T(8,128)S(1)}, f32[10,2,8,128]{3,2,1,0:T(8,128)S(1)}, u32[]{:S(2)}, u32[]{:S(2)}) collective-permute-start(f32[10,2,8,128]{3,2,1,0:T(8,128)S(1)} %pad_maximum_fusion), channel_id=1, source_target_pairs={{0,32},{32,64},{64,96},{96,128},{128,160},{160,192},{192,224},{1,3... | collective-permute-start | bytes 245768 | tf_op jit(solution)/shard_map/ppermute | solution.py:499
  41.9 1.3 %collective-permute-start.9 = (f32[10,2,8,128]{3,2,1,0:T(8,128)S(1)}, f32[10,2,8,128]{3,2,1,0:T(8,128)S(1)}, u32[]{:S(2)}, u32[]{:S(2)}) collective-permute-start(f32[10,2,8,128]{3,2,1,0:T(8,128)S(1)} %pad_maximum_fusion), channel_id=1, source_target_pairs={{32,0},{64,32},{96,64},{128,96},{160,128},{192,160},{224,192},{33,... | collective-permute-start | bytes 245768 | tf_op jit(solution)/shard_map/ppermute | solution.py:500
  43.2 2.4 %shard_map.105 = (f32[2,512,128]{2,1,0:T(8,128)S(1)}, f32[64,64]{1,0:T(8,128)S(1)}) custom-call(f32[6,832,128]{2,1,0:T(8,128)S(1)} %get-tuple-element.45.qs, f32[6,832,128]{2,1,0:T(8,128)S(1)} %get-tuple-element.46.ks, f32[8,25,8,128]{3,2,1,0:T(8,128)S(1)} %get-tuple-element.53.weights, f32[8,25,8,128]{3,2,1,0:T(8,128)S(1)} %get-tuple-element.54.prob_grads, ...), custom_call_target="tpu_custom_call" | custom-call | flops 2000000 | bytes 1000000 | tf_op jit(solution)/shard_map/pallas_call | solution.py:412
  45.6 0.0 collective-permute-done.6.left
  45.6 0.0 collective-permute-done.7.right
  45.7 3.3 %shard_map.104 = (f32[6,832,128]{2,1,0:T(8,128)S(1)}, f32[2,64,8,128]{3,2,1,0:T(8,128)S(1)}, f32[2,64,8,128]{3,2,1,0:T(8,128)S(1)}) custom-call(s32[1]{0:T(128)} %bitcast.side, f32[6,832,128]{2,1,0:T(8,128)S(1)} %get-tuple-element.45.qs, f32[6,832,128]{2,1,0:T(8,128)S(1)} %get-tuple-element.46.ks, ...), custom_call_target="tpu_custom_call", output_to_operand_aliasing={{0}: (12, {})} | custom-call | flops 3000000 | bytes 1000000 | tf_op jit(solution)/shard_map/pallas_call | solution.py:412
  48.9 0.0 collective-permute-done.8.left_st
  48.9 0.0 collective-permute-done.9.right_st
  48.9 5.4 %shard_map.106 = (bf16[8,2,64,128]{3,2,1,0:T(8,128)(2,1)}, f32[128,128]{1,0:T(8,128)S(1)}) custom-call(s32[1]{0:T(128)} %bitcast.side, f32[6,832,128]{2,1,0:T(8,128)S(1)} %get-tuple-element.45.qs, f32[6,832,128]{2,1,0:T(8,128)S(1)} %get-tuple-element.46.ks, f32[6,832,128]{2,1,0:T(8,128)S(1)} %get-tuple-element.47.vs, ...), custom_call_target="tpu_custom_call" | custom-call | flops 4000000 | bytes 1000000 | tf_op jit(solution)/shard_map/pallas_call | solution.py:412
  54.3 14.8 %all_to_all.15 = f32[16,8,128]{2,1,0:T(8,128)S(1)} all-to-all(f32[16,8,128]{2,1,0:T(8,128)S(1)} %bitcast.10), channel_id=1, replica_groups=mesh['vrow'=2,'vcol'=8,'px'=4,'py'=4,'pc'=2] {'px','pc','vrow'}, dimensions={0} | all-to-all | bytes 131072 | tf_op jit(solution)/shard_map/all_to_all | solution.py:429
  69.1 28.9 %all_to_all.16 = bf16[32,8,128]{2,1,0:T(8,128)(2,1)S(1)} all-to-all(bf16[32,8,128]{2,1,0:T(8,128)(2,1)S(1)} %broadcast_in_dim.4), channel_id=1, replica_groups=mesh['vrow'=2,'vcol'=8,'px'=4,'py'=4,'pc'=2] {'py','vcol'}, dimensions={0} | all-to-all | bytes 131072 | tf_op jit(solution)/shard_map/all_to_all | solution.py:432
  98.1 10.2 %all_to_all.17 = f32[16,8,128]{2,1,0:T(8,128)S(1)} all-to-all(f32[16,8,128]{2,1,0:T(8,128)S(1)} %broadcast_in_dim.5), channel_id=1, replica_groups=mesh['vrow'=2,'vcol'=8,'px'=4,'py'=4,'pc'=2] {'px','pc','vrow'}, dimensions={0} | all-to-all | bytes 131072 | tf_op jit(solution)/shard_map/all_to_all | solution.py:434
  108.3 0.7 shard_map.107
  (5 shorter events, 0.1 us)
Async XLA Ops:
  0.6 25.4 %collective-permute-start = (bf16[8,2,64,128]{3,2,1,0:T(8,128)(2,1)}, bf16[8,2,64,128]{3,2,1,0:T(8,128)(2,1)S(1)}, u32[]{:S(2)}, u32[]{:S(2)}) collective-permute-start(bf16[8,2,64,128]{3,2,1,0:T(8,128)(2,1)} %feats_hbm.1), channel_id=1, source_target_pairs={{0,32},{32,64},{64,96},{96,128},{128,160},{160,192},{192,224},{1,3... | collective-permute-start | bytes 786440 | tf_op jit(solution)/shard_map/ppermute | solution.py:449
  5.5 20.5 %collective-permute-start.1 = (bf16[8,2,64,128]{3,2,1,0:T(8,128)(2,1)}, bf16[8,2,64,128]{3,2,1,0:T(8,128)(2,1)S(1)}, u32[]{:S(2)}, u32[]{:S(2)}) collective-permute-start(bf16[8,2,64,128]{3,2,1,0:T(8,128)(2,1)} %feats_hbm.1), channel_id=1, source_target_pairs={{32,0},{64,32},{96,64},{128,96},{160,128},{192,160},{224,192},{33,... | collective-permute-start | bytes 786440 | tf_op jit(solution)/shard_map/ppermute | solution.py:450
  7.7 9.0 %collective-permute-start.2 = (bf16[2,2,128,128]{3,2,1,0:T(8,128)(2,1)S(1)}, bf16[2,2,128,128]{3,2,1,0:T(8,128)(2,1)S(1)}, u32[]{:S(2)}, u32[]{:S(2)}) collective-permute-start(bf16[2,2,128,128]{3,2,1,0:T(8,128)(2,1)S(1)} %shard_map.101), channel_id=1, source_target_pairs={{0,256},{256,0},{1,257},{257,1},{2,258},{258,2},{3,259},{259,3},{4... | collective-permute-start | bytes 393224 | tf_op jit(solution)/shard_map/ppermute | solution.py:457
  10.9 10.9 %collective-permute-start.3 = (bf16[2,2,128,128]{3,2,1,0:T(8,128)(2,1)S(1)}, bf16[2,2,128,128]{3,2,1,0:T(8,128)(2,1)S(1)}, u32[]{:S(2)}, u32[]{:S(2)}) collective-permute-start(bf16[2,2,128,128]{3,2,1,0:T(8,128)(2,1)S(1)} %shard_map.101), channel_id=1, source_target_pairs={{0,288},{32,320},{64,352},{96,384},{128,416},{160,448},{192,480},{... | collective-permute-start | bytes 393224 | tf_op jit(solution)/shard_map/ppermute | solution.py:458
  15.4 10.6 %collective-permute-start.4 = (bf16[2,2,128,128]{3,2,1,0:T(8,128)(2,1)S(1)}, bf16[2,2,128,128]{3,2,1,0:T(8,128)(2,1)S(1)}, u32[]{:S(2)}, u32[]{:S(2)}) collective-permute-start(bf16[2,2,128,128]{3,2,1,0:T(8,128)(2,1)S(1)} %shard_map.101), channel_id=1, source_target_pairs={{32,256},{64,288},{96,320},{128,352},{160,384},{192,416},{224,448}... | collective-permute-start | bytes 393224 | tf_op jit(solution)/shard_map/ppermute | solution.py:459
  16.7 28.9 %collective-permute-start.6 = (bf16[8,2,64,128]{3,2,1,0:T(8,128)(2,1)}, bf16[8,2,64,128]{3,2,1,0:T(8,128)(2,1)S(1)}, u32[]{:S(2)}, u32[]{:S(2)}) collective-permute-start(bf16[8,2,64,128]{3,2,1,0:T(8,128)(2,1)} %cot_hbm.1), channel_id=1, source_target_pairs={{0,32},{32,64},{64,96},{96,128},{128,160},{160,192},{192,224},{1,3... | collective-permute-start | bytes 786440 | tf_op jit(solution)/shard_map/ppermute | solution.py:481
  21.7 23.9 %collective-permute-start.7 = (bf16[8,2,64,128]{3,2,1,0:T(8,128)(2,1)}, bf16[8,2,64,128]{3,2,1,0:T(8,128)(2,1)S(1)}, u32[]{:S(2)}, u32[]{:S(2)}) collective-permute-start(bf16[8,2,64,128]{3,2,1,0:T(8,128)(2,1)} %cot_hbm.1), channel_id=1, source_target_pairs={{32,0},{64,32},{96,64},{128,96},{160,128},{192,160},{224,192},{33,... | collective-permute-start | bytes 786440 | tf_op jit(solution)/shard_map/ppermute | solution.py:482
  32.0 4.5 %collective-permute-start.5 = (f32[2,2,8,128]{3,2,1,0:T(8,128)S(1)}, f32[2,2,8,128]{3,2,1,0:T(8,128)S(1)}, u32[]{:S(2)}, u32[]{:S(2)}) collective-permute-start(f32[2,2,8,128]{3,2,1,0:T(8,128)S(1)} %bitcast.11), channel_id=1, source_target_pairs={{0,256},{256,0},{1,257},{257,1},{2,258},{258,2},{3,259},{259,3},{4... | collective-permute-start | bytes 49160 | tf_op jit(solution)/shard_map/ppermute | solution.py:491
  36.4 12.5 %collective-permute-start.8 = (f32[10,2,8,128]{3,2,1,0:T(8,128)S(1)}, f32[10,2,8,128]{3,2,1,0:T(8,128)S(1)}, u32[]{:S(2)}, u32[]{:S(2)}) collective-permute-start(f32[10,2,8,128]{3,2,1,0:T(8,128)S(1)} %pad_maximum_fusion), channel_id=1, source_target_pairs={{0,32},{32,64},{64,96},{96,128},{128,160},{160,192},{192,224},{1,3... | collective-permute-start | bytes 245768 | tf_op jit(solution)/shard_map/ppermute | solution.py:499
  41.9 7.0 %collective-permute-start.9 = (f32[10,2,8,128]{3,2,1,0:T(8,128)S(1)}, f32[10,2,8,128]{3,2,1,0:T(8,128)S(1)}, u32[]{:S(2)}, u32[]{:S(2)}) collective-permute-start(f32[10,2,8,128]{3,2,1,0:T(8,128)S(1)} %pad_maximum_fusion), channel_id=1, source_target_pairs={{32,0},{64,32},{96,64},{128,96},{160,128},{192,160},{224,192},{33,... | collective-permute-start | bytes 245768 | tf_op jit(solution)/shard_map/ppermute | solution.py:500

commit v3 on v2

v3 whole, which is shorter than its diff:
```python
import functools
import math

import jax
import jax.numpy as jnp
from jax import lax
from jax.experimental import pallas as pl
from jax.experimental.pallas import tpu as pltpu
from jax.sharding import PartitionSpec as P


AXES = ("vrow", "vcol", "px", "py", "pc")
HEADS = 4
SIZE = 16
CH = 64
ROWS = 8
COLS = 2
PIX = 128
S = 13
W = 13
EPSILON = 1e-06
SCALE = SIZE ** (-0.5)
F32 = jnp.float32
BF16 = jnp.bfloat16

VM = pl.BlockSpec(memory_space=pltpu.VMEM)
FAR = pl.BlockSpec(memory_space=pltpu.HBM)
SM = pl.BlockSpec(memory_space=pltpu.SMEM)


def inv_rms(values):
    return lax.rsqrt(jnp.mean(values * values, axis=0, keepdims=True) + EPSILON)


def total(terms):
    terms = list(terms)
    while len(terms) > 1:
        terms = [a + b for a, b in zip(terms[::2], terms[1::2])] + (
            [terms[-1]] if len(terms) % 2 else []
        )
    return terms[0]


def put(ref, col, row, values):
    ref[col, pl.ds(row, values.shape[0], stride=S), :] = values


def take(ref, col, start):
    return ref[col, pl.ds(start, ROWS), :]


def pair(ref, row, first=0):
    return jnp.concatenate([ref[row, first], ref[row, first + 1]], axis=1)


def each_row(count, visits):
    def one(row, carry):
        for visit in visits:
            visit(row)
        return carry

    lax.fori_loop(0, count, one, 0)


def halo_start(side_ref):
    side = side_ref[0]
    return 10 - 10 * side, 10 * side, 6 - 6 * side


def clear_rows(refs, row):
    for ref in refs:
        zeros = jnp.zeros((ref.shape[1] // S, PIX), F32)
        for col in range(ref.shape[0]):
            put(ref, col, row, zeros)
            put(ref, col, row + 1, zeros)


def eye():
    shape = (CH, CH)
    return lax.broadcasted_iota(jnp.int32, shape, 0) == lax.broadcasted_iota(jnp.int32, shape, 1)


def normed_views(ref, row, gain):
    out = []
    for j in range(2):
        values = ref[row, j].astype(F32)
        out.append((values * inv_rms(values) * gain).astype(BF16))
    return out


def project_keys(raw, to_row, col, j, ks, vs, k_inv):
    key, value = raw[:CH], raw[CH:]
    key_scale = inv_rms(key)
    put(ks, col + j, to_row, (key * key_scale).astype(BF16).astype(F32))
    put(vs, col + j, to_row, value.astype(BF16).astype(F32))
    k_inv[col + j, pl.ds(to_row, 1), :] = key_scale


def edge_kernel(side, feats, edge, sem):
    _, _, edge_row = halo_start(side)
    copy = pltpu.make_async_copy(feats.at[pl.ds(edge_row, 2)], edge, sem)
    copy.start()
    copy.wait()


def own_kernel(
    side, feats_hbm, cot_hbm, gain_hbm, w_q_hbm, w_kv_hbm, w_out_hbm,
    qs, ks, vs, ogs, q_inv, k_inv, normed, gain_out, w_in, w_back, feats, cot, w_q, w_kv, gain_row,
    w_out, sems,
):
    moves = (
        (gain_hbm, gain_row), (w_q_hbm, w_q), (w_kv_hbm, w_kv), (w_out_hbm, w_out),
        (feats_hbm, feats), (cot_hbm, cot),
    )
    copies = [pltpu.make_async_copy(a, b, sems.at[k]) for k, (a, b) in enumerate(moves)]
    for copy in copies:
        copy.start()
    _, clear_row, _ = halo_start(side)
    clear_rows((ks, vs), clear_row)
    clear_rows((qs, ogs), 0)
    clear_rows((qs, ogs), 10)
    for copy in copies[:4]:
        copy.wait()
    gain_col = jnp.sum(
        jnp.where(eye(), jnp.broadcast_to(gain_row[...], (CH, CH)), 0.0), axis=1, keepdims=True
    )
    gain_full = jnp.broadcast_to(gain_col, (CH, PIX))
    gain_out[...] = gain_full
    w_in[0:CH, :] = w_q[...].astype(F32).T.astype(BF16)
    w_in[CH:, :] = w_kv[...].astype(F32).T.astype(BF16)
    w_back[...] = jnp.concatenate([w_q[...].astype(F32), w_kv[...].astype(F32)], axis=1).astype(BF16)
    w_full = w_in[...]
    w_o = w_out[...]
    for copy in copies[4:]:
        copy.wait()

    def visit(row):
        views = normed_views(feats, row, gain_full)
        both = jnp.dot(w_full, jnp.concatenate(views, axis=1), preferred_element_type=F32)
        out_both = jnp.dot(w_o, pair(cot, row), preferred_element_type=F32)
        for j in range(2):
            normed[row, 2 + j] = views[j]
            raw = both[:, j * PIX : (j + 1) * PIX]
            query_scale = inv_rms(raw[:CH])
            put(qs, j, row + 2, (raw[:CH] * query_scale).astype(BF16).astype(F32))
            q_inv[j, pl.ds(row, 1), :] = query_scale
            project_keys(raw[CH:], row + 2, 2, j, ks, vs, k_inv)
            put(ogs, j, row + 2, out_both[:, j * PIX : (j + 1) * PIX])

    each_row(ROWS, (visit,))


def forward_kernel(
    side, left, right, row_halo, left_corner, right_corner, gain, w_in, ogs, qs,
    ks_in, vs_in, k_inv_in, normed_in,
    ks, vs, k_inv, normed, weights, prob_grads, attended, stats,
):
    halo_row, _, _ = halo_start(side)
    gain_full = gain[...]
    w_keys = w_in[CH:, :]

    def piece(ref, offset, first, col):
        def one(row):
            views = normed_views(ref, row, gain_full)
            both = jnp.dot(w_keys, jnp.concatenate(views, axis=1), preferred_element_type=F32)
            for j in range(2):
                normed[row + first, col + j] = views[j]
                project_keys(both[:, j * PIX : (j + 1) * PIX], row + offset, col, j, ks, vs, k_inv)

        return one

    each_row(ROWS, (piece(left, 2, 0, 0), piece(right, 2, 0, 4)))
    each_row(
        2,
        (
            piece(row_halo, halo_row, ROWS, 2),
            piece(left_corner, halo_row, ROWS, 0),
            piece(right_corner, halo_row, ROWS, 4),
        ),
    )

    def attend(step, carry):
        col, head = step // HEADS, step % HEADS
        base = head * (SIZE * S)
        query = [take(qs, col, base + d * S + 2) * SCALE for d in range(SIZE)]
        og = [take(ogs, col, base + d * S + 2) for d in range(SIZE)]
        acc = [jnp.zeros((ROWS, PIX), F32)] * SIZE
        exp_total = jnp.zeros((ROWS, PIX), F32)
        spread = jnp.zeros((ROWS, PIX), F32)
        for j in range(5):
            for i in range(5):
                key = [take(ks, col + j, base + d * S + i) for d in range(SIZE)]
                weight = jnp.exp(total(a * b for a, b in zip(query, key)))
                value = [take(vs, col + j, base + d * S + i) for d in range(SIZE)]
                prob_grad = total(a * b for a, b in zip(og, value))
                acc = [a + weight * b for a, b in zip(acc, value)]
                exp_total = exp_total + weight
                spread = spread + weight * prob_grad
                weights[step, 5 * j + i] = weight
                prob_grads[step, 5 * j + i] = prob_grad
        inv_total = 1.0 / exp_total
        for d in range(SIZE):
            attended[col, pl.ds(pl.multiple_of((head * SIZE + d) * ROWS, ROWS), ROWS), :] = (
                acc[d] * inv_total
            )
        stats[0, step] = inv_total
        stats[1, step] = spread * inv_total
        return carry

    lax.fori_loop(0, COLS * HEADS, attend, 0)


def unit_back(unit, scale, upstream):
    mean = jnp.sum(upstream * unit, axis=0, keepdims=True) * (1.0 / CH)
    return scale[None] * (upstream - unit * mean)


def window(ref, col, row):
    return jnp.stack([take(ref, col, d * S + row) for d in range(CH)], axis=0)


def outer(left, right):
    return lax.dot_general(left, right, (((1,), (1,)), ((), ())), preferred_element_type=F32)


def gradient_kernel(
    side, qs, ks, ogs, q_inv, k_inv, normed, weights, prob_grads, attended, stats, cot,
    weight_sums, raw_query, to_left, to_right, own_raw,
    probs, score_grads, grads, raws, halo_grads, halo_raws,
):
    _, _, edge_row = halo_start(side)
    zeros = jnp.zeros((ROWS, PIX), F32)

    def query_one(step, carry):
        col, head = step // HEADS, step % HEADS
        base = head * (SIZE * S)
        inv_total, spread = stats[0, step], stats[1, step]
        acc = [zeros] * SIZE
        for j in range(5):
            for i in range(5):
                o = 5 * j + i
                prob = weights[step, o] * inv_total
                score_grad = prob * (prob_grads[step, o] - spread) * SCALE
                for ref, values in ((probs, prob), (score_grads, score_grad)):
                    ref[step, pl.ds(o * W, 2), :] = zeros[:2]
                    ref[step, pl.ds(o * W + 2, ROWS), :] = values
                    ref[step, pl.ds(o * W + 10, 2), :] = zeros[:2]
                acc = [a + score_grad * take(ks, col + j, base + d * S + i) for d, a in enumerate(acc)]
        for d in range(SIZE):
            grads[0, head * SIZE + d + col * CH] = acc[d]
        return carry

    lax.fori_loop(0, COLS * HEADS, query_one, 0)

    def query_finish(col, carry):
        first = pl.multiple_of(col * CH, CH)
        raw = unit_back(window(qs, col, 2), q_inv[col], grads[0, pl.ds(first, CH)])
        raws[col, 0 : CH * ROWS, :] = raw.reshape(CH * ROWS, PIX)
        return carry

    lax.fori_loop(0, COLS, query_finish, 0)

    def query_sums(row, carry):
        query_acc, out_acc = carry
        raw = [raws[j, pl.ds(row, CH, stride=ROWS), :].astype(BF16) for j in range(2)]
        mixed = [attended[j, pl.ds(row, CH, stride=ROWS), :].astype(BF16) for j in range(2)]
        for j in range(2):
            raw_query[row, j] = raw[j]
        return (
            query_acc + outer(pair(normed, row, 2), jnp.concatenate(raw, axis=1)),
            out_acc + outer(jnp.concatenate(mixed, axis=1), pair(cot, row)),
        )

    flat = jnp.zeros((CH, CH), F32)
    query_acc, out_acc = lax.fori_loop(0, ROWS, query_sums, (flat, flat))
    weight_sums[CH : 2 * CH, :] = jnp.concatenate([query_acc, out_acc], axis=1)

    def key_step(acc, step, col, j, i, base, first_row):
        key_acc, value_acc = acc
        start = first_row - i + 2
        prob = probs[step, pl.ds((5 * j + i) * W + start, ROWS), :]
        score_grad = score_grads[step, pl.ds((5 * j + i) * W + start, ROWS), :]
        key_acc = [a + score_grad * take(qs, col, base + d * S + start) for d, a in enumerate(key_acc)]
        value_acc = [a + prob * take(ogs, col, base + d * S + start) for d, a in enumerate(value_acc)]
        return key_acc, value_acc

    edge_first, edge_offset = edge_row * 2 // 3, edge_row // 2

    def key_columns(view_col, head, cols):
        base = head * (SIZE * S)
        acc = ([zeros] * SIZE, [zeros] * SIZE)
        for col in cols:
            for i in range(5):
                acc = key_step(acc, col * HEADS + head, col, view_col - col, i, base, 2)
        for d in range(SIZE):
            grads[view_col, head * SIZE + d] = acc[0][d]
            grads[view_col, CH + head * SIZE + d] = acc[1][d]
        acc = ([zeros] * SIZE, [zeros] * SIZE)
        for col in cols:
            for i in range(2):
                acc = key_step(
                    acc, col * HEADS + head, col, view_col - col, edge_offset + i, base, edge_first
                )
        for d in range(SIZE):
            halo_grads[view_col, head * SIZE + d] = acc[0][d]
            halo_grads[view_col, CH + head * SIZE + d] = acc[1][d]

    def inner_columns(step, carry):
        key_columns(1 + step // HEADS, step % HEADS, (0, 1))
        return carry

    def outer_columns(step, carry):
        side_col = step // HEADS
        key_columns(5 * side_col, step % HEADS, (side_col,))
        return carry

    lax.fori_loop(0, 4 * HEADS, inner_columns, 0)
    lax.fori_loop(0, 2 * HEADS, outer_columns, 0)

    def key_finish(col, carry):
        for source, target, row in ((grads, raws, 2), (halo_grads, halo_raws, edge_first)):
            scale = k_inv[col, pl.ds(row, ROWS), :]
            raw = unit_back(window(ks, col, row), scale, source[col, 0:CH])
            target[col, 0 : CH * ROWS, :] = raw.reshape(CH * ROWS, PIX)
            target[col, CH * ROWS :, :] = source[col, CH:].reshape(CH * ROWS, PIX)
        return carry

    lax.fori_loop(0, 6, key_finish, 0)

    def key_sums(source, from_row, first):
        def one(row, acc):
            for col, target in ((0, to_left), (2, own_raw), (4, to_right)):
                raw = [
                    source[col + j, pl.ds(row + from_row, 2 * CH, stride=ROWS), :].astype(BF16)
                    for j in range(2)
                ]
                for j in range(2):
                    target[row + first, j] = raw[j]
                acc = acc + outer(pair(normed, row + first, col), jnp.concatenate(raw, axis=1))
            return acc

        return one

    acc = lax.fori_loop(0, ROWS, key_sums(raws, 0, 0), jnp.zeros((CH, 2 * CH), F32))
    weight_sums[0:CH, :] = lax.fori_loop(0, 2, key_sums(halo_raws, edge_row, ROWS), acc)


def features_kernel(
    side, own_raw, left_raw, right_raw, row_raw, raw_query, feats, cot, gain, w_back,
    feats_grad, shared,
):
    _, _, edge_row = halo_start(side)

    def join(row):
        for j in range(2):
            shared[row, j] = (
                own_raw[row, j].astype(F32) + left_raw[row, j].astype(F32)
                + right_raw[row, j].astype(F32)
            )

    def join_edge(row):
        for j in range(2):
            shared[row + edge_row, j] = shared[row + edge_row, j] + row_raw[row, j].astype(F32)

    each_row(ROWS, (join,))
    each_row(2, (join_edge,))
    gain_full = gain[...]
    w_b = w_back[...]

    def view_row(row):
        raw = jnp.concatenate([pair(raw_query, row), pair(shared, row).astype(BF16)], axis=0)
        normed_grad = jnp.dot(w_b, raw, preferred_element_type=F32)
        for j in range(2):
            values = feats[row, j].astype(F32)
            inv_norm = inv_rms(values)
            scaled = values * inv_norm
            scaled_grad = normed_grad[:, j * PIX : (j + 1) * PIX] * gain_full
            mean = jnp.mean(scaled_grad * scaled, axis=0, keepdims=True)
            branch = inv_norm * (scaled_grad - scaled * mean)
            feats_grad[row, j] = (cot[row, j].astype(F32) + branch).astype(BF16)

    each_row(ROWS, (view_row,))


def last_kernel(factor, sums, w_q, w_kv, gain, query_grad, keyval_grad, output_grad, gain_grad):
    keyval = sums[0:CH, :] * factor
    rest = sums[CH : 2 * CH, :] * factor
    query = rest[:, :CH]
    keyval_grad[...] = keyval
    query_grad[...] = query
    output_grad[...] = rest[:, CH:]
    col = jnp.sum(query * w_q[...].astype(F32), axis=1, keepdims=True) + jnp.sum(
        keyval * w_kv[...].astype(F32), axis=1, keepdims=True
    )
    line = jnp.sum(jnp.where(eye(), jnp.broadcast_to(col, (CH, CH)), 0.0), axis=0, keepdims=True)
    gain_grad[...] = line / gain[...]


def call(kernel, outs, scratch, flops, *operands, aliases=(), far=()):
    return pl.pallas_call(
        kernel,
        out_shape=[jax.ShapeDtypeStruct(shape, dtype) for shape, dtype in outs],
        in_specs=[
            SM if x.dtype == jnp.int32 else FAR if k in far else VM for k, x in enumerate(operands)
        ],
        out_specs=[VM] * len(outs),
        scratch_shapes=[pltpu.VMEM(x, F32) if isinstance(x, tuple) else x for x in scratch],
        input_output_aliases=dict(aliases),
        compiler_params=pltpu.CompilerParams(vmem_limit_bytes=32 * 1024 * 1024),
        cost_estimate=pl.CostEstimate(flops=flops, bytes_accessed=1000000, transcendentals=0),
    )(*operands)


def sum_everywhere(values):
    near, far = ("px", "pc", "vrow"), ("py", "vcol")
    near_count, far_count = (math.prod(lax.axis_size(a) for a in axes) for axes in (near, far))
    shares = lax.all_to_all(values.reshape(near_count, -1, PIX), near, 0, 0)
    share = jnp.sum(shares, axis=0).astype(BF16)
    copies = jnp.broadcast_to(share[None], (far_count,) + share.shape)
    shares = lax.all_to_all(copies, far, 0, 0)
    share = jnp.sum(shares.astype(F32), axis=0)
    copies = jnp.broadcast_to(share[None], (near_count,) + share.shape)
    return lax.all_to_all(copies, near, 0, 0).reshape(values.shape)


def layer(features, out_cotangent, norm_gain, query_proj, keyval_proj, output_proj):
    side = lax.axis_index("vrow").astype(jnp.int32).reshape(1)
    cols = lax.axis_size("vcol")
    up = [(i, i + 1) for i in range(cols - 1)]
    down = [(j, i) for i, j in up]
    cross = [(0, 1), (1, 0)]
    diag_up = [(a * cols + i, b * cols + j) for a, b in cross for i, j in up]
    diag_down = [(a * cols + i, b * cols + j) for a, b in cross for i, j in down]
    grid = ("vrow", "vcol")
    gain = norm_gain.reshape(1, CH)
    held = [
        pltpu.with_memory_space_constraint(x, pltpu.HBM)
        for x in (features, out_cotangent, gain, query_proj, keyval_proj, output_proj)
    ]

    left = lax.ppermute(features, "vcol", up)
    right = lax.ppermute(features, "vcol", down)
    (edge,) = call(
        edge_kernel, [((2, COLS, CH, PIX), BF16)], [pltpu.SemaphoreType.DMA], 1000, side, held[0],
        far=(1,),
    )
    row_halo = lax.ppermute(edge, "vrow", cross)
    left_corner = lax.ppermute(edge, grid, diag_up)
    right_corner = lax.ppermute(edge, grid, diag_down)

    own = ((COLS, CH * S, PIX), F32)
    padded = ((6, CH * S, PIX), F32)
    lanes = ((COLS, ROWS, PIX), F32)
    key_lanes = ((6, 16, PIX), F32)
    steps = COLS * HEADS
    offsets = ((steps, 25, ROWS, PIX), F32)
    views = ((ROWS, COLS, CH, PIX), BF16)
    all_views = ((ROWS + 2, 6, CH, PIX), BF16)
    key_views = ((ROWS + 2, COLS, 2 * CH, PIX), BF16)
    (
        qs, ks, vs, ogs, q_inv, k_inv, normed, gain_full, w_in, w_back, feats, cot, w_q, w_kv, gain_row,
    ) = call(
        own_kernel,
        [
            own, padded, padded, own, lanes, key_lanes, all_views, ((CH, PIX), F32),
            ((3 * CH, CH), BF16), ((CH, 3 * CH), BF16), views, views, ((CH, CH), BF16),
            ((CH, 2 * CH), BF16), ((1, CH), F32),
        ],
        [pltpu.VMEM((CH, CH), BF16), pltpu.SemaphoreType.DMA((6,))], 2000000,
        side, *held, far=(1, 2, 3, 4, 5, 6),
    )
    ks, vs, k_inv, normed, weights, prob_grads, attended, stats = call(
        forward_kernel,
        [
            padded, padded, key_lanes, all_views, offsets, offsets,
            ((COLS, CH * ROWS, PIX), F32), ((2, steps, ROWS, PIX), F32),
        ],
        [], 4000000,
        side, left, right, row_halo, left_corner, right_corner, gain_full, w_in, ogs, qs,
        ks, vs, k_inv, normed,
        aliases=((10, 0), (11, 1), (12, 2), (13, 3)),
    )
    weight_sums, raw_query, to_left, to_right, own_raw = call(
        gradient_kernel,
        [((2 * CH, PIX), F32), views, key_views, key_views, key_views],
        [
            (steps, 25 * W, PIX), (steps, 25 * W, PIX), (6, 2 * CH, ROWS, PIX),
            (6, 2 * CH * ROWS, PIX), (6, 2 * CH, ROWS, PIX), (6, 2 * CH * ROWS, PIX),
        ],
        5000000,
        side, qs, ks, ogs, q_inv, k_inv, normed, weights, prob_grads, attended, stats, cot,
    )
    sums = sum_everywhere(weight_sums)
    right_raw = lax.ppermute(to_left, "vcol", down)
    left_raw = lax.ppermute(to_right, "vcol", up)
    row_send = sum(x[ROWS:].astype(F32) for x in (own_raw, left_raw, right_raw)).astype(BF16)
    row_raw = lax.ppermute(row_send, "vrow", cross)
    (features_grad,) = call(
        features_kernel, [(features.shape, BF16)], [(ROWS, COLS, 2 * CH, PIX)], 2000000,
        side, own_raw, left_raw, right_raw, row_raw, raw_query, feats, cot, gain_full, w_back,
    )
    tokens_all = ROWS * COLS * PIX * math.prod(lax.axis_size(a) for a in AXES)
    query_grad, keyval_grad, output_grad, gain_grad = call(
        functools.partial(last_kernel, 1.0 / math.sqrt(tokens_all)),
        [((CH, CH), F32), ((CH, 2 * CH), F32), ((CH, CH), F32), ((1, CH), F32)],
        [], 100000,
        sums, w_q, w_kv, gain_row,
    )
    return features_grad, query_grad, keyval_grad, output_grad, gain_grad.reshape(CH)


def solution(mesh):
    rows, cols, _ = mesh.devices.shape
    parts = jax.sharding.Mesh(mesh.devices.reshape(rows, cols, 4, 4, 2), AXES)
    placed = P("vrow", "vcol", None, AXES[2:])
    return jax.shard_map(
        layer,
        mesh=parts,
        in_specs=(placed, placed, P(), P(), P(), P()),
        out_specs=(placed, P(), P(), P(), P()),
        check_vma=False,
    )
```

time: 110 us -> 97.8 us (0.89)
  blocking collectives: 53.9 us -> 23.1 us
  starting transfers between devices: 31 us -> 40.5 us
  waiting for transfers between devices: 1.67 us -> 9.3 us
  Pallas kernels: 21.6 us -> 22.9 us
    all_to_all x1 -> x0, blocking collectives: 28.9 us -> none  [sum_everywhere(): share = jnp.sum(lax.all_to_all(copies, far, 0, 0).astype(F32), axis=0)]
    all_to_all x0 -> x1, starting transfers between devices: none -> 17.1 us  [sum_everywhere(): shares = lax.all_to_all(copies, far, 0, 0)]
    all_to_all x0 -> x1, waiting for transfers between devices: none -> 8.82 us  [sum_everywhere(): shares = lax.all_to_all(copies, far, 0, 0)]
    ppermute x5 -> x3, starting transfers between devices: 15.9 us -> 7.58 us  [the longest x1 3.97 us: layer(): left_raw = lax.ppermute(to_right, 'vcol', up)]
    all_to_all x1, blocking collectives: 14.8 us -> 12.8 us  [sum_everywhere(): shares = lax.all_to_all(values.reshape(near_count, -1, PIX), near, 0, 0)]
    ppermute x1, starting transfers between devices: 4.51 us -> 6.26 us  [layer(): left_corner = lax.ppermute(edge, grid, diag_up)]
    ppermute x5 -> x3, waiting for transfers between devices: 1.66 us -> 0.01 us  [the longest x1 0.01 us: layer(): left_raw = lax.ppermute(to_right, 'vcol', up)]
    pallas_call x7 -> x6, Pallas kernels: 21.6 us -> 22.9 us  [call(): pl.pallas_call(kernel, out_shape=[jax.ShapeDtypeStruct(shape, dtype) for...]
  transfers between devices with their start and end apart: 10 -> 9, of which waited for: 1 -> 2; matrix products, arithmetic and copies ran while one was open for 0% -> 1% of each run, Pallas kernels for 14% -> 5%
where the time goes in v3:
time: 97.8 us; the launch traced here: 97.3 us
  starting transfers between devices  40.5 us (41%)
  blocking collectives  23.1 us (24%)
  Pallas kernels  22.9 us (23%)
  waiting for transfers between devices  9.3 us (10%)
    pallas_call x6, Pallas kernels, call(): pl.pallas_call(kernel, out_shape=[jax.ShapeDtypeStruct(shape, dtype) for...  22.9 us
    all_to_all x1, starting transfers between devices, sum_everywhere(): shares = lax.all_to_all(copies, far, 0, 0)  17.1 us
    all_to_all x1, blocking collectives, sum_everywhere(): shares = lax.all_to_all(values.reshape(near_count, -1, PIX), near, 0, 0)  12.8 us
    all_to_all x1, blocking collectives, sum_everywhere(): return lax.all_to_all(copies, near, 0, 0).reshape(values.shape)  10.2 us
    all_to_all x1, waiting for transfers between devices, sum_everywhere(): shares = lax.all_to_all(copies, far, 0, 0)  8.82 us
    ppermute x1, starting transfers between devices, layer(): left_corner = lax.ppermute(edge, grid, diag_up)  6.26 us
    ppermute x1, starting transfers between devices, layer(): left = lax.ppermute(features, 'vcol', up)  4.83 us
    ppermute x1, starting transfers between devices, layer(): left_raw = lax.ppermute(to_right, 'vcol', up)  3.97 us
  transfers between devices with their start and end apart: 9, of which 2 were waited for; matrix products, arithmetic and copies ran while one was open for 1% of the time, Pallas kernels for 5%

profile of v3, /device:TPU:1, one launch (start us, length us, event | category | flops | bytes accessed | tf_op | source)
XLA Modules:
  0.0 97.3 jit_solution(17294263661276634971)
XLA Ops:
  0.6 4.8 %collective-permute-start = (bf16[8,2,64,128]{3,2,1,0:T(8,128)(2,1)}, bf16[8,2,64,128]{3,2,1,0:T(8,128)(2,1)S(1)}, u32[]{:S(2)}, u32[]{:S(2)}) collective-permute-start(bf16[8,2,64,128]{3,2,1,0:T(8,128)(2,1)} %feats.1), channel_id=1, source_target_pairs={{0,32},{32,64},{64,96},{96,128},{128,160},{160,192},{192,224},{1,3... | collective-permute-start | bytes 786440 | tf_op jit(solution)/shard_map/ppermute | solution.py:441
  5.5 1.3 %collective-permute-start.1 = (bf16[8,2,64,128]{3,2,1,0:T(8,128)(2,1)}, bf16[8,2,64,128]{3,2,1,0:T(8,128)(2,1)S(1)}, u32[]{:S(2)}, u32[]{:S(2)}) collective-permute-start(bf16[8,2,64,128]{3,2,1,0:T(8,128)(2,1)} %feats.1), channel_id=1, source_target_pairs={{32,0},{64,32},{96,64},{128,96},{160,128},{192,160},{224,192},{33,... | collective-permute-start | bytes 786440 | tf_op jit(solution)/shard_map/ppermute | solution.py:442
  6.8 0.9 shard_map.102
  7.6 1.3 %collective-permute-start.4 = (bf16[2,2,64,128]{3,2,1,0:T(8,128)(2,1)S(1)}, bf16[2,2,64,128]{3,2,1,0:T(8,128)(2,1)S(1)}, u32[]{:S(2)}, u32[]{:S(2)}) collective-permute-start(bf16[2,2,64,128]{3,2,1,0:T(8,128)(2,1)S(1)} %shard_map.102), channel_id=1, source_target_pairs={{32,256},{64,288},{96,320},{128,352},{160,384},{192,416},{224,448}... | collective-permute-start | bytes 196616 | tf_op jit(solution)/shard_map/ppermute | solution.py:449
  8.9 6.3 %collective-permute-start.3 = (bf16[2,2,64,128]{3,2,1,0:T(8,128)(2,1)S(1)}, bf16[2,2,64,128]{3,2,1,0:T(8,128)(2,1)S(1)}, u32[]{:S(2)}, u32[]{:S(2)}) collective-permute-start(bf16[2,2,64,128]{3,2,1,0:T(8,128)(2,1)S(1)} %shard_map.102), channel_id=1, source_target_pairs={{0,288},{32,320},{64,352},{96,384},{128,416},{160,448},{192,480},{... | collective-permute-start | bytes 196616 | tf_op jit(solution)/shard_map/ppermute | solution.py:448
  15.2 2.1 %collective-permute-start.2 = (bf16[2,2,64,128]{3,2,1,0:T(8,128)(2,1)S(1)}, bf16[2,2,64,128]{3,2,1,0:T(8,128)(2,1)S(1)}, u32[]{:S(2)}, u32[]{:S(2)}) collective-permute-start(bf16[2,2,64,128]{3,2,1,0:T(8,128)(2,1)S(1)} %shard_map.102), channel_id=1, source_target_pairs={{0,256},{256,0},{1,257},{257,1},{2,258},{258,2},{3,259},{259,3},{4... | collective-permute-start | bytes 196616 | tf_op jit(solution)/shard_map/ppermute | solution.py:447
  17.3 2.9 %shard_map.101 = (f32[2,832,128]{2,1,0:T(8,128)S(1)}, f32[6,832,128]{2,1,0:T(8,128)S(1)}, f32[6,832,128]{2,1,0:T(8,128)S(1)}, f32[2,832,128]{2,1,0:T(8,128)S(1)}...) custom-call(s32[1]{0:T(128)} %bitcast.side, ...), custom_call_target="tpu_custom_call" | custom-call | flops 2000000 | bytes 1000000 | tf_op jit(solution)/shard_map/pallas_call | solution.py:400
  20.2 0.0 collective-permute-done.4.right_corner
  20.2 0.0 collective-permute-done.3.left_corner
  20.2 0.5 collective-permute-done.2.row_halo
  20.7 0.0 collective-permute-done.left
  20.7 0.0 collective-permute-done.1.right
  20.7 5.6 %shard_map.103 = (f32[6,832,128]{2,1,0:T(8,128)S(1)}, f32[6,832,128]{2,1,0:T(8,128)S(1)}, f32[6,16,128]{2,1,0:T(8,128)S(1)}, bf16[10,6,64,128]{3,2,1,0:T(8,128)(...) custom-call(s32[1]{0:T(128)} %bitcast.side, ...), custom_call_target="tpu_custom_call", output_to_operand_aliasing={{0}: (10, {}), {1}: (11, {}), {2}: (12, {}), {3}: (13, {})} | custom-call | flops 4000000 | bytes 1000000 | tf_op jit(solution)/shard_map/pallas_call | solution.py:400
  26.3 10.5 %shard_map.104 = (f32[128,128]{1,0:T(8,128)S(1)}, bf16[8,2,64,128]{3,2,1,0:T(8,128)(2,1)S(1)}, bf16[10,2,128,128]{3,2,1,0:T(8,128)(2,1)}, bf16[10,2,128,128]{3,2,1,0:T(8,128)(2,1)}, bf16[10,2,128,128]{3,2,1,0:T(8,128)(2,1)S(1)}) custom-call(s32[1]{0:T(128)} %bitcast.side, f32[2,832,128]{2,1,0:T(8,128)S(1)} %get-tuple-element.36.qs, ...), custom_call_target="tpu_custom_call" | custom-call | flops 5000000 | bytes 1000000 | tf_op jit(solution)/shard_map/pallas_call | solution.py:400
  36.8 4.0 %collective-permute-start.5 = (bf16[10,2,128,128]{3,2,1,0:T(8,128)(2,1)}, bf16[10,2,128,128]{3,2,1,0:T(8,128)(2,1)S(1)}, u32[]{:S(2)}, u32[]{:S(2)}) collective-permute-start(bf16[10,2,128,128]{3,2,1,0:T(8,128)(2,1)} %get-tuple-element.54), channel_id=1, source_target_pairs={{0,32},{32,64},{64,96},{96,128},{128,160},{160,192},{192,224},{1,3... | collective-permute-start | bytes 1966088 | tf_op jit(solution)/shard_map/ppermute | solution.py:495
  40.8 1.3 %collective-permute-start.6 = (bf16[10,2,128,128]{3,2,1,0:T(8,128)(2,1)}, bf16[10,2,128,128]{3,2,1,0:T(8,128)(2,1)S(1)}, u32[]{:S(2)}, u32[]{:S(2)}) collective-permute-start(bf16[10,2,128,128]{3,2,1,0:T(8,128)(2,1)} %get-tuple-element.55), channel_id=1, source_target_pairs={{32,0},{64,32},{96,64},{128,96},{160,128},{192,160},{224,192},{33,... | collective-permute-start | bytes 1966088 | tf_op jit(solution)/shard_map/ppermute | solution.py:494
  42.1 12.8 %all_to_all.15 = f32[16,8,128]{2,1,0:T(8,128)S(1)} all-to-all(f32[16,8,128]{2,1,0:T(8,128)S(1)} %bitcast.6), channel_id=1, replica_groups=mesh['vrow'=2,'vcol'=8,'px'=4,'py'=4,'pc'=2] {'px','pc','vrow'}, dimensions={0} | all-to-all | bytes 131072 | tf_op jit(solution)/shard_map/all_to_all | solution.py:417
  54.9 0.6 broadcast_in_dim.4
  55.6 17.1 %all-to-all-start.1 = ((bf16[32,8,128]{2,1,0:T(8,128)(2,1)}), bf16[32,8,128]{2,1,0:T(8,128)(2,1)S(1)}, u32[]{:S(2)}, u32[]{:S(2)}) async-start(bf16[32,8,128]{2,1,0:T(8,128)(2,1)} %broadcast_in_dim.4), calls=%async_computation.1 | async-start | bytes 131072 | tf_op jit(solution)/shard_map/all_to_all | solution.py:420
  72.7 0.0 collective-permute-done.5.left_raw
  72.7 0.0 collective-permute-done.6.right_raw
  72.7 0.1 add_convert_fusion
  72.8 2.3 %collective-permute-start.7 = (bf16[2,2,128,128]{3,2,1,0:T(8,128)(2,1)S(1)}, bf16[2,2,128,128]{3,2,1,0:T(8,128)(2,1)S(1)}, u32[]{:S(2)}, u32[]{:S(2)}) collective-permute-start(bf16[2,2,128,128]{3,2,1,0:T(8,128)(2,1)S(1)} %add_convert_fusion), channel_id=1, source_target_pairs={{0,256},{256,0},{1,257},{257,1},{2,258},{258,2},{3,259},{259,3},{4... | collective-permute-start | bytes 393224 | tf_op jit(solution)/shard_map/ppermute | solution.py:497
  75.1 8.8 %all-to-all-done.1 = bf16[32,8,128]{2,1,0:T(8,128)(2,1)S(1)} async-done(((bf16[32,8,128]{2,1,0:T(8,128)(2,1)}), bf16[32,8,128]{2,1,0:T(8,128)(2,1)S(1)}, u32[]{:S(2)}, u32[]{:S(2)}) %all-to-all-start.1) | async-done | bytes 65568 | tf_op jit(solution)/shard_map/all_to_all | solution.py:420
  84.0 10.2 %all_to_all.16 = f32[16,8,128]{2,1,0:T(8,128)S(1)} all-to-all(f32[16,8,128]{2,1,0:T(8,128)S(1)} %broadcast_in_dim.5), channel_id=1, replica_groups=mesh['vrow'=2,'vcol'=8,'px'=4,'py'=4,'pc'=2] {'px','pc','vrow'}, dimensions={0} | all-to-all | bytes 131072 | tf_op jit(solution)/shard_map/all_to_all | solution.py:423
  94.2 0.7 shard_map.106
  95.0 0.0 collective-permute-done.7.row_raw
  95.0 2.3 %shard_map.105 = bf16[8,2,64,128]{3,2,1,0:T(8,128)(2,1)} custom-call(s32[1]{0:T(128)} %bitcast.side, bf16[10,2,128,128]{3,2,1,0:T(8,128)(2,1)S(1)} %get-tuple-element.53.own_raw, bf16[10,2,128,128]{3,2,1,0:T(8,128)(2,1)S(1)} %collective-permute-done.5.left_raw, bf16[10,2,128,128]{3,2,1,0:T(8,128)(2,1)S(1)} %collective-permute-done.6.right_raw, ...), custom_call_target="tpu_custom_call" | custom-call | flops 2000000 | bytes 1000000 | tf_op jit(solution)/shard_map/pallas_call | solution.py:400
  (3 shorter events, 0.1 us)
Async XLA Ops:
  0.6 20.1 %collective-permute-start = (bf16[8,2,64,128]{3,2,1,0:T(8,128)(2,1)}, bf16[8,2,64,128]{3,2,1,0:T(8,128)(2,1)S(1)}, u32[]{:S(2)}, u32[]{:S(2)}) collective-permute-start(bf16[8,2,64,128]{3,2,1,0:T(8,128)(2,1)} %feats.1), channel_id=1, source_target_pairs={{0,32},{32,64},{64,96},{96,128},{128,160},{160,192},{192,224},{1,3... | collective-permute-start | bytes 786440 | tf_op jit(solution)/shard_map/ppermute | solution.py:441
  5.5 15.2 %collective-permute-start.1 = (bf16[8,2,64,128]{3,2,1,0:T(8,128)(2,1)}, bf16[8,2,64,128]{3,2,1,0:T(8,128)(2,1)S(1)}, u32[]{:S(2)}, u32[]{:S(2)}) collective-permute-start(bf16[8,2,64,128]{3,2,1,0:T(8,128)(2,1)} %feats.1), channel_id=1, source_target_pairs={{32,0},{64,32},{96,64},{128,96},{160,128},{192,160},{224,192},{33,... | collective-permute-start | bytes 786440 | tf_op jit(solution)/shard_map/ppermute | solution.py:442
  7.6 12.6 %collective-permute-start.4 = (bf16[2,2,64,128]{3,2,1,0:T(8,128)(2,1)S(1)}, bf16[2,2,64,128]{3,2,1,0:T(8,128)(2,1)S(1)}, u32[]{:S(2)}, u32[]{:S(2)}) collective-permute-start(bf16[2,2,64,128]{3,2,1,0:T(8,128)(2,1)S(1)} %shard_map.102), channel_id=1, source_target_pairs={{32,256},{64,288},{96,320},{128,352},{160,384},{192,416},{224,448}... | collective-permute-start | bytes 196616 | tf_op jit(solution)/shard_map/ppermute | solution.py:449
  8.9 11.3 %collective-permute-start.3 = (bf16[2,2,64,128]{3,2,1,0:T(8,128)(2,1)S(1)}, bf16[2,2,64,128]{3,2,1,0:T(8,128)(2,1)S(1)}, u32[]{:S(2)}, u32[]{:S(2)}) collective-permute-start(bf16[2,2,64,128]{3,2,1,0:T(8,128)(2,1)S(1)} %shard_map.102), channel_id=1, source_target_pairs={{0,288},{32,320},{64,352},{96,384},{128,416},{160,448},{192,480},{... | collective-permute-start | bytes 196616 | tf_op jit(solution)/shard_map/ppermute | solution.py:448
  15.2 5.5 %collective-permute-start.2 = (bf16[2,2,64,128]{3,2,1,0:T(8,128)(2,1)S(1)}, bf16[2,2,64,128]{3,2,1,0:T(8,128)(2,1)S(1)}, u32[]{:S(2)}, u32[]{:S(2)}) collective-permute-start(bf16[2,2,64,128]{3,2,1,0:T(8,128)(2,1)S(1)} %shard_map.102), channel_id=1, source_target_pairs={{0,256},{256,0},{1,257},{257,1},{2,258},{258,2},{3,259},{259,3},{4... | collective-permute-start | bytes 196616 | tf_op jit(solution)/shard_map/ppermute | solution.py:447
  36.8 35.9 %collective-permute-start.5 = (bf16[10,2,128,128]{3,2,1,0:T(8,128)(2,1)}, bf16[10,2,128,128]{3,2,1,0:T(8,128)(2,1)S(1)}, u32[]{:S(2)}, u32[]{:S(2)}) collective-permute-start(bf16[10,2,128,128]{3,2,1,0:T(8,128)(2,1)} %get-tuple-element.54), channel_id=1, source_target_pairs={{0,32},{32,64},{64,96},{96,128},{128,160},{160,192},{192,224},{1,3... | collective-permute-start | bytes 1966088 | tf_op jit(solution)/shard_map/ppermute | solution.py:495
  40.8 32.0 %collective-permute-start.6 = (bf16[10,2,128,128]{3,2,1,0:T(8,128)(2,1)}, bf16[10,2,128,128]{3,2,1,0:T(8,128)(2,1)S(1)}, u32[]{:S(2)}, u32[]{:S(2)}) collective-permute-start(bf16[10,2,128,128]{3,2,1,0:T(8,128)(2,1)} %get-tuple-element.55), channel_id=1, source_target_pairs={{32,0},{64,32},{96,64},{128,96},{160,128},{192,160},{224,192},{33,... | collective-permute-start | bytes 1966088 | tf_op jit(solution)/shard_map/ppermute | solution.py:494
  55.6 28.4 %all-to-all-start.1 = ((bf16[32,8,128]{2,1,0:T(8,128)(2,1)}), bf16[32,8,128]{2,1,0:T(8,128)(2,1)S(1)}, u32[]{:S(2)}, u32[]{:S(2)}) async-start(bf16[32,8,128]{2,1,0:T(8,128)(2,1)} %broadcast_in_dim.4), calls=%async_computation.1 | async-start | bytes 131072 | tf_op jit(solution)/shard_map/all_to_all | solution.py:420
  72.8 22.2 %collective-permute-start.7 = (bf16[2,2,128,128]{3,2,1,0:T(8,128)(2,1)S(1)}, bf16[2,2,128,128]{3,2,1,0:T(8,128)(2,1)S(1)}, u32[]{:S(2)}, u32[]{:S(2)}) collective-permute-start(bf16[2,2,128,128]{3,2,1,0:T(8,128)(2,1)S(1)} %add_convert_fusion), channel_id=1, source_target_pairs={{0,256},{256,0},{1,257},{257,1},{2,258},{258,2},{3,259},{259,3},{4... | collective-permute-start | bytes 393224 | tf_op jit(solution)/shard_map/ppermute | solution.py:497

commit v4 on v3

--- a/solution.py
+++ b/solution.py
@@ -18,6 +18,7 @@
 PIX = 128
 S = 13
 W = 13
+R = 9
 EPSILON = 1e-06
 SCALE = SIZE ** (-0.5)
 F32 = jnp.float32
@@ -200,9 +201,7 @@
                 prob_grads[step, 5 * j + i] = prob_grad
         inv_total = 1.0 / exp_total
         for d in range(SIZE):
-            attended[col, pl.ds(pl.multiple_of((head * SIZE + d) * ROWS, ROWS), ROWS), :] = (
-                acc[d] * inv_total
-            )
+            attended[col, pl.ds((head * SIZE + d) * R, ROWS), :] = acc[d] * inv_total
         stats[0, step] = inv_total
         stats[1, step] = spread * inv_total
         return carry
@@ -221,6 +220,10 @@
 
 def outer(left, right):
     return lax.dot_general(left, right, (((1,), (1,)), ((), ())), preferred_element_type=F32)
+
+
+def view(ref, col, row, channels):
+    return ref[col, pl.ds(row, channels, stride=R), :].astype(BF16)
 
 
 def gradient_kernel(
@@ -230,49 +233,55 @@
 ):
     _, _, edge_row = halo_start(side)
     zeros = jnp.zeros((ROWS, PIX), F32)
+    pads = jnp.zeros((25, PIX), F32)
 
     def query_one(step, carry):
         col, head = step // HEADS, step % HEADS
         base = head * (SIZE * S)
+        for ref in (probs, score_grads):
+            for row in (0, 1, 10, 11):
+                ref[step, pl.ds(row, 25, stride=W), :] = pads
         inv_total, spread = stats[0, step], stats[1, step]
         acc = [zeros] * SIZE
         for j in range(5):
             for i in range(5):
                 o = 5 * j + i
                 prob = weights[step, o] * inv_total
-                score_grad = prob * (prob_grads[step, o] - spread) * SCALE
-                for ref, values in ((probs, prob), (score_grads, score_grad)):
-                    ref[step, pl.ds(o * W, 2), :] = zeros[:2]
-                    ref[step, pl.ds(o * W + 2, ROWS), :] = values
-                    ref[step, pl.ds(o * W + 10, 2), :] = zeros[:2]
+                score_grad = prob * (prob_grads[step, o] - spread)
+                probs[step, pl.ds(o * W + 2, ROWS), :] = prob
+                score_grads[step, pl.ds(o * W + 2, ROWS), :] = score_grad
                 acc = [a + score_grad * take(ks, col + j, base + d * S + i) for d, a in enumerate(acc)]
         for d in range(SIZE):
-            grads[0, head * SIZE + d + col * CH] = acc[d]
+            grads[col, head * SIZE + d] = acc[d]
         return carry
 
     lax.fori_loop(0, COLS * HEADS, query_one, 0)
 
     def query_finish(col, carry):
-        first = pl.multiple_of(col * CH, CH)
-        raw = unit_back(window(qs, col, 2), q_inv[col], grads[0, pl.ds(first, CH)])
-        raws[col, 0 : CH * ROWS, :] = raw.reshape(CH * ROWS, PIX)
+        raw = unit_back(window(qs, col, 2), q_inv[col] * SCALE, grads[col])
+        for d in range(CH):
+            raws[col, pl.ds(d * R, ROWS), :] = raw[d]
         return carry
 
     lax.fori_loop(0, COLS, query_finish, 0)
 
-    def query_sums(row, carry):
+    def query_sums(half, carry):
         query_acc, out_acc = carry
-        raw = [raws[j, pl.ds(row, CH, stride=ROWS), :].astype(BF16) for j in range(2)]
-        mixed = [attended[j, pl.ds(row, CH, stride=ROWS), :].astype(BF16) for j in range(2)]
-        for j in range(2):
-            raw_query[row, j] = raw[j]
-        return (
-            query_acc + outer(pair(normed, row, 2), jnp.concatenate(raw, axis=1)),
-            out_acc + outer(jnp.concatenate(mixed, axis=1), pair(cot, row)),
+        raw, mixed, normed_all, cot_all = [], [], [], []
+        for row in (2 * half, 2 * half + 1):
+            for j in range(2):
+                raw.append(view(raws, j, row, CH))
+                raw_query[row, j] = raw[-1]
+                mixed.append(view(attended, j, row, CH))
+                normed_all.append(normed[row, 2 + j])
+                cot_all.append(cot[row, j])
+        raw, mixed, normed_all, cot_all = (
+            jnp.concatenate(x, axis=1) for x in (raw, mixed, normed_all, cot_all)
         )
+        return query_acc + outer(normed_all, raw), out_acc + outer(mixed, cot_all)
 
     flat = jnp.zeros((CH, CH), F32)
-    query_acc, out_acc = lax.fori_loop(0, ROWS, query_sums, (flat, flat))
+    query_acc, out_acc = lax.fori_loop(0, ROWS // 2, query_sums, (flat, flat))
     weight_sums[CH : 2 * CH, :] = jnp.concatenate([query_acc, out_acc], axis=1)
 
     def key_step(acc, step, col, j, i, base, first_row):
@@ -288,22 +297,18 @@
 
     def key_columns(view_col, head, cols):
         base = head * (SIZE * S)
-        acc = ([zeros] * SIZE, [zeros] * SIZE)
-        for col in cols:
-            for i in range(5):
-                acc = key_step(acc, col * HEADS + head, col, view_col - col, i, base, 2)
-        for d in range(SIZE):
-            grads[view_col, head * SIZE + d] = acc[0][d]
-            grads[view_col, CH + head * SIZE + d] = acc[1][d]
-        acc = ([zeros] * SIZE, [zeros] * SIZE)
-        for col in cols:
-            for i in range(2):
-                acc = key_step(
-                    acc, col * HEADS + head, col, view_col - col, edge_offset + i, base, edge_first
-                )
-        for d in range(SIZE):
-            halo_grads[view_col, head * SIZE + d] = acc[0][d]
-            halo_grads[view_col, CH + head * SIZE + d] = acc[1][d]
+        own_steps = [(i, 2) for i in range(5)]
+        halo_steps = [(edge_offset + i, edge_first) for i in range(2)]
+        for steps, key_ref, value_ref in (
+            (own_steps, grads, raws), (halo_steps, halo_grads, halo_raws)
+        ):
+            acc = ([zeros] * SIZE, [zeros] * SIZE)
+            for col in cols:
+                for i, first_row in steps:
+                    acc = key_step(acc, col * HEADS + head, col, view_col - col, i, base, first_row)
+            for d in range(SIZE):
+                key_ref[view_col, head * SIZE + d] = acc[0][d]
+                value_ref[view_col, pl.ds((CH + head * SIZE + d) * R, ROWS), :] = acc[1][d]
 
     def inner_columns(step, carry):
         key_columns(1 + step // HEADS, step % HEADS, (0, 1))
@@ -319,30 +324,34 @@
 
     def key_finish(col, carry):
         for source, target, row in ((grads, raws, 2), (halo_grads, halo_raws, edge_first)):
-            scale = k_inv[col, pl.ds(row, ROWS), :]
-            raw = unit_back(window(ks, col, row), scale, source[col, 0:CH])
-            target[col, 0 : CH * ROWS, :] = raw.reshape(CH * ROWS, PIX)
-            target[col, CH * ROWS :, :] = source[col, CH:].reshape(CH * ROWS, PIX)
+            scale = k_inv[col, pl.ds(row, ROWS), :] * SCALE
+            raw = unit_back(window(ks, col, row), scale, source[col])
+            for d in range(CH):
+                target[col, pl.ds(d * R, ROWS), :] = raw[d]
         return carry
 
     lax.fori_loop(0, 6, key_finish, 0)
 
     def key_sums(source, from_row, first):
         def one(row, acc):
-            for col, target in ((0, to_left), (2, own_raw), (4, to_right)):
-                raw = [
-                    source[col + j, pl.ds(row + from_row, 2 * CH, stride=ROWS), :].astype(BF16)
-                    for j in range(2)
-                ]
-                for j in range(2):
-                    target[row + first, j] = raw[j]
-                acc = acc + outer(pair(normed, row + first, col), jnp.concatenate(raw, axis=1))
-            return acc
+            raw = [view(source, col, row + from_row, 2 * CH) for col in range(6)]
+            for col in range(6):
+                (to_left, own_raw, to_right)[col // 2][row + first, col % 2] = raw[col]
+            normed_all = [normed[row + first, col] for col in range(6)]
+            return acc + outer(jnp.concatenate(normed_all, axis=1), jnp.concatenate(raw, axis=1))
 
         return one
 
     acc = lax.fori_loop(0, ROWS, key_sums(raws, 0, 0), jnp.zeros((CH, 2 * CH), F32))
     weight_sums[0:CH, :] = lax.fori_loop(0, 2, key_sums(halo_raws, edge_row, ROWS), acc)
+
+
+def row_kernel(own_raw, left_raw, right_raw, row_send):
+    for row in range(2):
+        for j in range(2):
+            row_send[row, j] = sum(
+                x[ROWS + row, j].astype(F32) for x in (own_raw, left_raw, right_raw)
+            ).astype(BF16)
 
 
 def features_kernel(
@@ -406,20 +415,33 @@
         out_specs=[VM] * len(outs),
         scratch_shapes=[pltpu.VMEM(x, F32) if isinstance(x, tuple) else x for x in scratch],
         input_output_aliases=dict(aliases),
-        compiler_params=pltpu.CompilerParams(vmem_limit_bytes=32 * 1024 * 1024),
+        compiler_params=pltpu.CompilerParams(vmem_limit_bytes=20 * 1024 * 1024),
         cost_estimate=pl.CostEstimate(flops=flops, bytes_accessed=1000000, transcendentals=0),
     )(*operands)
+
+
+def near_memory(x):
+    return pltpu.with_memory_space_constraint(x, pltpu.VMEM)
+
+
+def sum_kernel(shares, copies):
+    share = jnp.sum(shares[...].astype(F32), axis=0).astype(copies.dtype)
+    for k in range(copies.shape[0]):
+        copies[k] = share
 
 
 def sum_everywhere(values):
     near, far = ("px", "pc", "vrow"), ("py", "vcol")
     near_count, far_count = (math.prod(lax.axis_size(a) for a in axes) for axes in (near, far))
-    shares = lax.all_to_all(values.reshape(near_count, -1, PIX), near, 0, 0)
-    share = jnp.sum(shares, axis=0).astype(BF16)
-    copies = jnp.broadcast_to(share[None], (far_count,) + share.shape)
-    shares = lax.all_to_all(copies, far, 0, 0)
-    share = jnp.sum(shares.astype(F32), axis=0)
-    copies = jnp.broadcast_to(share[None], (near_count,) + share.shape)
+    size = values.size // (near_count * PIX)
+
+    def exchange(copies, axes):
+        return near_memory(lax.all_to_all(copies, axes, 0, 0))
+
+    shares = exchange(values.reshape(near_count, size, PIX), near)
+    (copies,) = call(sum_kernel, [((far_count, size, PIX), BF16)], [], 100000, shares)
+    shares = exchange(copies, far)
+    (copies,) = call(sum_kernel, [((near_count, size, PIX), F32)], [], 100000, shares)
     return lax.all_to_all(copies, near, 0, 0).reshape(values.shape)
 
 
@@ -473,7 +495,7 @@
         forward_kernel,
         [
             padded, padded, key_lanes, all_views, offsets, offsets,
-            ((COLS, CH * ROWS, PIX), F32), ((2, steps, ROWS, PIX), F32),
+            ((COLS, CH * R, PIX), F32), ((2, steps, ROWS, PIX), F32),
         ],
         [], 4000000,
         side, left, right, row_halo, left_corner, right_corner, gain_full, w_in, ogs, qs,
@@ -484,16 +506,18 @@
         gradient_kernel,
         [((2 * CH, PIX), F32), views, key_views, key_views, key_views],
         [
-            (steps, 25 * W, PIX), (steps, 25 * W, PIX), (6, 2 * CH, ROWS, PIX),
-            (6, 2 * CH * ROWS, PIX), (6, 2 * CH, ROWS, PIX), (6, 2 * CH * ROWS, PIX),
+            (steps, 25 * W, PIX), (steps, 25 * W, PIX), (6, CH, ROWS, PIX), (6, 2 * CH * R, PIX),
+            (6, CH, ROWS, PIX), (6, 2 * CH * R, PIX),
         ],
         5000000,
         side, qs, ks, ogs, q_inv, k_inv, normed, weights, prob_grads, attended, stats, cot,
     )
     sums = sum_everywhere(weight_sums)
-    right_raw = lax.ppermute(to_left, "vcol", down)
-    left_raw = lax.ppermute(to_right, "vcol", up)
-    row_send = sum(x[ROWS:].astype(F32) for x in (own_raw, left_raw, right_raw)).astype(BF16)
+    right_raw = lax.ppermute(pltpu.with_memory_space_constraint(to_left, pltpu.HBM), "vcol", down)
+    left_raw = lax.ppermute(pltpu.with_memory_space_constraint(to_right, pltpu.HBM), "vcol", up)
+    (row_send,) = call(
+        row_kernel, [((2, COLS, 2 * CH, PIX), BF16)], [], 10000, own_raw, left_raw, right_raw
+    )
     row_raw = lax.ppermute(row_send, "vrow", cross)
     (features_grad,) = call(
         features_kernel, [(features.shape, BF16)], [(ROWS, COLS, 2 * CH, PIX)], 2000000,

time: 97.8 us -> 96.8 us (0.990)
  waiting for transfers between devices: 9.3 us -> 8.02 us
  Pallas kernels: 22.9 us -> 23.9 us
    all_to_all x1, waiting for transfers between devices: 8.82 us -> 7.55 us  [exchange(): return near_memory(lax.all_to_all(copies, axes, 0, 0))]
    pallas_call x6 -> x9, Pallas kernels: 22.9 us -> 23.9 us  [call(): pl.pallas_call(kernel, out_shape=[jax.ShapeDtypeStruct(shape, dtype) for...]
  transfers between devices with their start and end apart: 9 -> 9, of which waited for: 2 -> 2; matrix products, arithmetic and copies ran while one was open for 1% -> 0% of each run, Pallas kernels for 5% -> 7%
where the time goes in v4:
time: 96.8 us; the launch traced here: 96.3 us
  starting transfers between devices  40.5 us (42%)
  Pallas kernels  23.9 us (25%)
  blocking collectives  23.1 us (24%)
  waiting for transfers between devices  8.02 us (8%)
    pallas_call x9, Pallas kernels, call(): pl.pallas_call(kernel, out_shape=[jax.ShapeDtypeStruct(shape, dtype) for...  23.9 us
    all_to_all x1, starting transfers between devices, exchange(): return near_memory(lax.all_to_all(copies, axes, 0, 0))  16.3 us
    all_to_all x1, blocking collectives, exchange(): return near_memory(lax.all_to_all(copies, axes, 0, 0))  12.8 us
    all_to_all x1, blocking collectives, sum_everywhere(): return lax.all_to_all(copies, near, 0, 0).reshape(values.shape)  10.2 us
    all_to_all x1, waiting for transfers between devices, exchange(): return near_memory(lax.all_to_all(copies, axes, 0, 0))  7.55 us
    ppermute x1, starting transfers between devices, layer(): left_corner = lax.ppermute(edge, grid, diag_up)  6.26 us
    ppermute x1, starting transfers between devices, layer(): left = lax.ppermute(features, 'vcol', up)  4.83 us
    ppermute x1, starting transfers between devices, layer(): lax.ppermute(pltpu.with_memory_space_constraint(to_right, pltpu.HBM), 'vc...  4.81 us
  transfers between devices with their start and end apart: 9, of which 2 were waited for; matrix products, arithmetic and copies ran while one was open for 0% of the time, Pallas kernels for 7%

profile of v4, /device:TPU:1, one launch (start us, length us, event | category | flops | bytes accessed | tf_op | source)
XLA Modules:
  0.0 96.3 jit_solution(6605058558744002723)
XLA Ops:
  0.6 4.8 %collective-permute-start = (bf16[8,2,64,128]{3,2,1,0:T(8,128)(2,1)}, bf16[8,2,64,128]{3,2,1,0:T(8,128)(2,1)S(1)}, u32[]{:S(2)}, u32[]{:S(2)}) collective-permute-start(bf16[8,2,64,128]{3,2,1,0:T(8,128)(2,1)} %feats.1), channel_id=1, source_target_pairs={{0,32},{32,64},{64,96},{96,128},{128,160},{160,192},{192,224},{1,3... | collective-permute-start | bytes 786440 | tf_op jit(solution)/shard_map/ppermute | solution.py:463
  5.5 1.3 %collective-permute-start.1 = (bf16[8,2,64,128]{3,2,1,0:T(8,128)(2,1)}, bf16[8,2,64,128]{3,2,1,0:T(8,128)(2,1)S(1)}, u32[]{:S(2)}, u32[]{:S(2)}) collective-permute-start(bf16[8,2,64,128]{3,2,1,0:T(8,128)(2,1)} %feats.1), channel_id=1, source_target_pairs={{32,0},{64,32},{96,64},{128,96},{160,128},{192,160},{224,192},{33,... | collective-permute-start | bytes 786440 | tf_op jit(solution)/shard_map/ppermute | solution.py:464
  6.8 0.9 shard_map.102
  7.6 1.3 %collective-permute-start.4 = (bf16[2,2,64,128]{3,2,1,0:T(8,128)(2,1)S(1)}, bf16[2,2,64,128]{3,2,1,0:T(8,128)(2,1)S(1)}, u32[]{:S(2)}, u32[]{:S(2)}) collective-permute-start(bf16[2,2,64,128]{3,2,1,0:T(8,128)(2,1)S(1)} %shard_map.102), channel_id=1, source_target_pairs={{32,256},{64,288},{96,320},{128,352},{160,384},{192,416},{224,448}... | collective-permute-start | bytes 196616 | tf_op jit(solution)/shard_map/ppermute | solution.py:471
  8.9 6.3 %collective-permute-start.3 = (bf16[2,2,64,128]{3,2,1,0:T(8,128)(2,1)S(1)}, bf16[2,2,64,128]{3,2,1,0:T(8,128)(2,1)S(1)}, u32[]{:S(2)}, u32[]{:S(2)}) collective-permute-start(bf16[2,2,64,128]{3,2,1,0:T(8,128)(2,1)S(1)} %shard_map.102), channel_id=1, source_target_pairs={{0,288},{32,320},{64,352},{96,384},{128,416},{160,448},{192,480},{... | collective-permute-start | bytes 196616 | tf_op jit(solution)/shard_map/ppermute | solution.py:470
  15.2 2.1 %collective-permute-start.2 = (bf16[2,2,64,128]{3,2,1,0:T(8,128)(2,1)S(1)}, bf16[2,2,64,128]{3,2,1,0:T(8,128)(2,1)S(1)}, u32[]{:S(2)}, u32[]{:S(2)}) collective-permute-start(bf16[2,2,64,128]{3,2,1,0:T(8,128)(2,1)S(1)} %shard_map.102), channel_id=1, source_target_pairs={{0,256},{256,0},{1,257},{257,1},{2,258},{258,2},{3,259},{259,3},{4... | collective-permute-start | bytes 196616 | tf_op jit(solution)/shard_map/ppermute | solution.py:469
  17.3 2.9 %shard_map.101 = (f32[2,832,128]{2,1,0:T(8,128)S(1)}, f32[6,832,128]{2,1,0:T(8,128)S(1)}, f32[6,832,128]{2,1,0:T(8,128)S(1)}, f32[2,832,128]{2,1,0:T(8,128)S(1)}...) custom-call(s32[1]{0:T(128)} %bitcast.side, ...), custom_call_target="tpu_custom_call" | custom-call | flops 2000000 | bytes 1000000 | tf_op jit(solution)/shard_map/pallas_call | solution.py:409
  20.2 0.0 collective-permute-done.4.right_corner
  20.2 0.0 collective-permute-done.3.left_corner
  20.2 0.5 collective-permute-done.2.row_halo
  20.7 0.0 collective-permute-done.left
  20.7 0.0 collective-permute-done.1.right
  20.7 5.6 %shard_map.103 = (f32[6,832,128]{2,1,0:T(8,128)S(1)}, f32[6,832,128]{2,1,0:T(8,128)S(1)}, f32[6,16,128]{2,1,0:T(8,128)S(1)}, bf16[10,6,64,128]{3,2,1,0:T(8,128)(...) custom-call(s32[1]{0:T(128)} %bitcast.side, ...), custom_call_target="tpu_custom_call", output_to_operand_aliasing={{0}: (10, {}), {1}: (11, {}), {2}: (12, {}), {3}: (13, {})} | custom-call | flops 4000000 | bytes 1000000 | tf_op jit(solution)/shard_map/pallas_call | solution.py:409
  26.3 8.2 %shard_map.104 = (f32[128,128]{1,0:T(8,128)S(1)}, bf16[8,2,64,128]{3,2,1,0:T(8,128)(2,1)S(1)}, bf16[10,2,128,128]{3,2,1,0:T(8,128)(2,1)S(1)}, bf16[10,2,128,128]...) custom-call(s32[1]{0:T(128)} %bitcast.side, f32[2,832,128]{2,1,0:T(8,128)S(1)} %get-tuple-element.36.qs, ...), custom_call_target="tpu_custom_call" | custom-call | flops 5000000 | bytes 1000000 | tf_op jit(solution)/shard_map/pallas_call | solution.py:409
  34.5 4.8 %collective-permute-start.5 = (bf16[10,2,128,128]{3,2,1,0:T(8,128)(2,1)S(1)}, bf16[10,2,128,128]{3,2,1,0:T(8,128)(2,1)}, u32[]{:S(2)}, u32[]{:S(2)}) collective-permute-start(bf16[10,2,128,128]{3,2,1,0:T(8,128)(2,1)S(1)} %get-tuple-element.54), channel_id=1, source_target_pairs={{0,32},{32,64},{64,96},{96,128},{128,160},{160,192},{192,224},{1,3... | collective-permute-start | bytes 1966088 | tf_op jit(solution)/shard_map/ppermute | solution.py:517
  39.3 1.3 %collective-permute-start.6 = (bf16[10,2,128,128]{3,2,1,0:T(8,128)(2,1)S(1)}, bf16[10,2,128,128]{3,2,1,0:T(8,128)(2,1)}, u32[]{:S(2)}, u32[]{:S(2)}) collective-permute-start(bf16[10,2,128,128]{3,2,1,0:T(8,128)(2,1)S(1)} %get-tuple-element.55), channel_id=1, source_target_pairs={{32,0},{64,32},{96,64},{128,96},{160,128},{192,160},{224,192},{33,... | collective-permute-start | bytes 1966088 | tf_op jit(solution)/shard_map/ppermute | solution.py:516
  40.6 12.8 %all_to_all.15.shares = f32[16,8,128]{2,1,0:T(8,128)S(1)} all-to-all(f32[16,8,128]{2,1,0:T(8,128)S(1)} %bitcast.6), channel_id=1, replica_groups=mesh['vrow'=2,'vcol'=8,'px'=4,'py'=4,'pc'=2] {'px','pc','vrow'}, dimensions={0} | all-to-all | bytes 131072 | tf_op jit(solution)/shard_map/all_to_all | solution.py:439
  53.4 0.7 shard_map.107
  54.1 16.3 %all-to-all-start.1 = ((bf16[32,8,128]{2,1,0:T(8,128)(2,1)}), bf16[32,8,128]{2,1,0:T(8,128)(2,1)S(1)}, u32[]{:S(2)}, u32[]{:S(2)}) async-start(bf16[32,8,128]{2,1,0:T(8,128)(2,1)} %shard_map.107), calls=%async_computation.1 | async-start | bytes 131072 | tf_op jit(solution)/shard_map/all_to_all | solution.py:439
  70.4 0.0 collective-permute-done.5.left_raw
  70.4 0.0 collective-permute-done.6.right_raw
  70.4 1.3 %shard_map.105 = bf16[2,2,128,128]{3,2,1,0:T(8,128)(2,1)S(1)} custom-call(bf16[10,2,128,128]{3,2,1,0:T(8,128)(2,1)S(1)} %get-tuple-element.53.own_raw, bf16[10,2,128,128]{3,2,1,0:T(8,128)(2,1)} %collective-permute-done.5.left_raw, bf16[10,2,128,128]{3,2,1,0:T(8,128)(2,1)} %collective-permute-done.6.right_raw), custom_call_target="tpu_custom_call" | custom-call | flops 10000 | bytes 1000000 | tf_op jit(solution)/shard_map/pallas_call | solution.py:409
  71.8 2.3 %collective-permute-start.7 = (bf16[2,2,128,128]{3,2,1,0:T(8,128)(2,1)S(1)}, bf16[2,2,128,128]{3,2,1,0:T(8,128)(2,1)S(1)}, u32[]{:S(2)}, u32[]{:S(2)}) collective-permute-start(bf16[2,2,128,128]{3,2,1,0:T(8,128)(2,1)S(1)} %shard_map.105), channel_id=1, source_target_pairs={{0,256},{256,0},{1,257},{257,1},{2,258},{258,2},{3,259},{259,3},{4... | collective-permute-start | bytes 393224 | tf_op jit(solution)/shard_map/ppermute | solution.py:521
  74.1 7.5 %all-to-all-done.1.shares = bf16[32,8,128]{2,1,0:T(8,128)(2,1)S(1)} async-done(((bf16[32,8,128]{2,1,0:T(8,128)(2,1)}), bf16[32,8,128]{2,1,0:T(8,128)(2,1)S(1)}, u32[]{:S(2)}, u32[]{:S(2)}) %all-to-all-start.1) | async-done | bytes 65568 | tf_op jit(solution)/shard_map/all_to_all | solution.py:439
  81.7 10.2 %all_to_all.16 = f32[16,8,128]{2,1,0:T(8,128)S(1)} all-to-all(f32[16,8,128]{2,1,0:T(8,128)S(1)} %shard_map.108), channel_id=1, replica_groups=mesh['vrow'=2,'vcol'=8,'px'=4,'py'=4,'pc'=2] {'px','pc','vrow'}, dimensions={0} | all-to-all | bytes 131072 | tf_op jit(solution)/shard_map/all_to_all | solution.py:445
  91.9 0.7 shard_map.109
  92.7 0.0 collective-permute-done.7.row_raw
  92.7 3.6 %shard_map.106 = bf16[8,2,64,128]{3,2,1,0:T(8,128)(2,1)} custom-call(s32[1]{0:T(128)} %bitcast.side, bf16[10,2,128,128]{3,2,1,0:T(8,128)(2,1)S(1)} %get-tuple-element.53.own_raw, bf16[10,2,128,128]{3,2,1,0:T(8,128)(2,1)} %collective-permute-done.5.left_raw, bf16[10,2,128,128]{3,2,1,0:T(8,128)(2,1)} %collective-permute-done.6.right_raw, ...), custom_call_target="tpu_custom_call" | custom-call | flops 2000000 | bytes 1000000 | tf_op jit(solution)/shard_map/pallas_call | solution.py:409
  (1 shorter events, 0.0 us)
Async XLA Ops:
  0.6 20.1 %collective-permute-start = (bf16[8,2,64,128]{3,2,1,0:T(8,128)(2,1)}, bf16[8,2,64,128]{3,2,1,0:T(8,128)(2,1)S(1)}, u32[]{:S(2)}, u32[]{:S(2)}) collective-permute-start(bf16[8,2,64,128]{3,2,1,0:T(8,128)(2,1)} %feats.1), channel_id=1, source_target_pairs={{0,32},{32,64},{64,96},{96,128},{128,160},{160,192},{192,224},{1,3... | collective-permute-start | bytes 786440 | tf_op jit(solution)/shard_map/ppermute | solution.py:463
  5.5 15.2 %collective-permute-start.1 = (bf16[8,2,64,128]{3,2,1,0:T(8,128)(2,1)}, bf16[8,2,64,128]{3,2,1,0:T(8,128)(2,1)S(1)}, u32[]{:S(2)}, u32[]{:S(2)}) collective-permute-start(bf16[8,2,64,128]{3,2,1,0:T(8,128)(2,1)} %feats.1), channel_id=1, source_target_pairs={{32,0},{64,32},{96,64},{128,96},{160,128},{192,160},{224,192},{33,... | collective-permute-start | bytes 786440 | tf_op jit(solution)/shard_map/ppermute | solution.py:464
  7.6 12.6 %collective-permute-start.4 = (bf16[2,2,64,128]{3,2,1,0:T(8,128)(2,1)S(1)}, bf16[2,2,64,128]{3,2,1,0:T(8,128)(2,1)S(1)}, u32[]{:S(2)}, u32[]{:S(2)}) collective-permute-start(bf16[2,2,64,128]{3,2,1,0:T(8,128)(2,1)S(1)} %shard_map.102), channel_id=1, source_target_pairs={{32,256},{64,288},{96,320},{128,352},{160,384},{192,416},{224,448}... | collective-permute-start | bytes 196616 | tf_op jit(solution)/shard_map/ppermute | solution.py:471
  8.9 11.3 %collective-permute-start.3 = (bf16[2,2,64,128]{3,2,1,0:T(8,128)(2,1)S(1)}, bf16[2,2,64,128]{3,2,1,0:T(8,128)(2,1)S(1)}, u32[]{:S(2)}, u32[]{:S(2)}) collective-permute-start(bf16[2,2,64,128]{3,2,1,0:T(8,128)(2,1)S(1)} %shard_map.102), channel_id=1, source_target_pairs={{0,288},{32,320},{64,352},{96,384},{128,416},{160,448},{192,480},{... | collective-permute-start | bytes 196616 | tf_op jit(solution)/shard_map/ppermute | solution.py:470
  15.2 5.5 %collective-permute-start.2 = (bf16[2,2,64,128]{3,2,1,0:T(8,128)(2,1)S(1)}, bf16[2,2,64,128]{3,2,1,0:T(8,128)(2,1)S(1)}, u32[]{:S(2)}, u32[]{:S(2)}) collective-permute-start(bf16[2,2,64,128]{3,2,1,0:T(8,128)(2,1)S(1)} %shard_map.102), channel_id=1, source_target_pairs={{0,256},{256,0},{1,257},{257,1},{2,258},{258,2},{3,259},{259,3},{4... | collective-permute-start | bytes 196616 | tf_op jit(solution)/shard_map/ppermute | solution.py:469
  34.5 35.9 %collective-permute-start.5 = (bf16[10,2,128,128]{3,2,1,0:T(8,128)(2,1)S(1)}, bf16[10,2,128,128]{3,2,1,0:T(8,128)(2,1)}, u32[]{:S(2)}, u32[]{:S(2)}) collective-permute-start(bf16[10,2,128,128]{3,2,1,0:T(8,128)(2,1)S(1)} %get-tuple-element.54), channel_id=1, source_target_pairs={{0,32},{32,64},{64,96},{96,128},{128,160},{160,192},{192,224},{1,3... | collective-permute-start | bytes 1966088 | tf_op jit(solution)/shard_map/ppermute | solution.py:517
  39.3 31.1 %collective-permute-start.6 = (bf16[10,2,128,128]{3,2,1,0:T(8,128)(2,1)S(1)}, bf16[10,2,128,128]{3,2,1,0:T(8,128)(2,1)}, u32[]{:S(2)}, u32[]{:S(2)}) collective-permute-start(bf16[10,2,128,128]{3,2,1,0:T(8,128)(2,1)S(1)} %get-tuple-element.55), channel_id=1, source_target_pairs={{32,0},{64,32},{96,64},{128,96},{160,128},{192,160},{224,192},{33,... | collective-permute-start | bytes 1966088 | tf_op jit(solution)/shard_map/ppermute | solution.py:516
  54.1 27.6 %all-to-all-start.1 = ((bf16[32,8,128]{2,1,0:T(8,128)(2,1)}), bf16[32,8,128]{2,1,0:T(8,128)(2,1)S(1)}, u32[]{:S(2)}, u32[]{:S(2)}) async-start(bf16[32,8,128]{2,1,0:T(8,128)(2,1)} %shard_map.107), calls=%async_computation.1 | async-start | bytes 131072 | tf_op jit(solution)/shard_map/all_to_all | solution.py:439
  71.8 20.9 %collective-permute-start.7 = (bf16[2,2,128,128]{3,2,1,0:T(8,128)(2,1)S(1)}, bf16[2,2,128,128]{3,2,1,0:T(8,128)(2,1)S(1)}, u32[]{:S(2)}, u32[]{:S(2)}) collective-permute-start(bf16[2,2,128,128]{3,2,1,0:T(8,128)(2,1)S(1)} %shard_map.105), channel_id=1, source_target_pairs={{0,256},{256,0},{1,257},{257,1},{2,258},{258,2},{3,259},{259,3},{4... | collective-permute-start | bytes 393224 | tf_op jit(solution)/shard_map/ppermute | solution.py:521

commit v5 on v4

--- a/solution.py
+++ b/solution.py
@@ -64,8 +64,13 @@
 
 
 def halo_start(side_ref):
-    side = side_ref[0]
+    side = jnp.right_shift(side_ref[0], 1)
     return 10 - 10 * side, 10 * side, 6 - 6 * side
+
+
+def partner_cols(side_ref):
+    odd = jnp.bitwise_and(side_ref[0], 1)
+    return 4 - 4 * odd, 4 * odd
 
 
 def clear_rows(refs, row):
@@ -152,31 +157,32 @@
 
 
 def forward_kernel(
-    side, left, right, row_halo, left_corner, right_corner, gain, w_in, ogs, qs,
+    side, first, second, row_halo, first_corner, second_corner, gain, w_in, ogs, qs,
     ks_in, vs_in, k_inv_in, normed_in,
     ks, vs, k_inv, normed, weights, prob_grads, attended, stats,
 ):
     halo_row, _, _ = halo_start(side)
+    first_col, second_col = partner_cols(side)
     gain_full = gain[...]
     w_keys = w_in[CH:, :]
 
-    def piece(ref, offset, first, col):
+    def piece(ref, offset, to_row, col):
         def one(row):
             views = normed_views(ref, row, gain_full)
             both = jnp.dot(w_keys, jnp.concatenate(views, axis=1), preferred_element_type=F32)
             for j in range(2):
-                normed[row + first, col + j] = views[j]
+                normed[row + to_row, col + j] = views[j]
                 project_keys(both[:, j * PIX : (j + 1) * PIX], row + offset, col, j, ks, vs, k_inv)
 
         return one
 
-    each_row(ROWS, (piece(left, 2, 0, 0), piece(right, 2, 0, 4)))
+    each_row(ROWS, (piece(first, 2, 0, first_col), piece(second, 2, 0, second_col)))
     each_row(
         2,
         (
             piece(row_halo, halo_row, ROWS, 2),
-            piece(left_corner, halo_row, ROWS, 0),
-            piece(right_corner, halo_row, ROWS, 4),
+            piece(first_corner, halo_row, ROWS, first_col),
+            piece(second_corner, halo_row, ROWS, second_col),
         ),
     )
 
@@ -228,10 +234,11 @@
 
 def gradient_kernel(
     side, qs, ks, ogs, q_inv, k_inv, normed, weights, prob_grads, attended, stats, cot,
-    weight_sums, raw_query, to_left, to_right, own_raw,
+    weight_sums, raw_query, to_first, to_second, own_raw,
     probs, score_grads, grads, raws, halo_grads, halo_raws,
 ):
     _, _, edge_row = halo_start(side)
+    first_col, second_col = partner_cols(side)
     zeros = jnp.zeros((ROWS, PIX), F32)
     pads = jnp.zeros((25, PIX), F32)
 
@@ -334,10 +341,12 @@
 
     def key_sums(source, from_row, first):
         def one(row, acc):
-            raw = [view(source, col, row + from_row, 2 * CH) for col in range(6)]
-            for col in range(6):
-                (to_left, own_raw, to_right)[col // 2][row + first, col % 2] = raw[col]
-            normed_all = [normed[row + first, col] for col in range(6)]
+            raw, normed_all = [], []
+            for target, col in ((to_first, first_col), (own_raw, 2), (to_second, second_col)):
+                for j in range(2):
+                    raw.append(view(source, col + j, row + from_row, 2 * CH))
+                    target[row + first, j] = raw[-1]
+                    normed_all.append(normed[row + first, col + j])
             return acc + outer(jnp.concatenate(normed_all, axis=1), jnp.concatenate(raw, axis=1))
 
         return one
@@ -346,16 +355,16 @@
     weight_sums[0:CH, :] = lax.fori_loop(0, 2, key_sums(halo_raws, edge_row, ROWS), acc)
 
 
-def row_kernel(own_raw, left_raw, right_raw, row_send):
+def row_kernel(own_raw, first_raw, second_raw, row_send):
     for row in range(2):
         for j in range(2):
             row_send[row, j] = sum(
-                x[ROWS + row, j].astype(F32) for x in (own_raw, left_raw, right_raw)
+                x[ROWS + row, j].astype(F32) for x in (own_raw, first_raw, second_raw)
             ).astype(BF16)
 
 
 def features_kernel(
-    side, own_raw, left_raw, right_raw, row_raw, raw_query, feats, cot, gain, w_back,
+    side, own_raw, first_raw, second_raw, row_raw, raw_query, feats, cot, gain, w_back,
     feats_grad, shared,
 ):
     _, _, edge_row = halo_start(side)
@@ -363,8 +372,8 @@
     def join(row):
         for j in range(2):
             shared[row, j] = (
-                own_raw[row, j].astype(F32) + left_raw[row, j].astype(F32)
-                + right_raw[row, j].astype(F32)
+                own_raw[row, j].astype(F32) + first_raw[row, j].astype(F32)
+                + second_raw[row, j].astype(F32)
             )
 
     def join_edge(row):
@@ -446,29 +455,36 @@
 
 
 def layer(features, out_cotangent, norm_gain, query_proj, keyval_proj, output_proj):
-    side = lax.axis_index("vrow").astype(jnp.int32).reshape(1)
+    place = lax.axis_index("vrow") * 2 + jnp.bitwise_and(lax.axis_index("vcol"), 1)
+    side = place.astype(jnp.int32).reshape(1)
     cols = lax.axis_size("vcol")
-    up = [(i, i + 1) for i in range(cols - 1)]
-    down = [(j, i) for i, j in up]
-    cross = [(0, 1), (1, 0)]
-    diag_up = [(a * cols + i, b * cols + j) for a, b in cross for i, j in up]
-    diag_down = [(a * cols + i, b * cols + j) for a, b in cross for i, j in down]
     grid = ("vrow", "vcol")
+
+    def both_ways(pairs):
+        return [*pairs, *((b, a) for a, b in pairs)]
+
+    rounds = [[(i, i + 1) for i in range(start, cols - 1, 2)] for start in (0, 1)]
+    first_swap, second_swap = (both_ways(pairs) for pairs in rounds)
+    first_cross, second_cross = (
+        [(a * cols + i, (1 - a) * cols + j) for a in (0, 1) for i, j in swap]
+        for swap in (first_swap, second_swap)
+    )
+    row_swap = both_ways([(0, 1)])
     gain = norm_gain.reshape(1, CH)
     held = [
         pltpu.with_memory_space_constraint(x, pltpu.HBM)
         for x in (features, out_cotangent, gain, query_proj, keyval_proj, output_proj)
     ]
 
-    left = lax.ppermute(features, "vcol", up)
-    right = lax.ppermute(features, "vcol", down)
+    first = lax.ppermute(features, "vcol", first_swap)
+    second = lax.ppermute(features, "vcol", second_swap)
     (edge,) = call(
         edge_kernel, [((2, COLS, CH, PIX), BF16)], [pltpu.SemaphoreType.DMA], 1000, side, held[0],
         far=(1,),
     )
-    row_halo = lax.ppermute(edge, "vrow", cross)
-    left_corner = lax.ppermute(edge, grid, diag_up)
-    right_corner = lax.ppermute(edge, grid, diag_down)
+    row_halo = lax.ppermute(edge, "vrow", row_swap)
+    first_corner = lax.ppermute(edge, grid, first_cross)
+    second_corner = lax.ppermute(edge, grid, second_cross)
 
     own = ((COLS, CH * S, PIX), F32)
     padded = ((6, CH * S, PIX), F32)
@@ -498,11 +514,11 @@
             ((COLS, CH * R, PIX), F32), ((2, steps, ROWS, PIX), F32),
         ],
         [], 4000000,
-        side, left, right, row_halo, left_corner, right_corner, gain_full, w_in, ogs, qs,
+        side, first, second, row_halo, first_corner, second_corner, gain_full, w_in, ogs, qs,
         ks, vs, k_inv, normed,
         aliases=((10, 0), (11, 1), (12, 2), (13, 3)),
     )
-    weight_sums, raw_query, to_left, to_right, own_raw = call(
+    weight_sums, raw_query, to_first, to_second, own_raw = call(
         gradient_kernel,
         [((2 * CH, PIX), F32), views, key_views, key_views, key_views],
         [
@@ -513,15 +529,17 @@
         side, qs, ks, ogs, q_inv, k_inv, normed, weights, prob_grads, attended, stats, cot,
     )
     sums = sum_everywhere(weight_sums)
-    right_raw = lax.ppermute(pltpu.with_memory_space_constraint(to_left, pltpu.HBM), "vcol", down)
-    left_raw = lax.ppermute(pltpu.with_memory_space_constraint(to_right, pltpu.HBM), "vcol", up)
+    first_raw, second_raw = (
+        lax.ppermute(pltpu.with_memory_space_constraint(x, pltpu.HBM), "vcol", swap)
+        for x, swap in ((to_first, first_swap), (to_second, second_swap))
+    )
     (row_send,) = call(
-        row_kernel, [((2, COLS, 2 * CH, PIX), BF16)], [], 10000, own_raw, left_raw, right_raw
-    )
-    row_raw = lax.ppermute(row_send, "vrow", cross)
+        row_kernel, [((2, COLS, 2 * CH, PIX), BF16)], [], 10000, own_raw, first_raw, second_raw
+    )
+    row_raw = lax.ppermute(row_send, "vrow", row_swap)
     (features_grad,) = call(
         features_kernel, [(features.shape, BF16)], [(ROWS, COLS, 2 * CH, PIX)], 2000000,
-        side, own_raw, left_raw, right_raw, row_raw, raw_query, feats, cot, gain_full, w_back,
+        side, own_raw, first_raw, second_raw, row_raw, raw_query, feats, cot, gain_full, w_back,
     )
     tokens_all = ROWS * COLS * PIX * math.prod(lax.axis_size(a) for a in AXES)
     query_grad, keyval_grad, output_grad, gain_grad = call(

time: 96.8 us -> 95.6 us (0.988)
  transfers between devices with their start and end apart: 9 -> 9, of which waited for: 2 -> 1; matrix products, arithmetic and copies ran while one was open for 0% -> 0% of each run, Pallas kernels for 7% -> 7%
where the time goes in v5:
time: 95.6 us; the launch traced here: 95.1 us
  starting transfers between devices  40 us (42%)
  Pallas kernels  24 us (25%)
  blocking collectives  22.8 us (24%)
  waiting for transfers between devices  7.57 us (8%)
    pallas_call x9, Pallas kernels, call(): pl.pallas_call(kernel, out_shape=[jax.ShapeDtypeStruct(shape, dtype) for...  24 us
    all_to_all x1, starting transfers between devices, exchange(): return near_memory(lax.all_to_all(copies, axes, 0, 0))  15.4 us
    all_to_all x1, blocking collectives, exchange(): return near_memory(lax.all_to_all(copies, axes, 0, 0))  12.5 us
    all_to_all x1, blocking collectives, sum_everywhere(): return lax.all_to_all(copies, near, 0, 0).reshape(values.shape)  10.2 us
    ppermute x1, starting transfers between devices, layer(): first_corner = lax.ppermute(edge, grid, first_cross)  9.59 us
    all_to_all x1, waiting for transfers between devices, exchange(): return near_memory(lax.all_to_all(copies, axes, 0, 0))  7.55 us
    ppermute x1, starting transfers between devices, layer(): first = lax.ppermute(features, 'vcol', first_swap)  4.82 us
    ppermute x2, starting transfers between devices, layer(): lax.ppermute(pltpu.with_memory_space_constraint(x, pltpu.HBM), 'vcol', swap)  3.45 us
  transfers between devices with their start and end apart: 9, of which 1 were waited for; matrix products, arithmetic and copies ran while one was open for 0% of the time, Pallas kernels for 7%

profile of v5, /device:TPU:1, one launch (start us, length us, event | category | flops | bytes accessed | tf_op | source)
XLA Modules:
  0.0 95.1 jit_solution(429710156727797819)
XLA Ops:
  0.6 4.8 %collective-permute-start = (bf16[8,2,64,128]{3,2,1,0:T(8,128)(2,1)}, bf16[8,2,64,128]{3,2,1,0:T(8,128)(2,1)S(1)}, u32[]{:S(2)}, u32[]{:S(2)}) collective-permute-start(bf16[8,2,64,128]{3,2,1,0:T(8,128)(2,1)} %feats.1), channel_id=1, source_target_pairs={{0,32},{64,96},{128,160},{192,224},{32,0},{96,64},{160,128},{224,1... | collective-permute-start | bytes 786440 | tf_op jit(solution)/shard_map/ppermute | solution.py:479
  5.5 0.7 collective-permute-start.1
  6.2 0.9 shard_map.102
  7.0 0.7 collective-permute-start.4
  7.7 9.6 %collective-permute-start.3 = (bf16[2,2,64,128]{3,2,1,0:T(8,128)(2,1)S(1)}, bf16[2,2,64,128]{3,2,1,0:T(8,128)(2,1)S(1)}, u32[]{:S(2)}, u32[]{:S(2)}) collective-permute-start(bf16[2,2,64,128]{3,2,1,0:T(8,128)(2,1)S(1)} %shard_map.102), channel_id=1, source_target_pairs={{0,288},{64,352},{128,416},{192,480},{32,256},{96,320},{160,384},{... | collective-permute-start | bytes 196616 | tf_op jit(solution)/shard_map/ppermute | solution.py:486
  17.3 3.1 %collective-permute-start.2 = (bf16[2,2,64,128]{3,2,1,0:T(8,128)(2,1)S(1)}, bf16[2,2,64,128]{3,2,1,0:T(8,128)(2,1)S(1)}, u32[]{:S(2)}, u32[]{:S(2)}) collective-permute-start(bf16[2,2,64,128]{3,2,1,0:T(8,128)(2,1)S(1)} %shard_map.102), channel_id=1, source_target_pairs={{0,256},{256,0},{1,257},{257,1},{2,258},{258,2},{3,259},{259,3},{4... | collective-permute-start | bytes 196616 | tf_op jit(solution)/shard_map/ppermute | solution.py:485
  20.4 2.9 %shard_map.101 = (f32[2,832,128]{2,1,0:T(8,128)S(1)}, f32[6,832,128]{2,1,0:T(8,128)S(1)}, f32[6,832,128]{2,1,0:T(8,128)S(1)}, f32[2,832,128]{2,1,0:T(8,128)S(1)}...) custom-call(s32[1]{0:T(128)} %bitcast.side, ...), custom_call_target="tpu_custom_call" | custom-call | flops 2000000 | bytes 1000000 | tf_op jit(solution)/shard_map/pallas_call | solution.py:418
  23.3 0.0 collective-permute-done.4.second_corner
  23.3 0.0 collective-permute-done.3.first_corner
  23.3 0.0 collective-permute-done.2.row_halo
  23.3 0.0 collective-permute-done.first
  23.4 0.0 collective-permute-done.1.second
  23.4 5.6 %shard_map.103 = (f32[6,832,128]{2,1,0:T(8,128)S(1)}, f32[6,832,128]{2,1,0:T(8,128)S(1)}, f32[6,16,128]{2,1,0:T(8,128)S(1)}, bf16[10,6,64,128]{3,2,1,0:T(8,128)(...) custom-call(s32[1]{0:T(128)} %bitcast.side, ...), custom_call_target="tpu_custom_call", output_to_operand_aliasing={{0}: (10, {}), {1}: (11, {}), {2}: (12, {}), {3}: (13, {})} | custom-call | flops 4000000 | bytes 1000000 | tf_op jit(solution)/shard_map/pallas_call | solution.py:418
  29.0 8.2 %shard_map.104 = (f32[128,128]{1,0:T(8,128)S(1)}, bf16[8,2,64,128]{3,2,1,0:T(8,128)(2,1)S(1)}, bf16[10,2,128,128]{3,2,1,0:T(8,128)(2,1)S(1)}, bf16[10,2,128,128]...) custom-call(s32[1]{0:T(128)} %bitcast.side, f32[2,832,128]{2,1,0:T(8,128)S(1)} %get-tuple-element.36.qs, ...), custom_call_target="tpu_custom_call" | custom-call | flops 5000000 | bytes 1000000 | tf_op jit(solution)/shard_map/pallas_call | solution.py:418
  37.2 1.9 %collective-permute-start.5 = (bf16[10,2,128,128]{3,2,1,0:T(8,128)(2,1)S(1)}, bf16[10,2,128,128]{3,2,1,0:T(8,128)(2,1)}, u32[]{:S(2)}, u32[]{:S(2)}) collective-permute-start(bf16[10,2,128,128]{3,2,1,0:T(8,128)(2,1)S(1)} %get-tuple-element.54), channel_id=1, source_target_pairs={{0,32},{64,96},{128,160},{192,224},{32,0},{96,64},{160,128},{224,1... | collective-permute-start | bytes 1966088 | tf_op jit(solution)/shard_map/ppermute | solution.py:533
  39.1 1.5 %collective-permute-start.6 = (bf16[10,2,128,128]{3,2,1,0:T(8,128)(2,1)S(1)}, bf16[10,2,128,128]{3,2,1,0:T(8,128)(2,1)}, u32[]{:S(2)}, u32[]{:S(2)}) collective-permute-start(bf16[10,2,128,128]{3,2,1,0:T(8,128)(2,1)S(1)} %get-tuple-element.55), channel_id=1, source_target_pairs={{32,64},{96,128},{160,192},{64,32},{128,96},{192,160},{33,65},{97,... | collective-permute-start | bytes 1966088 | tf_op jit(solution)/shard_map/ppermute | solution.py:533
  40.7 12.5 %all_to_all.15.shares = f32[16,8,128]{2,1,0:T(8,128)S(1)} all-to-all(f32[16,8,128]{2,1,0:T(8,128)S(1)} %bitcast.6), channel_id=1, replica_groups=mesh['vrow'=2,'vcol'=8,'px'=4,'py'=4,'pc'=2] {'px','pc','vrow'}, dimensions={0} | all-to-all | bytes 131072 | tf_op jit(solution)/shard_map/all_to_all | solution.py:448
  53.2 0.7 shard_map.107
  53.8 15.4 %all-to-all-start.1 = ((bf16[32,8,128]{2,1,0:T(8,128)(2,1)}), bf16[32,8,128]{2,1,0:T(8,128)(2,1)S(1)}, u32[]{:S(2)}, u32[]{:S(2)}) async-start(bf16[32,8,128]{2,1,0:T(8,128)(2,1)} %shard_map.107), calls=%async_computation.1 | async-start | bytes 131072 | tf_op jit(solution)/shard_map/all_to_all | solution.py:448
  69.3 0.0 collective-permute-done.5.first_raw
  69.3 0.0 collective-permute-done.6.second_raw
  69.3 1.3 %shard_map.105 = bf16[2,2,128,128]{3,2,1,0:T(8,128)(2,1)S(1)} custom-call(bf16[10,2,128,128]{3,2,1,0:T(8,128)(2,1)S(1)} %get-tuple-element.53.own_raw, bf16[10,2,128,128]{3,2,1,0:T(8,128)(2,1)} %collective-permute-done.5.first_raw, bf16[10,2,128,128]{3,2,1,0:T(8,128)(2,1)} %collective-permute-done.6.second_raw), custom_call_target="tpu_custom_call" | custom-call | flops 10000 | bytes 1000000 | tf_op jit(solution)/shard_map/pallas_call | solution.py:418
  70.6 2.3 %collective-permute-start.7 = (bf16[2,2,128,128]{3,2,1,0:T(8,128)(2,1)S(1)}, bf16[2,2,128,128]{3,2,1,0:T(8,128)(2,1)S(1)}, u32[]{:S(2)}, u32[]{:S(2)}) collective-permute-start(bf16[2,2,128,128]{3,2,1,0:T(8,128)(2,1)S(1)} %shard_map.105), channel_id=1, source_target_pairs={{0,256},{256,0},{1,257},{257,1},{2,258},{258,2},{3,259},{259,3},{4... | collective-permute-start | bytes 393224 | tf_op jit(solution)/shard_map/ppermute | solution.py:539
  72.9 7.5 %all-to-all-done.1.shares = bf16[32,8,128]{2,1,0:T(8,128)(2,1)S(1)} async-done(((bf16[32,8,128]{2,1,0:T(8,128)(2,1)}), bf16[32,8,128]{2,1,0:T(8,128)(2,1)S(1)}, u32[]{:S(2)}, u32[]{:S(2)}) %all-to-all-start.1) | async-done | bytes 65568 | tf_op jit(solution)/shard_map/all_to_all | solution.py:448
  80.5 10.2 %all_to_all.16 = f32[16,8,128]{2,1,0:T(8,128)S(1)} all-to-all(f32[16,8,128]{2,1,0:T(8,128)S(1)} %shard_map.108), channel_id=1, replica_groups=mesh['vrow'=2,'vcol'=8,'px'=4,'py'=4,'pc'=2] {'px','pc','vrow'}, dimensions={0} | all-to-all | bytes 131072 | tf_op jit(solution)/shard_map/all_to_all | solution.py:454
  90.8 0.7 shard_map.109
  91.5 0.0 collective-permute-done.7.row_raw
  91.5 3.6 %shard_map.106 = bf16[8,2,64,128]{3,2,1,0:T(8,128)(2,1)} custom-call(s32[1]{0:T(128)} %bitcast.side, bf16[10,2,128,128]{3,2,1,0:T(8,128)(2,1)S(1)} %get-tuple-element.53.own_raw, bf16[10,2,128,128]{3,2,1,0:T(8,128)(2,1)} %collective-permute-done.5.first_raw, bf16[10,2,128,128]{3,2,1,0:T(8,128)(2,1)} %collective-permute-done.6.second_raw, ...), custom_call_target="tpu_custom_call" | custom-call | flops 2000000 | bytes 1000000 | tf_op jit(solution)/shard_map/pallas_call | solution.py:418
  (1 shorter events, 0.0 us)
Async XLA Ops:
  0.6 22.7 %collective-permute-start = (bf16[8,2,64,128]{3,2,1,0:T(8,128)(2,1)}, bf16[8,2,64,128]{3,2,1,0:T(8,128)(2,1)S(1)}, u32[]{:S(2)}, u32[]{:S(2)}) collective-permute-start(bf16[8,2,64,128]{3,2,1,0:T(8,128)(2,1)} %feats.1), channel_id=1, source_target_pairs={{0,32},{64,96},{128,160},{192,224},{32,0},{96,64},{160,128},{224,1... | collective-permute-start | bytes 786440 | tf_op jit(solution)/shard_map/ppermute | solution.py:479
  5.5 17.9 %collective-permute-start.1 = (bf16[8,2,64,128]{3,2,1,0:T(8,128)(2,1)}, bf16[8,2,64,128]{3,2,1,0:T(8,128)(2,1)S(1)}, u32[]{:S(2)}, u32[]{:S(2)}) collective-permute-start(bf16[8,2,64,128]{3,2,1,0:T(8,128)(2,1)} %feats.1), channel_id=1, source_target_pairs={{32,64},{96,128},{160,192},{64,32},{128,96},{192,160},{33,65},{97,... | collective-permute-start | bytes 786440 | tf_op jit(solution)/shard_map/ppermute | solution.py:480
  7.0 16.3 %collective-permute-start.4 = (bf16[2,2,64,128]{3,2,1,0:T(8,128)(2,1)S(1)}, bf16[2,2,64,128]{3,2,1,0:T(8,128)(2,1)S(1)}, u32[]{:S(2)}, u32[]{:S(2)}) collective-permute-start(bf16[2,2,64,128]{3,2,1,0:T(8,128)(2,1)S(1)} %shard_map.102), channel_id=1, source_target_pairs={{32,320},{96,384},{160,448},{64,288},{128,352},{192,416},{288,64},... | collective-permute-start | bytes 196616 | tf_op jit(solution)/shard_map/ppermute | solution.py:487
  7.7 15.6 %collective-permute-start.3 = (bf16[2,2,64,128]{3,2,1,0:T(8,128)(2,1)S(1)}, bf16[2,2,64,128]{3,2,1,0:T(8,128)(2,1)S(1)}, u32[]{:S(2)}, u32[]{:S(2)}) collective-permute-start(bf16[2,2,64,128]{3,2,1,0:T(8,128)(2,1)S(1)} %shard_map.102), channel_id=1, source_target_pairs={{0,288},{64,352},{128,416},{192,480},{32,256},{96,320},{160,384},{... | collective-permute-start | bytes 196616 | tf_op jit(solution)/shard_map/ppermute | solution.py:486
  17.3 6.0 %collective-permute-start.2 = (bf16[2,2,64,128]{3,2,1,0:T(8,128)(2,1)S(1)}, bf16[2,2,64,128]{3,2,1,0:T(8,128)(2,1)S(1)}, u32[]{:S(2)}, u32[]{:S(2)}) collective-permute-start(bf16[2,2,64,128]{3,2,1,0:T(8,128)(2,1)S(1)} %shard_map.102), channel_id=1, source_target_pairs={{0,256},{256,0},{1,257},{257,1},{2,258},{258,2},{3,259},{259,3},{4... | collective-permute-start | bytes 196616 | tf_op jit(solution)/shard_map/ppermute | solution.py:485
  37.2 32.1 %collective-permute-start.5 = (bf16[10,2,128,128]{3,2,1,0:T(8,128)(2,1)S(1)}, bf16[10,2,128,128]{3,2,1,0:T(8,128)(2,1)}, u32[]{:S(2)}, u32[]{:S(2)}) collective-permute-start(bf16[10,2,128,128]{3,2,1,0:T(8,128)(2,1)S(1)} %get-tuple-element.54), channel_id=1, source_target_pairs={{0,32},{64,96},{128,160},{192,224},{32,0},{96,64},{160,128},{224,1... | collective-permute-start | bytes 1966088 | tf_op jit(solution)/shard_map/ppermute | solution.py:533
  39.1 30.1 %collective-permute-start.6 = (bf16[10,2,128,128]{3,2,1,0:T(8,128)(2,1)S(1)}, bf16[10,2,128,128]{3,2,1,0:T(8,128)(2,1)}, u32[]{:S(2)}, u32[]{:S(2)}) collective-permute-start(bf16[10,2,128,128]{3,2,1,0:T(8,128)(2,1)S(1)} %get-tuple-element.55), channel_id=1, source_target_pairs={{32,64},{96,128},{160,192},{64,32},{128,96},{192,160},{33,65},{97,... | collective-permute-start | bytes 1966088 | tf_op jit(solution)/shard_map/ppermute | solution.py:533
  53.8 26.6 %all-to-all-start.1 = ((bf16[32,8,128]{2,1,0:T(8,128)(2,1)}), bf16[32,8,128]{2,1,0:T(8,128)(2,1)S(1)}, u32[]{:S(2)}, u32[]{:S(2)}) async-start(bf16[32,8,128]{2,1,0:T(8,128)(2,1)} %shard_map.107), calls=%async_computation.1 | async-start | bytes 131072 | tf_op jit(solution)/shard_map/all_to_all | solution.py:448
  70.6 20.9 %collective-permute-start.7 = (bf16[2,2,128,128]{3,2,1,0:T(8,128)(2,1)S(1)}, bf16[2,2,128,128]{3,2,1,0:T(8,128)(2,1)S(1)}, u32[]{:S(2)}, u32[]{:S(2)}) collective-permute-start(bf16[2,2,128,128]{3,2,1,0:T(8,128)(2,1)S(1)} %shard_map.105), channel_id=1, source_target_pairs={{0,256},{256,0},{1,257},{257,1},{2,258},{258,2},{3,259},{259,3},{4... | collective-permute-start | bytes 393224 | tf_op jit(solution)/shard_map/ppermute | solution.py:539

commit v6 on v5

--- a/solution.py
+++ b/solution.py
@@ -355,11 +355,21 @@
     weight_sums[0:CH, :] = lax.fori_loop(0, 2, key_sums(halo_raws, edge_row, ROWS), acc)
 
 
-def row_kernel(own_raw, first_raw, second_raw, row_send):
+def row_kernel(own_raw, first_raw, second_raw, row_send, parts, sems):
+    copies = [
+        pltpu.make_async_copy(x.at[pl.ds(ROWS, 2)], parts.at[k], sems.at[k])
+        for k, x in enumerate((first_raw, second_raw))
+    ]
+    for copy in copies:
+        copy.start()
+    for copy in copies:
+        copy.wait()
     for row in range(2):
         for j in range(2):
-            row_send[row, j] = sum(
-                x[ROWS + row, j].astype(F32) for x in (own_raw, first_raw, second_raw)
+            row_send[row, j] = (
+                own_raw[ROWS + row, j].astype(F32)
+                + parts[0, row, j].astype(F32)
+                + parts[1, row, j].astype(F32)
             ).astype(BF16)
 
 
@@ -476,15 +486,15 @@
         for x in (features, out_cotangent, gain, query_proj, keyval_proj, output_proj)
     ]
 
-    first = lax.ppermute(features, "vcol", first_swap)
-    second = lax.ppermute(features, "vcol", second_swap)
     (edge,) = call(
         edge_kernel, [((2, COLS, CH, PIX), BF16)], [pltpu.SemaphoreType.DMA], 1000, side, held[0],
         far=(1,),
     )
-    row_halo = lax.ppermute(edge, "vrow", row_swap)
     first_corner = lax.ppermute(edge, grid, first_cross)
     second_corner = lax.ppermute(edge, grid, second_cross)
+    first = lax.ppermute(features, "vcol", first_swap)
+    second = lax.ppermute(features, "vcol", second_swap)
+    row_halo = lax.ppermute(edge, "vrow", row_swap)
 
     own = ((COLS, CH * S, PIX), F32)
     padded = ((6, CH * S, PIX), F32)
@@ -534,7 +544,9 @@
         for x, swap in ((to_first, first_swap), (to_second, second_swap))
     )
     (row_send,) = call(
-        row_kernel, [((2, COLS, 2 * CH, PIX), BF16)], [], 10000, own_raw, first_raw, second_raw
+        row_kernel, [((2, COLS, 2 * CH, PIX), BF16)],
+        [pltpu.VMEM((2, 2, COLS, 2 * CH, PIX), BF16), pltpu.SemaphoreType.DMA((2,))], 10000,
+        own_raw, first_raw, second_raw, far=(1, 2),
     )
     row_raw = lax.ppermute(row_send, "vrow", row_swap)
     (features_grad,) = call(

time: 95.6 us -> 95.6 us (level)
  no operation moved by 1% of the time
where the time goes in v6:
time: 95.6 us; the launch traced here: 95.1 us
  starting transfers between devices  40 us (42%)
  Pallas kernels  23.7 us (25%)
  blocking collectives  22.8 us (24%)
  waiting for transfers between devices  7.86 us (8%)
    pallas_call x9, Pallas kernels, call(): pl.pallas_call(kernel, out_shape=[jax.ShapeDtypeStruct(shape, dtype) for...  23.7 us
    all_to_all x1, starting transfers between devices, exchange(): return near_memory(lax.all_to_all(copies, axes, 0, 0))  15.4 us
    all_to_all x1, blocking collectives, exchange(): return near_memory(lax.all_to_all(copies, axes, 0, 0))  12.5 us
    all_to_all x1, blocking collectives, sum_everywhere(): return lax.all_to_all(copies, near, 0, 0).reshape(values.shape)  10.2 us
    ppermute x1, starting transfers between devices, layer(): first_corner = lax.ppermute(edge, grid, first_cross)  9.59 us
    all_to_all x1, waiting for transfers between devices, exchange(): return near_memory(lax.all_to_all(copies, axes, 0, 0))  7.84 us
    ppermute x1, starting transfers between devices, layer(): first = lax.ppermute(features, 'vcol', first_swap)  4.82 us
    ppermute x2, starting transfers between devices, layer(): lax.ppermute(pltpu.with_memory_space_constraint(x, pltpu.HBM), 'vcol', swap)  3.45 us
  transfers between devices with their start and end apart: 9, of which 1 were waited for; matrix products, arithmetic and copies ran while one was open for 0% of the time, Pallas kernels for 7%

profile of v6, /device:TPU:1, one launch (start us, length us, event | category | flops | bytes accessed | tf_op | source)
XLA Modules:
  0.0 95.1 jit_solution(8617622723945291779)
XLA Ops:
  0.6 4.8 %collective-permute-start = (bf16[8,2,64,128]{3,2,1,0:T(8,128)(2,1)}, bf16[8,2,64,128]{3,2,1,0:T(8,128)(2,1)S(1)}, u32[]{:S(2)}, u32[]{:S(2)}) collective-permute-start(bf16[8,2,64,128]{3,2,1,0:T(8,128)(2,1)} %feats.1), channel_id=1, source_target_pairs={{0,32},{64,96},{128,160},{192,224},{32,0},{96,64},{160,128},{224,1... | collective-permute-start | bytes 786440 | tf_op jit(solution)/shard_map/ppermute | solution.py:495
  5.5 0.7 collective-permute-start.1
  6.2 0.9 shard_map.102
  7.0 0.7 collective-permute-start.4
  7.7 9.6 %collective-permute-start.3 = (bf16[2,2,64,128]{3,2,1,0:T(8,128)(2,1)S(1)}, bf16[2,2,64,128]{3,2,1,0:T(8,128)(2,1)S(1)}, u32[]{:S(2)}, u32[]{:S(2)}) collective-permute-start(bf16[2,2,64,128]{3,2,1,0:T(8,128)(2,1)S(1)} %shard_map.102), channel_id=1, source_target_pairs={{0,288},{64,352},{128,416},{192,480},{32,256},{96,320},{160,384},{... | collective-permute-start | bytes 196616 | tf_op jit(solution)/shard_map/ppermute | solution.py:493
  17.3 3.1 %collective-permute-start.2 = (bf16[2,2,64,128]{3,2,1,0:T(8,128)(2,1)S(1)}, bf16[2,2,64,128]{3,2,1,0:T(8,128)(2,1)S(1)}, u32[]{:S(2)}, u32[]{:S(2)}) collective-permute-start(bf16[2,2,64,128]{3,2,1,0:T(8,128)(2,1)S(1)} %shard_map.102), channel_id=1, source_target_pairs={{0,256},{256,0},{1,257},{257,1},{2,258},{258,2},{3,259},{259,3},{4... | collective-permute-start | bytes 196616 | tf_op jit(solution)/shard_map/ppermute | solution.py:497
  20.4 2.9 %shard_map.101 = (f32[2,832,128]{2,1,0:T(8,128)S(1)}, f32[6,832,128]{2,1,0:T(8,128)S(1)}, f32[6,832,128]{2,1,0:T(8,128)S(1)}, f32[2,832,128]{2,1,0:T(8,128)S(1)}...) custom-call(s32[1]{0:T(128)} %bitcast.side, ...), custom_call_target="tpu_custom_call" | custom-call | flops 2000000 | bytes 1000000 | tf_op jit(solution)/shard_map/pallas_call | solution.py:428
  23.3 0.0 collective-permute-done.4.second_corner
  23.3 0.0 collective-permute-done.3.first_corner
  23.3 0.0 collective-permute-done.2.row_halo
  23.3 0.0 collective-permute-done.first
  23.4 0.0 collective-permute-done.1.second
  23.4 5.6 %shard_map.103 = (f32[6,832,128]{2,1,0:T(8,128)S(1)}, f32[6,832,128]{2,1,0:T(8,128)S(1)}, f32[6,16,128]{2,1,0:T(8,128)S(1)}, bf16[10,6,64,128]{3,2,1,0:T(8,128)(...) custom-call(s32[1]{0:T(128)} %bitcast.side, ...), custom_call_target="tpu_custom_call", output_to_operand_aliasing={{0}: (10, {}), {1}: (11, {}), {2}: (12, {}), {3}: (13, {})} | custom-call | flops 4000000 | bytes 1000000 | tf_op jit(solution)/shard_map/pallas_call | solution.py:428
  29.0 8.2 %shard_map.104 = (f32[128,128]{1,0:T(8,128)S(1)}, bf16[8,2,64,128]{3,2,1,0:T(8,128)(2,1)S(1)}, bf16[10,2,128,128]{3,2,1,0:T(8,128)(2,1)S(1)}, bf16[10,2,128,128]...) custom-call(s32[1]{0:T(128)} %bitcast.side, f32[2,832,128]{2,1,0:T(8,128)S(1)} %get-tuple-element.36.qs, ...), custom_call_target="tpu_custom_call" | custom-call | flops 5000000 | bytes 1000000 | tf_op jit(solution)/shard_map/pallas_call | solution.py:428
  37.2 1.9 %collective-permute-start.5 = (bf16[10,2,128,128]{3,2,1,0:T(8,128)(2,1)S(1)}, bf16[10,2,128,128]{3,2,1,0:T(8,128)(2,1)}, u32[]{:S(2)}, u32[]{:S(2)}) collective-permute-start(bf16[10,2,128,128]{3,2,1,0:T(8,128)(2,1)S(1)} %get-tuple-element.54), channel_id=1, source_target_pairs={{0,32},{64,96},{128,160},{192,224},{32,0},{96,64},{160,128},{224,1... | collective-permute-start | bytes 1966088 | tf_op jit(solution)/shard_map/ppermute | solution.py:543
  39.1 1.5 %collective-permute-start.6 = (bf16[10,2,128,128]{3,2,1,0:T(8,128)(2,1)S(1)}, bf16[10,2,128,128]{3,2,1,0:T(8,128)(2,1)}, u32[]{:S(2)}, u32[]{:S(2)}) collective-permute-start(bf16[10,2,128,128]{3,2,1,0:T(8,128)(2,1)S(1)} %get-tuple-element.55), channel_id=1, source_target_pairs={{32,64},{96,128},{160,192},{64,32},{128,96},{192,160},{33,65},{97,... | collective-permute-start | bytes 1966088 | tf_op jit(solution)/shard_map/ppermute | solution.py:543
  40.7 12.5 %all_to_all.15.shares = f32[16,8,128]{2,1,0:T(8,128)S(1)} all-to-all(f32[16,8,128]{2,1,0:T(8,128)S(1)} %bitcast.6), channel_id=1, replica_groups=mesh['vrow'=2,'vcol'=8,'px'=4,'py'=4,'pc'=2] {'px','pc','vrow'}, dimensions={0} | all-to-all | bytes 131072 | tf_op jit(solution)/shard_map/all_to_all | solution.py:458
  53.2 0.7 shard_map.107
  53.8 15.4 %all-to-all-start.1 = ((bf16[32,8,128]{2,1,0:T(8,128)(2,1)}), bf16[32,8,128]{2,1,0:T(8,128)(2,1)S(1)}, u32[]{:S(2)}, u32[]{:S(2)}) async-start(bf16[32,8,128]{2,1,0:T(8,128)(2,1)} %shard_map.107), calls=%async_computation.1 | async-start | bytes 131072 | tf_op jit(solution)/shard_map/all_to_all | solution.py:458
  69.3 0.0 collective-permute-done.5.first_raw
  69.3 0.0 collective-permute-done.6.second_raw
  69.3 1.0 %shard_map.105 = bf16[2,2,128,128]{3,2,1,0:T(8,128)(2,1)S(1)} custom-call(bf16[10,2,128,128]{3,2,1,0:T(8,128)(2,1)S(1)} %get-tuple-element.53.own_raw, bf16[10,2,128,128]{3,2,1,0:T(8,128)(2,1)} %collective-permute-done.5.first_raw, bf16[10,2,128,128]{3,2,1,0:T(8,128)(2,1)} %collective-permute-done.6.second_raw), custom_call_target="tpu_custom_call" | custom-call | flops 10000 | bytes 1000000 | tf_op jit(solution)/shard_map/pallas_call | solution.py:428
  70.3 2.3 %collective-permute-start.7 = (bf16[2,2,128,128]{3,2,1,0:T(8,128)(2,1)S(1)}, bf16[2,2,128,128]{3,2,1,0:T(8,128)(2,1)S(1)}, u32[]{:S(2)}, u32[]{:S(2)}) collective-permute-start(bf16[2,2,128,128]{3,2,1,0:T(8,128)(2,1)S(1)} %shard_map.105), channel_id=1, source_target_pairs={{0,256},{256,0},{1,257},{257,1},{2,258},{258,2},{3,259},{259,3},{4... | collective-permute-start | bytes 393224 | tf_op jit(solution)/shard_map/ppermute | solution.py:551
  72.6 7.8 %all-to-all-done.1.shares = bf16[32,8,128]{2,1,0:T(8,128)(2,1)S(1)} async-done(((bf16[32,8,128]{2,1,0:T(8,128)(2,1)}), bf16[32,8,128]{2,1,0:T(8,128)(2,1)S(1)}, u32[]{:S(2)}, u32[]{:S(2)}) %all-to-all-start.1) | async-done | bytes 65568 | tf_op jit(solution)/shard_map/all_to_all | solution.py:458
  80.5 10.2 %all_to_all.16 = f32[16,8,128]{2,1,0:T(8,128)S(1)} all-to-all(f32[16,8,128]{2,1,0:T(8,128)S(1)} %shard_map.108), channel_id=1, replica_groups=mesh['vrow'=2,'vcol'=8,'px'=4,'py'=4,'pc'=2] {'px','pc','vrow'}, dimensions={0} | all-to-all | bytes 131072 | tf_op jit(solution)/shard_map/all_to_all | solution.py:464
  90.8 0.7 shard_map.109
  91.5 0.0 collective-permute-done.7.row_raw
  91.5 3.6 %shard_map.106 = bf16[8,2,64,128]{3,2,1,0:T(8,128)(2,1)} custom-call(s32[1]{0:T(128)} %bitcast.side, bf16[10,2,128,128]{3,2,1,0:T(8,128)(2,1)S(1)} %get-tuple-element.53.own_raw, bf16[10,2,128,128]{3,2,1,0:T(8,128)(2,1)} %collective-permute-done.5.first_raw, bf16[10,2,128,128]{3,2,1,0:T(8,128)(2,1)} %collective-permute-done.6.second_raw, ...), custom_call_target="tpu_custom_call" | custom-call | flops 2000000 | bytes 1000000 | tf_op jit(solution)/shard_map/pallas_call | solution.py:428
  (1 shorter events, 0.0 us)
Async XLA Ops:
  0.6 22.7 %collective-permute-start = (bf16[8,2,64,128]{3,2,1,0:T(8,128)(2,1)}, bf16[8,2,64,128]{3,2,1,0:T(8,128)(2,1)S(1)}, u32[]{:S(2)}, u32[]{:S(2)}) collective-permute-start(bf16[8,2,64,128]{3,2,1,0:T(8,128)(2,1)} %feats.1), channel_id=1, source_target_pairs={{0,32},{64,96},{128,160},{192,224},{32,0},{96,64},{160,128},{224,1... | collective-permute-start | bytes 786440 | tf_op jit(solution)/shard_map/ppermute | solution.py:495
  5.5 17.9 %collective-permute-start.1 = (bf16[8,2,64,128]{3,2,1,0:T(8,128)(2,1)}, bf16[8,2,64,128]{3,2,1,0:T(8,128)(2,1)S(1)}, u32[]{:S(2)}, u32[]{:S(2)}) collective-permute-start(bf16[8,2,64,128]{3,2,1,0:T(8,128)(2,1)} %feats.1), channel_id=1, source_target_pairs={{32,64},{96,128},{160,192},{64,32},{128,96},{192,160},{33,65},{97,... | collective-permute-start | bytes 786440 | tf_op jit(solution)/shard_map/ppermute | solution.py:496
  7.0 16.3 %collective-permute-start.4 = (bf16[2,2,64,128]{3,2,1,0:T(8,128)(2,1)S(1)}, bf16[2,2,64,128]{3,2,1,0:T(8,128)(2,1)S(1)}, u32[]{:S(2)}, u32[]{:S(2)}) collective-permute-start(bf16[2,2,64,128]{3,2,1,0:T(8,128)(2,1)S(1)} %shard_map.102), channel_id=1, source_target_pairs={{32,320},{96,384},{160,448},{64,288},{128,352},{192,416},{288,64},... | collective-permute-start | bytes 196616 | tf_op jit(solution)/shard_map/ppermute | solution.py:494
  7.7 15.6 %collective-permute-start.3 = (bf16[2,2,64,128]{3,2,1,0:T(8,128)(2,1)S(1)}, bf16[2,2,64,128]{3,2,1,0:T(8,128)(2,1)S(1)}, u32[]{:S(2)}, u32[]{:S(2)}) collective-permute-start(bf16[2,2,64,128]{3,2,1,0:T(8,128)(2,1)S(1)} %shard_map.102), channel_id=1, source_target_pairs={{0,288},{64,352},{128,416},{192,480},{32,256},{96,320},{160,384},{... | collective-permute-start | bytes 196616 | tf_op jit(solution)/shard_map/ppermute | solution.py:493
  17.3 6.0 %collective-permute-start.2 = (bf16[2,2,64,128]{3,2,1,0:T(8,128)(2,1)S(1)}, bf16[2,2,64,128]{3,2,1,0:T(8,128)(2,1)S(1)}, u32[]{:S(2)}, u32[]{:S(2)}) collective-permute-start(bf16[2,2,64,128]{3,2,1,0:T(8,128)(2,1)S(1)} %shard_map.102), channel_id=1, source_target_pairs={{0,256},{256,0},{1,257},{257,1},{2,258},{258,2},{3,259},{259,3},{4... | collective-permute-start | bytes 196616 | tf_op jit(solution)/shard_map/ppermute | solution.py:497
  37.2 32.1 %collective-permute-start.5 = (bf16[10,2,128,128]{3,2,1,0:T(8,128)(2,1)S(1)}, bf16[10,2,128,128]{3,2,1,0:T(8,128)(2,1)}, u32[]{:S(2)}, u32[]{:S(2)}) collective-permute-start(bf16[10,2,128,128]{3,2,1,0:T(8,128)(2,1)S(1)} %get-tuple-element.54), channel_id=1, source_target_pairs={{0,32},{64,96},{128,160},{192,224},{32,0},{96,64},{160,128},{224,1... | collective-permute-start | bytes 1966088 | tf_op jit(solution)/shard_map/ppermute | solution.py:543
  39.1 30.1 %collective-permute-start.6 = (bf16[10,2,128,128]{3,2,1,0:T(8,128)(2,1)S(1)}, bf16[10,2,128,128]{3,2,1,0:T(8,128)(2,1)}, u32[]{:S(2)}, u32[]{:S(2)}) collective-permute-start(bf16[10,2,128,128]{3,2,1,0:T(8,128)(2,1)S(1)} %get-tuple-element.55), channel_id=1, source_target_pairs={{32,64},{96,128},{160,192},{64,32},{128,96},{192,160},{33,65},{97,... | collective-permute-start | bytes 1966088 | tf_op jit(solution)/shard_map/ppermute | solution.py:543
  53.8 26.6 %all-to-all-start.1 = ((bf16[32,8,128]{2,1,0:T(8,128)(2,1)}), bf16[32,8,128]{2,1,0:T(8,128)(2,1)S(1)}, u32[]{:S(2)}, u32[]{:S(2)}) async-start(bf16[32,8,128]{2,1,0:T(8,128)(2,1)} %shard_map.107), calls=%async_computation.1 | async-start | bytes 131072 | tf_op jit(solution)/shard_map/all_to_all | solution.py:458
  70.3 21.2 %collective-permute-start.7 = (bf16[2,2,128,128]{3,2,1,0:T(8,128)(2,1)S(1)}, bf16[2,2,128,128]{3,2,1,0:T(8,128)(2,1)S(1)}, u32[]{:S(2)}, u32[]{:S(2)}) collective-permute-start(bf16[2,2,128,128]{3,2,1,0:T(8,128)(2,1)S(1)} %shard_map.105), channel_id=1, source_target_pairs={{0,256},{256,0},{1,257},{257,1},{2,258},{258,2},{3,259},{259,3},{4... | collective-permute-start | bytes 393224 | tf_op jit(solution)/shard_map/ppermute | solution.py:551

commit v7 on v6

--- a/solution.py
+++ b/solution.py
@@ -102,31 +102,30 @@
     k_inv[col + j, pl.ds(to_row, 1), :] = key_scale
 
 
-def edge_kernel(side, feats, edge, sem):
+def fetch_kernel(
+    side, feats_hbm, cot_hbm, gain_hbm, w_q_hbm, w_kv_hbm, w_out_hbm,
+    edge, feats, cot, gain_row, w_q, w_kv, w_out, sems,
+):
     _, _, edge_row = halo_start(side)
-    copy = pltpu.make_async_copy(feats.at[pl.ds(edge_row, 2)], edge, sem)
-    copy.start()
-    copy.wait()
-
-
-def own_kernel(
-    side, feats_hbm, cot_hbm, gain_hbm, w_q_hbm, w_kv_hbm, w_out_hbm,
-    qs, ks, vs, ogs, q_inv, k_inv, normed, gain_out, w_in, w_back, feats, cot, w_q, w_kv, gain_row,
-    w_out, sems,
-):
     moves = (
+        (feats_hbm.at[pl.ds(edge_row, 2)], edge), (feats_hbm, feats), (cot_hbm, cot),
         (gain_hbm, gain_row), (w_q_hbm, w_q), (w_kv_hbm, w_kv), (w_out_hbm, w_out),
-        (feats_hbm, feats), (cot_hbm, cot),
     )
     copies = [pltpu.make_async_copy(a, b, sems.at[k]) for k, (a, b) in enumerate(moves)]
     for copy in copies:
         copy.start()
+    for copy in copies:
+        copy.wait()
+
+
+def own_kernel(
+    side, feats, cot, gain_row, w_q, w_kv, w_out,
+    qs, ks, vs, ogs, q_inv, k_inv, normed, gain_out, w_in, w_back,
+):
     _, clear_row, _ = halo_start(side)
     clear_rows((ks, vs), clear_row)
     clear_rows((qs, ogs), 0)
     clear_rows((qs, ogs), 10)
-    for copy in copies[:4]:
-        copy.wait()
     gain_col = jnp.sum(
         jnp.where(eye(), jnp.broadcast_to(gain_row[...], (CH, CH)), 0.0), axis=1, keepdims=True
     )
@@ -137,8 +136,6 @@
     w_back[...] = jnp.concatenate([w_q[...].astype(F32), w_kv[...].astype(F32)], axis=1).astype(BF16)
     w_full = w_in[...]
     w_o = w_out[...]
-    for copy in copies[4:]:
-        copy.wait()
 
     def visit(row):
         views = normed_views(feats, row, gain_full)
@@ -291,39 +288,42 @@
     query_acc, out_acc = lax.fori_loop(0, ROWS // 2, query_sums, (flat, flat))
     weight_sums[CH : 2 * CH, :] = jnp.concatenate([query_acc, out_acc], axis=1)
 
-    def key_step(acc, step, col, j, i, base, first_row):
-        key_acc, value_acc = acc
-        start = first_row - i + 2
-        prob = probs[step, pl.ds((5 * j + i) * W + start, ROWS), :]
-        score_grad = score_grads[step, pl.ds((5 * j + i) * W + start, ROWS), :]
-        key_acc = [a + score_grad * take(qs, col, base + d * S + start) for d, a in enumerate(key_acc)]
-        value_acc = [a + prob * take(ogs, col, base + d * S + start) for d, a in enumerate(value_acc)]
-        return key_acc, value_acc
-
     edge_first, edge_offset = edge_row * 2 // 3, edge_row // 2
 
-    def key_columns(view_col, head, cols):
-        base = head * (SIZE * S)
+    def key_columns(view_cols, channel, count, head, cols):
         own_steps = [(i, 2) for i in range(5)]
         halo_steps = [(edge_offset + i, edge_first) for i in range(2)]
         for steps, key_ref, value_ref in (
             (own_steps, grads, raws), (halo_steps, halo_grads, halo_raws)
         ):
-            acc = ([zeros] * SIZE, [zeros] * SIZE)
+            key_acc = [[zeros] * count for _ in view_cols]
+            value_acc = [[zeros] * count for _ in view_cols]
             for col in cols:
                 for i, first_row in steps:
-                    acc = key_step(acc, col * HEADS + head, col, view_col - col, i, base, first_row)
-            for d in range(SIZE):
-                key_ref[view_col, head * SIZE + d] = acc[0][d]
-                value_ref[view_col, pl.ds((CH + head * SIZE + d) * R, ROWS), :] = acc[1][d]
+                    start = first_row - i + 2
+                    query = [take(qs, col, (channel + d) * S + start) for d in range(count)]
+                    og = [take(ogs, col, (channel + d) * S + start) for d in range(count)]
+                    for k, view_col in enumerate(view_cols):
+                        row = (5 * (view_col - col) + i) * W + start
+                        prob = probs[col * HEADS + head, pl.ds(row, ROWS), :]
+                        score_grad = score_grads[col * HEADS + head, pl.ds(row, ROWS), :]
+                        key_acc[k] = [a + score_grad * b for a, b in zip(key_acc[k], query)]
+                        value_acc[k] = [a + prob * b for a, b in zip(value_acc[k], og)]
+            for k, view_col in enumerate(view_cols):
+                for d in range(count):
+                    key_ref[view_col, channel + d] = key_acc[k][d]
+                    value_ref[view_col, pl.ds((CH + channel + d) * R, ROWS), :] = value_acc[k][d]
+
+    half = SIZE // 2
 
     def inner_columns(step, carry):
-        key_columns(1 + step // HEADS, step % HEADS, (0, 1))
+        first, part = 1 + step // (2 * HEADS) * 2, step % (2 * HEADS)
+        key_columns((first, first + 1), part * half, half, part // 2, (0, 1))
         return carry
 
     def outer_columns(step, carry):
-        side_col = step // HEADS
-        key_columns(5 * side_col, step % HEADS, (side_col,))
+        side_col, head = step // HEADS, step % HEADS
+        key_columns((5 * side_col,), head * SIZE, SIZE, head, (side_col,))
         return carry
 
     lax.fori_loop(0, 4 * HEADS, inner_columns, 0)
@@ -375,15 +375,30 @@
 
 def features_kernel(
     side, own_raw, first_raw, second_raw, row_raw, raw_query, feats, cot, gain, w_back,
-    feats_grad, shared,
+    feats_grad, shared, query_part, parts, sems,
 ):
+    copies = [
+        pltpu.make_async_copy(x.at[pl.ds(0, ROWS)], parts.at[k], sems.at[k])
+        for k, x in enumerate((first_raw, second_raw))
+    ]
+    for copy in copies:
+        copy.start()
     _, _, edge_row = halo_start(side)
+    gain_full = gain[...]
+    w_query, w_keys = w_back[:, :CH], w_back[:, CH:]
+
+    def query_row(row):
+        query_part[row] = jnp.dot(w_query, pair(raw_query, row), preferred_element_type=F32)
+
+    each_row(ROWS, (query_row,))
+    for copy in copies:
+        copy.wait()
 
     def join(row):
         for j in range(2):
             shared[row, j] = (
-                own_raw[row, j].astype(F32) + first_raw[row, j].astype(F32)
-                + second_raw[row, j].astype(F32)
+                own_raw[row, j].astype(F32) + parts[0, row, j].astype(F32)
+                + parts[1, row, j].astype(F32)
             )
 
     def join_edge(row):
@@ -392,12 +407,10 @@
 
     each_row(ROWS, (join,))
     each_row(2, (join_edge,))
-    gain_full = gain[...]
-    w_b = w_back[...]
 
     def view_row(row):
-        raw = jnp.concatenate([pair(raw_query, row), pair(shared, row).astype(BF16)], axis=0)
-        normed_grad = jnp.dot(w_b, raw, preferred_element_type=F32)
+        raw = pair(shared, row).astype(BF16)
+        normed_grad = query_part[row] + jnp.dot(w_keys, raw, preferred_element_type=F32)
         for j in range(2):
             values = feats[row, j].astype(F32)
             inv_norm = inv_rms(values)
@@ -486,9 +499,14 @@
         for x in (features, out_cotangent, gain, query_proj, keyval_proj, output_proj)
     ]
 
-    (edge,) = call(
-        edge_kernel, [((2, COLS, CH, PIX), BF16)], [pltpu.SemaphoreType.DMA], 1000, side, held[0],
-        far=(1,),
+    views = ((ROWS, COLS, CH, PIX), BF16)
+    edge, feats, cot, gain_row, w_q, w_kv, w_out = call(
+        fetch_kernel,
+        [
+            ((2, COLS, CH, PIX), BF16), views, views, ((1, CH), F32), ((CH, CH), BF16),
+            ((CH, 2 * CH), BF16), ((CH, CH), BF16),
+        ],
+        [pltpu.SemaphoreType.DMA((7,))], 1000, side, *held, far=(1, 2, 3, 4, 5, 6),
     )
     first_corner = lax.ppermute(edge, grid, first_cross)
     second_corner = lax.ppermute(edge, grid, second_cross)
@@ -502,20 +520,16 @@
     key_lanes = ((6, 16, PIX), F32)
     steps = COLS * HEADS
     offsets = ((steps, 25, ROWS, PIX), F32)
-    views = ((ROWS, COLS, CH, PIX), BF16)
     all_views = ((ROWS + 2, 6, CH, PIX), BF16)
     key_views = ((ROWS + 2, COLS, 2 * CH, PIX), BF16)
-    (
-        qs, ks, vs, ogs, q_inv, k_inv, normed, gain_full, w_in, w_back, feats, cot, w_q, w_kv, gain_row,
-    ) = call(
+    qs, ks, vs, ogs, q_inv, k_inv, normed, gain_full, w_in, w_back = call(
         own_kernel,
         [
             own, padded, padded, own, lanes, key_lanes, all_views, ((CH, PIX), F32),
-            ((3 * CH, CH), BF16), ((CH, 3 * CH), BF16), views, views, ((CH, CH), BF16),
-            ((CH, 2 * CH), BF16), ((1, CH), F32),
+            ((3 * CH, CH), BF16), ((CH, 3 * CH), BF16),
         ],
-        [pltpu.VMEM((CH, CH), BF16), pltpu.SemaphoreType.DMA((6,))], 2000000,
-        side, *held, far=(1, 2, 3, 4, 5, 6),
+        [], 2000000,
+        side, feats, cot, gain_row, w_q, w_kv, w_out,
     )
     ks, vs, k_inv, normed, weights, prob_grads, attended, stats = call(
         forward_kernel,
@@ -550,8 +564,14 @@
     )
     row_raw = lax.ppermute(row_send, "vrow", row_swap)
     (features_grad,) = call(
-        features_kernel, [(features.shape, BF16)], [(ROWS, COLS, 2 * CH, PIX)], 2000000,
+        features_kernel, [(features.shape, BF16)],
+        [
+            (ROWS, COLS, 2 * CH, PIX), (ROWS, CH, COLS * PIX),
+            pltpu.VMEM((2, ROWS, COLS, 2 * CH, PIX), BF16), pltpu.SemaphoreType.DMA((2,)),
+        ],
+        2000000,
         side, own_raw, first_raw, second_raw, row_raw, raw_query, feats, cot, gain_full, w_back,
+        far=(2, 3),
     )
     tokens_all = ROWS * COLS * PIX * math.prod(lax.axis_size(a) for a in AXES)
     query_grad, keyval_grad, output_grad, gain_grad = call(

time: 95.6 us -> 97 us (1.015)
    ppermute x1, starting transfers between devices: 4.82 us -> 8.14 us  [layer(): first = lax.ppermute(features, 'vcol', first_swap)]
    all_to_all x1, starting transfers between devices: 15.4 us -> 12.7 us  [exchange(): return near_memory(lax.all_to_all(copies, axes, 0, 0))]
  transfers between devices with their start and end apart: 9 -> 9, of which waited for: 1 -> 2; matrix products, arithmetic and copies ran while one was open for 0% -> 0% of each run, Pallas kernels for 7% -> 6%
where the time goes in v7:
time: 97 us; the launch traced here: 96.5 us
  starting transfers between devices  40.6 us (42%)
  blocking collectives  23.6 us (24%)
  Pallas kernels  23.3 us (24%)
  waiting for transfers between devices  8.32 us (9%)
    pallas_call x9, Pallas kernels, call(): pl.pallas_call(kernel, out_shape=[jax.ShapeDtypeStruct(shape, dtype) for...  23.3 us
    all_to_all x1, blocking collectives, exchange(): return near_memory(lax.all_to_all(copies, axes, 0, 0))  13.4 us
    all_to_all x1, starting transfers between devices, exchange(): return near_memory(lax.all_to_all(copies, axes, 0, 0))  12.7 us
    all_to_all x1, blocking collectives, sum_everywhere(): return lax.all_to_all(copies, near, 0, 0).reshape(values.shape)  10.2 us
    ppermute x1, starting transfers between devices, layer(): first_corner = lax.ppermute(edge, grid, first_cross)  9.45 us
    ppermute x1, starting transfers between devices, layer(): first = lax.ppermute(features, 'vcol', first_swap)  8.14 us
    all_to_all x1, waiting for transfers between devices, exchange(): return near_memory(lax.all_to_all(copies, axes, 0, 0))  7.84 us
    ppermute x2, starting transfers between devices, layer(): lax.ppermute(pltpu.with_memory_space_constraint(x, pltpu.HBM), 'vcol', swap)  3.44 us
  transfers between devices with their start and end apart: 9, of which 2 were waited for; matrix products, arithmetic and copies ran while one was open for 0% of the time, Pallas kernels for 6%

profile of v7, /device:TPU:1, one launch (start us, length us, event | category | flops | bytes accessed | tf_op | source)
XLA Modules:
  0.0 96.5 jit_solution(9562189633034999244)
XLA Ops:
  0.6 0.7 collective-permute-start.1
  1.3 8.1 %collective-permute-start = (bf16[8,2,64,128]{3,2,1,0:T(8,128)(2,1)}, bf16[8,2,64,128]{3,2,1,0:T(8,128)(2,1)S(1)}, u32[]{:S(2)}, u32[]{:S(2)}) collective-permute-start(bf16[8,2,64,128]{3,2,1,0:T(8,128)(2,1)} %feats_hbm.1), channel_id=1, source_target_pairs={{0,32},{64,96},{128,160},{192,224},{32,0},{96,64},{160,128},{224,1... | collective-permute-start | bytes 786440 | tf_op jit(solution)/shard_map/ppermute | solution.py:513
  9.5 1.1 %shard_map.101 = (bf16[2,2,64,128]{3,2,1,0:T(8,128)(2,1)S(1)}, bf16[8,2,64,128]{3,2,1,0:T(8,128)(2,1)S(1)}, bf16[8,2,64,128]{3,2,1,0:T(8,128)(2,1)S(1)}, f32[1,6...) custom-call(s32[1]{0:T(128)} %bitcast.side, ...), custom_call_target="tpu_custom_call" | custom-call | flops 1000 | bytes 1000000 | tf_op jit(solution)/shard_map/pallas_call | solution.py:441
  10.6 0.7 collective-permute-start.4
  11.3 9.4 %collective-permute-start.3 = (bf16[2,2,64,128]{3,2,1,0:T(8,128)(2,1)S(1)}, bf16[2,2,64,128]{3,2,1,0:T(8,128)(2,1)S(1)}, u32[]{:S(2)}, u32[]{:S(2)}) collective-permute-start(bf16[2,2,64,128]{3,2,1,0:T(8,128)(2,1)S(1)} %get-tuple-element.45), channel_id=1, source_target_pairs={{0,288},{64,352},{128,416},{192,480},{32,256},{96,320},{160,384},{... | collective-permute-start | bytes 196616 | tf_op jit(solution)/shard_map/ppermute | solution.py:511
  20.7 3.2 %collective-permute-start.2 = (bf16[2,2,64,128]{3,2,1,0:T(8,128)(2,1)S(1)}, bf16[2,2,64,128]{3,2,1,0:T(8,128)(2,1)S(1)}, u32[]{:S(2)}, u32[]{:S(2)}) collective-permute-start(bf16[2,2,64,128]{3,2,1,0:T(8,128)(2,1)S(1)} %get-tuple-element.45), channel_id=1, source_target_pairs={{0,256},{256,0},{1,257},{257,1},{2,258},{258,2},{3,259},{259,3},{4... | collective-permute-start | bytes 196616 | tf_op jit(solution)/shard_map/ppermute | solution.py:515
  24.0 1.9 %shard_map.102 = (f32[2,832,128]{2,1,0:T(8,128)S(1)}, f32[6,832,128]{2,1,0:T(8,128)S(1)}, f32[6,832,128]{2,1,0:T(8,128)S(1)}, f32[2,832,128]{2,1,0:T(8,128)S(1)}...) custom-call(s32[1]{0:T(128)} %bitcast.side, ...), custom_call_target="tpu_custom_call" | custom-call | flops 2000000 | bytes 1000000 | tf_op jit(solution)/shard_map/pallas_call | solution.py:441
  25.9 0.0 collective-permute-done.4.second_corner
  25.9 0.0 collective-permute-done.3.first_corner
  25.9 0.5 collective-permute-done.2.row_halo
  26.4 0.0 collective-permute-done.1.second
  26.4 0.0 collective-permute-done.first
  26.4 5.5 %shard_map.103 = (f32[6,832,128]{2,1,0:T(8,128)S(1)}, f32[6,832,128]{2,1,0:T(8,128)S(1)}, f32[6,16,128]{2,1,0:T(8,128)S(1)}, bf16[10,6,64,128]{3,2,1,0:T(8,128)(...) custom-call(s32[1]{0:T(128)} %bitcast.side, ...), custom_call_target="tpu_custom_call", output_to_operand_aliasing={{0}: (10, {}), {1}: (11, {}), {2}: (12, {}), {3}: (13, {})} | custom-call | flops 4000000 | bytes 1000000 | tf_op jit(solution)/shard_map/pallas_call | solution.py:441
  31.8 8.4 %shard_map.104 = (f32[128,128]{1,0:T(8,128)S(1)}, bf16[8,2,64,128]{3,2,1,0:T(8,128)(2,1)S(1)}, bf16[10,2,128,128]{3,2,1,0:T(8,128)(2,1)S(1)}, bf16[10,2,128,128]...) custom-call(s32[1]{0:T(128)} %bitcast.side, f32[2,832,128]{2,1,0:T(8,128)S(1)} %get-tuple-element.44.qs, ...), custom_call_target="tpu_custom_call" | custom-call | flops 5000000 | bytes 1000000 | tf_op jit(solution)/shard_map/pallas_call | solution.py:441
  40.2 1.9 %collective-permute-start.5 = (bf16[10,2,128,128]{3,2,1,0:T(8,128)(2,1)S(1)}, bf16[10,2,128,128]{3,2,1,0:T(8,128)(2,1)}, u32[]{:S(2)}, u32[]{:S(2)}) collective-permute-start(bf16[10,2,128,128]{3,2,1,0:T(8,128)(2,1)S(1)} %get-tuple-element.62), channel_id=1, source_target_pairs={{0,32},{64,96},{128,160},{192,224},{32,0},{96,64},{160,128},{224,1... | collective-permute-start | bytes 1966088 | tf_op jit(solution)/shard_map/ppermute | solution.py:557
  42.2 1.5 %collective-permute-start.6 = (bf16[10,2,128,128]{3,2,1,0:T(8,128)(2,1)S(1)}, bf16[10,2,128,128]{3,2,1,0:T(8,128)(2,1)}, u32[]{:S(2)}, u32[]{:S(2)}) collective-permute-start(bf16[10,2,128,128]{3,2,1,0:T(8,128)(2,1)S(1)} %get-tuple-element.63), channel_id=1, source_target_pairs={{32,64},{96,128},{160,192},{64,32},{128,96},{192,160},{33,65},{97,... | collective-permute-start | bytes 1966088 | tf_op jit(solution)/shard_map/ppermute | solution.py:557
  43.7 13.4 %all_to_all.15.shares = f32[16,8,128]{2,1,0:T(8,128)S(1)} all-to-all(f32[16,8,128]{2,1,0:T(8,128)S(1)} %bitcast.6), channel_id=1, replica_groups=mesh['vrow'=2,'vcol'=8,'px'=4,'py'=4,'pc'=2] {'px','pc','vrow'}, dimensions={0} | all-to-all | bytes 131072 | tf_op jit(solution)/shard_map/all_to_all | solution.py:471
  57.1 0.7 shard_map.107
  57.7 12.7 %all-to-all-start.1 = ((bf16[32,8,128]{2,1,0:T(8,128)(2,1)}), bf16[32,8,128]{2,1,0:T(8,128)(2,1)S(1)}, u32[]{:S(2)}, u32[]{:S(2)}) async-start(bf16[32,8,128]{2,1,0:T(8,128)(2,1)} %shard_map.107), calls=%async_computation.1 | async-start | bytes 131072 | tf_op jit(solution)/shard_map/all_to_all | solution.py:471
  70.4 0.0 collective-permute-done.5.first_raw
  70.4 0.0 collective-permute-done.6.second_raw
  70.4 1.0 %shard_map.105 = bf16[2,2,128,128]{3,2,1,0:T(8,128)(2,1)S(1)} custom-call(bf16[10,2,128,128]{3,2,1,0:T(8,128)(2,1)S(1)} %get-tuple-element.61.own_raw, bf16[10,2,128,128]{3,2,1,0:T(8,128)(2,1)} %collective-permute-done.5.first_raw, bf16[10,2,128,128]{3,2,1,0:T(8,128)(2,1)} %collective-permute-done.6.second_raw), custom_call_target="tpu_custom_call" | custom-call | flops 10000 | bytes 1000000 | tf_op jit(solution)/shard_map/pallas_call | solution.py:441
  71.5 2.3 %collective-permute-start.7 = (bf16[2,2,128,128]{3,2,1,0:T(8,128)(2,1)S(1)}, bf16[2,2,128,128]{3,2,1,0:T(8,128)(2,1)S(1)}, u32[]{:S(2)}, u32[]{:S(2)}) collective-permute-start(bf16[2,2,128,128]{3,2,1,0:T(8,128)(2,1)S(1)} %shard_map.105), channel_id=1, source_target_pairs={{0,256},{256,0},{1,257},{257,1},{2,258},{258,2},{3,259},{259,3},{4... | collective-permute-start | bytes 393224 | tf_op jit(solution)/shard_map/ppermute | solution.py:565
  73.8 7.8 %all-to-all-done.1.shares = bf16[32,8,128]{2,1,0:T(8,128)(2,1)S(1)} async-done(((bf16[32,8,128]{2,1,0:T(8,128)(2,1)}), bf16[32,8,128]{2,1,0:T(8,128)(2,1)S(1)}, u32[]{:S(2)}, u32[]{:S(2)}) %all-to-all-start.1) | async-done | bytes 65568 | tf_op jit(solution)/shard_map/all_to_all | solution.py:471
  81.7 10.2 %all_to_all.16 = f32[16,8,128]{2,1,0:T(8,128)S(1)} all-to-all(f32[16,8,128]{2,1,0:T(8,128)S(1)} %shard_map.108), channel_id=1, replica_groups=mesh['vrow'=2,'vcol'=8,'px'=4,'py'=4,'pc'=2] {'px','pc','vrow'}, dimensions={0} | all-to-all | bytes 131072 | tf_op jit(solution)/shard_map/all_to_all | solution.py:477
  91.9 0.7 shard_map.109
  92.6 0.0 collective-permute-done.7.row_raw
  92.6 3.9 %shard_map.106 = bf16[8,2,64,128]{3,2,1,0:T(8,128)(2,1)} custom-call(s32[1]{0:T(128)} %bitcast.side, bf16[10,2,128,128]{3,2,1,0:T(8,128)(2,1)S(1)} %get-tuple-element.61.own_raw, bf16[10,2,128,128]{3,2,1,0:T(8,128)(2,1)} %collective-permute-done.5.first_raw, bf16[10,2,128,128]{3,2,1,0:T(8,128)(2,1)} %collective-permute-done.6.second_raw, ...), custom_call_target="tpu_custom_call" | custom-call | flops 2000000 | bytes 1000000 | tf_op jit(solution)/shard_map/pallas_call | solution.py:441
  (1 shorter events, 0.0 us)
Async XLA Ops:
  0.6 25.7 %collective-permute-start.1 = (bf16[8,2,64,128]{3,2,1,0:T(8,128)(2,1)}, bf16[8,2,64,128]{3,2,1,0:T(8,128)(2,1)S(1)}, u32[]{:S(2)}, u32[]{:S(2)}) collective-permute-start(bf16[8,2,64,128]{3,2,1,0:T(8,128)(2,1)} %feats_hbm.1), channel_id=1, source_target_pairs={{32,64},{96,128},{160,192},{64,32},{128,96},{192,160},{33,65},{97,... | collective-permute-start | bytes 786440 | tf_op jit(solution)/shard_map/ppermute | solution.py:514
  1.3 25.0 %collective-permute-start = (bf16[8,2,64,128]{3,2,1,0:T(8,128)(2,1)}, bf16[8,2,64,128]{3,2,1,0:T(8,128)(2,1)S(1)}, u32[]{:S(2)}, u32[]{:S(2)}) collective-permute-start(bf16[8,2,64,128]{3,2,1,0:T(8,128)(2,1)} %feats_hbm.1), channel_id=1, source_target_pairs={{0,32},{64,96},{128,160},{192,224},{32,0},{96,64},{160,128},{224,1... | collective-permute-start | bytes 786440 | tf_op jit(solution)/shard_map/ppermute | solution.py:513
  10.6 15.3 %collective-permute-start.4 = (bf16[2,2,64,128]{3,2,1,0:T(8,128)(2,1)S(1)}, bf16[2,2,64,128]{3,2,1,0:T(8,128)(2,1)S(1)}, u32[]{:S(2)}, u32[]{:S(2)}) collective-permute-start(bf16[2,2,64,128]{3,2,1,0:T(8,128)(2,1)S(1)} %get-tuple-element.45), channel_id=1, source_target_pairs={{32,320},{96,384},{160,448},{64,288},{128,352},{192,416},{288,64},... | collective-permute-start | bytes 196616 | tf_op jit(solution)/shard_map/ppermute | solution.py:512
  11.3 14.6 %collective-permute-start.3 = (bf16[2,2,64,128]{3,2,1,0:T(8,128)(2,1)S(1)}, bf16[2,2,64,128]{3,2,1,0:T(8,128)(2,1)S(1)}, u32[]{:S(2)}, u32[]{:S(2)}) collective-permute-start(bf16[2,2,64,128]{3,2,1,0:T(8,128)(2,1)S(1)} %get-tuple-element.45), channel_id=1, source_target_pairs={{0,288},{64,352},{128,416},{192,480},{32,256},{96,320},{160,384},{... | collective-permute-start | bytes 196616 | tf_op jit(solution)/shard_map/ppermute | solution.py:511
  20.7 5.6 %collective-permute-start.2 = (bf16[2,2,64,128]{3,2,1,0:T(8,128)(2,1)S(1)}, bf16[2,2,64,128]{3,2,1,0:T(8,128)(2,1)S(1)}, u32[]{:S(2)}, u32[]{:S(2)}) collective-permute-start(bf16[2,2,64,128]{3,2,1,0:T(8,128)(2,1)S(1)} %get-tuple-element.45), channel_id=1, source_target_pairs={{0,256},{256,0},{1,257},{257,1},{2,258},{258,2},{3,259},{259,3},{4... | collective-permute-start | bytes 196616 | tf_op jit(solution)/shard_map/ppermute | solution.py:515
  40.2 30.2 %collective-permute-start.5 = (bf16[10,2,128,128]{3,2,1,0:T(8,128)(2,1)S(1)}, bf16[10,2,128,128]{3,2,1,0:T(8,128)(2,1)}, u32[]{:S(2)}, u32[]{:S(2)}) collective-permute-start(bf16[10,2,128,128]{3,2,1,0:T(8,128)(2,1)S(1)} %get-tuple-element.62), channel_id=1, source_target_pairs={{0,32},{64,96},{128,160},{192,224},{32,0},{96,64},{160,128},{224,1... | collective-permute-start | bytes 1966088 | tf_op jit(solution)/shard_map/ppermute | solution.py:557
  42.2 28.3 %collective-permute-start.6 = (bf16[10,2,128,128]{3,2,1,0:T(8,128)(2,1)S(1)}, bf16[10,2,128,128]{3,2,1,0:T(8,128)(2,1)}, u32[]{:S(2)}, u32[]{:S(2)}) collective-permute-start(bf16[10,2,128,128]{3,2,1,0:T(8,128)(2,1)S(1)} %get-tuple-element.63), channel_id=1, source_target_pairs={{32,64},{96,128},{160,192},{64,32},{128,96},{192,160},{33,65},{97,... | collective-permute-start | bytes 1966088 | tf_op jit(solution)/shard_map/ppermute | solution.py:557
  57.7 23.9 %all-to-all-start.1 = ((bf16[32,8,128]{2,1,0:T(8,128)(2,1)}), bf16[32,8,128]{2,1,0:T(8,128)(2,1)S(1)}, u32[]{:S(2)}, u32[]{:S(2)}) async-start(bf16[32,8,128]{2,1,0:T(8,128)(2,1)} %shard_map.107), calls=%async_computation.1 | async-start | bytes 131072 | tf_op jit(solution)/shard_map/all_to_all | solution.py:471
  71.5 21.2 %collective-permute-start.7 = (bf16[2,2,128,128]{3,2,1,0:T(8,128)(2,1)S(1)}, bf16[2,2,128,128]{3,2,1,0:T(8,128)(2,1)S(1)}, u32[]{:S(2)}, u32[]{:S(2)}) collective-permute-start(bf16[2,2,128,128]{3,2,1,0:T(8,128)(2,1)S(1)} %shard_map.105), channel_id=1, source_target_pairs={{0,256},{256,0},{1,257},{257,1},{2,258},{258,2},{3,259},{259,3},{4... | collective-permute-start | bytes 393224 | tf_op jit(solution)/shard_map/ppermute | solution.py:565
